TPU v7x, 32 devices: a whole 2x2x4 slice. The times are simulated.
32 devices in a mesh: seq: 4 (over z), fsdp: 8 (over y, x, core).
Axes of the slice: x: 2, y: 2, z: 4, core: 2. Of those that a mesh axis runs over, the one named last changes fastest.
Arguments:
- middle_state: bfloat16 [8, 2048, 4096], P('fsdp', 'seq'), may hold values from -80 to 80
- newest_state: bfloat16 [8, 2048, 4096], P('fsdp', 'seq'), may hold values from -6 to 6
- middle_cotangent: bfloat16 [8, 2048, 4096], P('fsdp', 'seq'), may hold values from -6 to 6
- newest_cotangent: bfloat16 [8, 2048, 4096], P('fsdp', 'seq'), may hold values from -6 to 6
- log_decay: int32 [8, 2048, 32], P('fsdp', 'seq'), may hold values from -3079 to 0
- state_weights: bfloat16 [4096, 256], P('fsdp'), may hold values from -0.09375 to 0.09375
- skip_gain: float32 [32], replicated, may hold values from 0.5 to 1.5
Outputs:
- rebuilt_oldest: bfloat16 [8, 2048, 4096], P('fsdp', 'seq')
- middle_gradient: bfloat16 [8, 2048, 4096], P('fsdp', 'seq')
- weights_gradient: float32 [4096, 256], P(('seq', 'fsdp'))
All inputs are finite; a program needn't handle non-finite values.
Results may differ from a plain program's by a relative error of at most 0.017.
Values may be sent and summed in bfloat16 or wider, within the bound.
No kernel may reach another device: no remote copies, remote signals or barrier semaphores. Data moves between devices by JAX's collectives and lax.ppermute only.
A program may use at most 256 MiB of HBM per device.

v0:
```python
import functools

import jax
import jax.numpy as jnp
from jax import lax
from jax.experimental import pallas as pl
from jax.experimental.pallas import tpu as pltpu
from jax.sharding import PartitionSpec as P


CHUNK = 128
PIECES = 4
MIB = 1024 * 1024

f32 = jnp.float32
bf16 = jnp.bfloat16
norm_epsilon = 1e-05
decay_unit = 1.0 / 4096.0


def dot(a, b, ca, cb):
    return lax.dot_general(a, b, (((ca,), (cb,)), ((), ())), preferred_element_type=f32)


def params(mib):
    return pltpu.CompilerParams(vmem_limit_bytes=mib * MIB)


def cost(flops, nbytes):
    return pl.CostEstimate(flops=int(flops), bytes_accessed=int(nbytes), transcendentals=0)


def shape(s, d):
    return jax.ShapeDtypeStruct(s, d)


def in_hbm(x):
    return pltpu.with_memory_space_constraint(x, pltpu.HBM)


def near(x):
    return pltpu.with_memory_space_constraint(x, pltpu.VMEM)


def kept(s, d):
    return pltpu.VMEM(s, d)


def normalize_kernel(meta, mid, decay, x_o, rstd_o, a_o, b_o, half_o, *, heads):
    del meta
    q, d = mid.shape
    ps = d // heads
    values = mid[...].astype(f32)
    rstd = lax.rsqrt(jnp.mean(values * values, axis=-1, keepdims=True) + norm_epsilon)
    rstd_o[...] = rstd
    x_o[...] = (values * rstd).astype(bf16)
    rates = decay[...].astype(f32)
    running = (
        jnp.dot(causal(q).astype(f32), rates, precision=lax.Precision.HIGHEST, preferred_element_type=f32)
        * decay_unit
    )
    mid_log = 0.5 * running[q - 1 : q, :]
    a_o[...] = jnp.exp(running - mid_log) * (ps ** (-0.5))
    b_o[...] = jnp.exp(mid_log - running) * jnp.sqrt(1.0 - jnp.exp(2.0 * (rates * decay_unit)))
    half = jnp.exp(mid_log)
    for h in range(heads):
        half_o[0, :, h * ps : (h + 1) * ps] = jnp.broadcast_to(half[:, h : h + 1], (8, ps))


def normalize(meta, mid, decay):
    t, d = mid.shape
    heads = decay.shape[1]
    n = t // CHUNK
    row = lambda w: pl.BlockSpec((CHUNK, w), lambda i: (i, 0))
    return pl.pallas_call(
        functools.partial(normalize_kernel, heads=heads),
        grid=(n,),
        in_specs=[pl.BlockSpec(memory_space=pltpu.SMEM), row(d), row(heads)],
        out_specs=[row(d), row(1), row(heads), row(heads), pl.BlockSpec((1, 8, d), lambda i: (i, 0, 0))],
        out_shape=[kept((t, d), bf16), kept((t, 1), f32), kept((t, heads), f32), kept((t, heads), f32),
                   kept((n, 8, d), f32)],
        compiler_params=params(12),
        cost_estimate=cost(30 * t * d, 4 * t * d),
        name="normalize",
    )(meta, in_hbm(mid), decay)


def scale_heads_kernel(x, cot, a, b, v_o, g_o, *, heads):
    ps = x.shape[1] // heads
    for h in range(heads):
        cols = slice(h * ps, (h + 1) * ps)
        v_o[:, cols] = (x[:, cols].astype(f32) * b[:, h : h + 1]).astype(bf16)
        g_o[:, cols] = (cot[:, cols].astype(f32) * a[:, h : h + 1]).astype(bf16)


def scale_heads(x, cot, a, b):
    t, d = x.shape
    heads = a.shape[1]
    row = lambda w: pl.BlockSpec((CHUNK, w), lambda i: (i, 0))
    return pl.pallas_call(
        functools.partial(scale_heads_kernel, heads=heads),
        grid=(t // CHUNK,),
        in_specs=[row(d), row(d), row(heads), row(heads)],
        out_specs=[row(d), row(d)],
        out_shape=[kept((t, d), bf16)] * 2,
        compiler_params=params(12),
        cost_estimate=cost(10 * t * d, 8 * t * d),
        name="scale_heads",
    )(near(x), in_hbm(cot), near(a), near(b))


def project_kernel(meta, x, *refs, keys, block):
    weights, (out, full) = refs[:-2], refs[-2:]
    f = meta[0]
    total = None
    for (k, lo), w in zip(keys, weights):
        start = pl.multiple_of(jnp.bitwise_xor(f, k) * block + lo, 128)
        full[pl.ds(start, w.shape[0]), :] = w[...]
        part = dot(x[:, pl.ds(start, w.shape[0])], w[...], 1, 0)
        total = part if total is None else total + part
    out[...] = total.astype(bf16)


def project(meta, x, keys, pieces, block):
    t, d = x.shape
    n2 = pieces[0].shape[1]
    full = pl.BlockSpec(memory_space=pltpu.VMEM)
    return pl.pallas_call(
        functools.partial(project_kernel, keys=keys, block=block),
        in_specs=[pl.BlockSpec(memory_space=pltpu.SMEM), full] + [full] * len(pieces),
        out_specs=[full, full],
        out_shape=[kept((t, n2), bf16), kept((d, n2), bf16)],
        compiler_params=params(16),
        cost_estimate=cost(2 * t * d * n2, 2 * (t * d + d * n2)),
        name="project",
    )(meta, near(x), *pieces)


def states_kernel(p, v, g, half, sl_o, dl_o, loc_o, dtot_o):
    t, w = v.shape
    n = p.shape[1] // 2
    count = t // CHUNK
    state = jnp.zeros((n, w), f32)
    total = jnp.ones((8, w), f32)
    for k in range(count):
        rows = slice(k * CHUNK, (k + 1) * CHUNK)
        hk = half[k, 0:1, :]
        state = state * hk
        sl_o[k] = state.astype(bf16)
        state = (state + dot(p[rows, :n], v[rows, :], 0, 0)) * hk
        total = total * half[k] * half[k]
    loc_o[0, 0] = state.astype(bf16)
    dtot_o[...] = total
    state = jnp.zeros((n, w), f32)
    for k in reversed(range(count)):
        rows = slice(k * CHUNK, (k + 1) * CHUNK)
        hk = half[k, 0:1, :]
        state = state * hk
        dl_o[k] = state.astype(bf16)
        state = (state + dot(p[rows, n:], g[rows, :], 0, 0)) * hk
    loc_o[1, 0] = state.astype(bf16)


def states(p, v, g, half):
    t, d = v.shape
    n = p.shape[1] // 2
    count = t // CHUNK
    w = d // PIECES
    cols = pl.BlockSpec((t, w), lambda i: (0, i))
    chunked = pl.BlockSpec((count, n, w), lambda i: (0, 0, i))
    piece = pl.BlockSpec((2, 1, n, w), lambda i: (0, i, 0, 0))
    return pl.pallas_call(
        states_kernel,
        grid=(PIECES,),
        in_specs=[pl.BlockSpec((t, 2 * n), lambda i: (0, 0)), cols, cols,
                  pl.BlockSpec((count, 8, w), lambda i: (0, 0, i))],
        out_specs=[chunked, chunked, piece, pl.BlockSpec((8, w), lambda i: (0, i))],
        out_shape=[kept((count, n, d), bf16)] * 2
        + [kept((2, PIECES, n, w), bf16), kept((8, d), f32)],
        compiler_params=params(12),
        cost_estimate=cost(4 * t * d * n, 8 * t * d),
        name="states",
    )(near(p), near(v), near(g), near(half))


def hop_kernel(ids, ra, rb, la, lb, da, db, oa, ob):
    del ids
    oa[...] = (la[0, 0].astype(f32) + da[0:1, :] * rb[...].astype(f32)).astype(bf16)
    ob[...] = (lb[0, 0].astype(f32) + db[0:1, :] * ra[...].astype(f32)).astype(bf16)


def hop(ids, j, ra, rb, loc, dtot):
    n, w = ra.shape
    whole = pl.BlockSpec((n, w), lambda i, s: (0, 0))
    own = lambda c: pl.BlockSpec((1, 1, n, w), lambda i, s: (s[2 + 8 * j + c], s[2 + 8 * j + c + 1], 0, 0))
    dec = lambda c: pl.BlockSpec((8, w), lambda i, s: (0, s[2 + 8 * j + c + 1]))
    return pl.pallas_call(
        hop_kernel,
        grid_spec=pltpu.PrefetchScalarGridSpec(
            num_scalar_prefetch=1,
            grid=(1,),
            in_specs=[whole, whole, own(0), own(2), dec(0), dec(2)],
            out_specs=[whole, whole],
        ),
        out_shape=[shape((n, w), bf16)] * 2,
        compiler_params=params(8),
        cost_estimate=cost(4 * n * w, 12 * n * w),
    )(ids, ra, rb, near(loc), near(loc), near(dtot), near(dtot))


def absorb_kernel(ids, ra, rb, v, g, hf, hb, *refs, j):
    si_o, di_o, acc = refs[-3:]
    t, _ = v.shape
    n = ra.shape[0]
    count = t // CHUNK
    odd = ids[2 + 8 * j] == 1
    zero = jnp.zeros(ra.shape, f32)
    fa = ra[...].astype(f32)
    fb = rb[...].astype(f32)
    ahead = jnp.where(odd, fa, fb)
    behind = jnp.where(odd, fb, fa)
    si_o[0] = ahead.astype(bf16)
    di_o[0] = behind.astype(bf16)
    ahead = jnp.where(ids[2 + 8 * j + 4] == ids[2 + 8 * j + 5], ahead, zero)
    behind = jnp.where(ids[2 + 8 * j + 6] == ids[2 + 8 * j + 7], behind, zero)
    carry = jnp.ones(hf[0, 0:1, :].shape, f32)
    for k in range(count):
        rows = slice(k * CHUNK, (k + 1) * CHUNK)
        hk = hf[k, 0:1, :]
        part = dot(g[rows, :], (ahead * (carry * hk)).astype(bf16), 1, 1)
        acc[rows, n:] = part if len(refs) == 5 else refs[2][rows, n:] + part
        carry = carry * hk * hk
    carry = jnp.ones(hf[0, 0:1, :].shape, f32)
    for k in reversed(range(count)):
        rows = slice(k * CHUNK, (k + 1) * CHUNK)
        hk = hb[k, 0:1, :]
        part = dot(v[rows, :], (behind * (carry * hk)).astype(bf16), 1, 1)
        acc[rows, :n] = part if len(refs) == 5 else refs[2][rows, :n] + part
        carry = carry * hk * hk


def absorb(ids, j, ra, rb, v, g, half, si, di, acc):
    t, _ = v.shape
    n, w = ra.shape
    count = t // CHUNK
    whole = lambda *s: pl.BlockSpec(s, lambda i, q: (0,) * len(s))
    cols = lambda c: pl.BlockSpec((t, w), lambda i, q: (0, q[2 + 8 * j + c]))
    dec = lambda c: pl.BlockSpec((count, 8, w), lambda i, q: (0, 0, q[2 + 8 * j + c]))
    slot = lambda c: pl.BlockSpec((1, n, w), lambda i, q: (q[2 + 8 * j + c], 0, 0))
    anyspace = pl.BlockSpec(memory_space=pl.ANY)
    args = [ids, ra, rb, near(v), near(g), near(half), near(half), si, di]
    in_specs = [whole(n, w), whole(n, w), cols(6), cols(4), dec(4), dec(6), anyspace, anyspace]
    if acc is not None:
        args.append(near(acc))
        in_specs.append(whole(t, 2 * n))
    return pl.pallas_call(
        functools.partial(absorb_kernel, j=j),
        grid_spec=pltpu.PrefetchScalarGridSpec(
            num_scalar_prefetch=1,
            grid=(1,),
            in_specs=in_specs,
            out_specs=[slot(5), slot(7), whole(t, 2 * n)],
        ),
        out_shape=[shape(si.shape, bf16), shape(di.shape, bf16), kept((t, 2 * n), f32)],
        input_output_aliases={7: 0, 8: 1},
        compiler_params=params(8),
        cost_estimate=cost(4 * t * w * n, 4 * t * w),
    )(*args)


def pick_kernel(ids, la, lb, oa, ob):
    del ids
    oa[...] = la[0, 0]
    ob[...] = lb[0, 0]


def pick(ids, loc):
    _, _, n, w = loc.shape
    whole = pl.BlockSpec((n, w), lambda i, s: (0, 0))
    own = lambda c: pl.BlockSpec((1, 1, n, w), lambda i, s: (s[2 + c], s[3 + c], 0, 0))
    return pl.pallas_call(
        pick_kernel,
        grid_spec=pltpu.PrefetchScalarGridSpec(
            num_scalar_prefetch=1, grid=(1,), in_specs=[own(0), own(2)], out_specs=[whole, whole]),
        out_shape=[shape((n, w), bf16)] * 2,
        compiler_params=params(8),
        cost_estimate=cost(0, 8 * n * w),
        name="pick",
    )(ids, near(loc), near(loc))


def places():
    count = lax.axis_size("seq")
    z = lax.axis_index("seq")
    j = jnp.arange(PIECES + count - 2, dtype=jnp.int32)
    odd = jnp.zeros_like(j) + z % 2
    clip = lambda at: jnp.clip(at, 0, PIECES - 1)
    slot = lambda at: jnp.where((at >= 0) & (at < PIECES), at, PIECES)
    ahead, behind = j - z, j - (count - 1 - z)
    first = jnp.where(odd == 1, behind, ahead)
    second = jnp.where(odd == 1, ahead, behind)
    ids = jnp.stack(
        [odd, clip(first), 1 - odd, clip(second),
         clip(ahead + 1), slot(ahead + 1), clip(behind + 1), slot(behind + 1)], axis=1).reshape(-1)
    own = jnp.stack([lax.axis_index("fsdp"), z]).astype(jnp.int32)
    return jnp.concatenate([own, ids])


def pass_states(ids, loc, dtot, v, g, half):
    count = lax.axis_size("seq")
    _, _, n, w = loc.shape
    steps = PIECES + count - 2
    pairs_a = [(i, i ^ 1) for i in range(count) if i ^ 1 < count]
    pairs_b = [p for i in range(1, count - 1, 2) for p in ((i, i + 1), (i + 1, i))]
    si = jnp.zeros((PIECES + 1, n, w), bf16)
    di = jnp.zeros((PIECES + 1, n, w), bf16)
    acc = None
    done = []
    for step in range(steps):
        if step == 0:
            sa, sb = pick(ids, loc)
        else:
            sa, sb = hop(ids, step, ra, rb, loc, dtot)
        ra = lax.ppermute(sa, "seq", pairs_a)
        rb = lax.ppermute(sb, "seq", pairs_b)
        si, di, acc = absorb(ids, step, ra, rb, v, g, half, si, di, acc)
        if step >= count - 2:
            done.append((si, di))
    return acc, done


def causal(q):
    return lax.broadcasted_iota(jnp.int32, (q, q), 0) >= lax.broadcasted_iota(jnp.int32, (q, q), 1)


def inner_grad_kernel(p, v, g, sl, dl, out):
    n = p.shape[1] // 2
    entry, readout = p[:, :n], p[:, n:]
    scores = jnp.where(causal(p.shape[0]), dot(g[...], v[...], 1, 1), 0.0).astype(bf16)
    out[:, :n] = dot(scores, readout, 0, 0) + dot(v[...], dl[0], 1, 1)
    out[:, n:] = dot(scores, entry, 1, 0) + dot(g[...], sl[0], 1, 1)


def inner_grad(p, v, g, sl, dl, k):
    _, d = v.shape
    n2 = p.shape[1]
    row = lambda w: pl.BlockSpec((CHUNK, w), lambda i: (k, 0))
    st = pl.BlockSpec((1, n2 // 2, d), lambda i: (k, 0, 0))
    return pl.pallas_call(
        inner_grad_kernel,
        grid=(1,),
        in_specs=[row(n2), row(d), row(d), st, st],
        out_specs=pl.BlockSpec((CHUNK, n2), lambda i: (0, 0)),
        out_shape=kept((CHUNK, n2), f32),
        compiler_params=params(12),
        cost_estimate=cost(6 * CHUNK * d * CHUNK, 8 * CHUNK * d),
    )(near(p), near(v), near(g), near(sl), near(dl))


def weight_grad_kernel(meta, x, acc, *refs):
    inner, (away, kept_o, low_o, low, term) = refs[:-5], refs[-5:]

    @pl.when(pl.program_id(0) == 0)
    def _():
        for k, part in enumerate(inner):
            rows = slice(k * CHUNK, (k + 1) * CHUNK)
            low[rows, :] = (acc[rows, :] + part[...]).astype(bf16)
        low_o[...] = low[...]

    term[...] = dot(x[...], low[...], 0, 0)
    _, half, rows, _ = away.shape
    mine = lax.rem(meta[0], 2)
    for i in range(half):
        start = pl.multiple_of((2 * i + mine) * rows, 8)
        kept_o[0, i] = term[pl.ds(start, rows), :].astype(bf16)
        start = pl.multiple_of((2 * i + 1 - mine) * rows, 8)
        away[0, i] = term[pl.ds(start, rows), :].astype(bf16)


def weight_grad(meta, x, acc, inner):
    t, d = x.shape
    n2 = acc.shape[1]
    along, count = lax.axis_size("seq"), lax.axis_size("fsdp")
    w = d // along
    whole = lambda r: pl.BlockSpec((r, n2), lambda i: (0, 0))
    blocks = (along, count // 2, w // count, n2)
    split = pl.BlockSpec((1,) + blocks[1:], lambda i: (i, 0, 0, 0))
    return pl.pallas_call(
        weight_grad_kernel,
        grid=(along,),
        in_specs=[pl.BlockSpec(memory_space=pltpu.SMEM), pl.BlockSpec((t, w), lambda i: (0, i)), whole(t)]
        + [whole(CHUNK)] * len(inner),
        out_specs=[split, split, whole(t)],
        out_shape=[shape(blocks, bf16), kept(blocks, bf16), kept((t, n2), bf16)],
        scratch_shapes=[pltpu.VMEM((t, n2), bf16), pltpu.VMEM((w, n2), f32)],
        compiler_params=params(12),
        cost_estimate=cost(2 * t * d * n2, 2 * t * d),
        name="weight_grad",
    )(meta, near(x), near(acc), *map(near, inner))


def piece_kernel(x, v, g, cot, newest, p, sl, dl, si, di, half, skip, a, b, *refs, piece, ps):
    rebuilt_o, back_o = refs[-2:]
    w = x.shape[1]
    n = p.shape[1] // 2
    per = w // ps
    k = pl.program_id(0)
    ahead = jnp.ones((1, w), f32)
    behind = ahead
    for j in range(half.shape[0]):
        hj = half[j, 0:1, :]
        sq = hj * hj
        own = jnp.where(j == k, hj, 1.0)
        ahead = ahead * jnp.where(j < k, sq, own)
        behind = behind * jnp.where(j > k, sq, own)
    entry, readout = p[:, :n], p[:, n:]
    scores = jnp.where(causal(CHUNK), dot(readout, entry, 1, 1), 0.0).astype(bf16)
    state = (sl[0].astype(f32) + si[0].astype(f32) * ahead).astype(bf16)
    mixed = dot(scores, v[...], 1, 0) + dot(readout, state, 1, 0)
    state = (dl[0].astype(f32) + di[0].astype(f32) * behind).astype(bf16)
    back = dot(scores, g[...], 0, 0) + dot(entry, state, 1, 0)
    for h in range(per):
        hh = piece * per + h
        own = slice(h * ps, (h + 1) * ps)
        sk = skip[0:1, own]
        y = mixed[:, own] * a[:, hh : hh + 1] + sk * x[:, own].astype(f32)
        rebuilt_o[:, own] = (newest[:, own].astype(f32) - y).astype(bf16)
        gr = back[:, own] * b[:, hh : hh + 1] + sk * cot[:, own].astype(f32)
        back_o[:, own] = gr.astype(bf16)


def state_piece(x, v, g, cot, newest, p, sl, dl, si, di, half, skip, a, b, piece, previous):
    t, d = x.shape
    n2 = p.shape[1]
    n = n2 // 2
    heads = a.shape[1]
    count = half.shape[0]
    w = d // PIECES
    cols = pl.BlockSpec((CHUNK, w), lambda i: (i, piece))
    chunked = pl.BlockSpec((1, n, w), lambda i: (i, 0, piece))
    inc = pl.BlockSpec((1, n, w), lambda i: (piece, 0, 0))
    row = lambda m: pl.BlockSpec((CHUNK, m), lambda i: (i, 0))
    args = [near(x), near(v), near(g), in_hbm(cot), in_hbm(newest), near(p), near(sl), near(dl), si, di, near(half),
            skip, near(a), near(b)]
    in_specs = [cols] * 5 + [row(n2), chunked, chunked, inc, inc,
                             pl.BlockSpec((count, 8, w), lambda i: (0, 0, piece)),
                             pl.BlockSpec((1, w), lambda i: (0, piece)), row(heads), row(heads)]
    aliases = {}
    if previous is not None:
        aliases = {len(args): 0}
        args.append(previous)
        in_specs.append(pl.BlockSpec(memory_space=pltpu.HBM))
    return pl.pallas_call(
        functools.partial(piece_kernel, piece=piece, ps=d // heads),
        grid=(t // CHUNK,),
        in_specs=in_specs,
        out_specs=[cols, pl.BlockSpec((CHUNK, w), lambda i: (i, 0))],
        out_shape=[pltpu.HBM((t, d), bf16), kept((t, w), bf16)],
        input_output_aliases=aliases,
        compiler_params=params(10),
        cost_estimate=cost(8 * t * w * n, 18 * t * w),
    )(*args)


def finish_kernel(x, midcot, low, rstd, weights, *refs):
    backs = refs[:PIECES]
    grad_o, grad = refs[-2:]
    d = x.shape[1]
    grad[...] = dot(low[...], weights[...], 1, 1)
    w = d // PIECES
    dots = jnp.zeros((x.shape[0], 1), f32)
    for i, back in enumerate(backs):
        cols = slice(i * w, (i + 1) * w)
        gr = grad[:, cols] + back[...].astype(f32)
        grad[:, cols] = gr
        dots = dots + jnp.sum(gr * x[:, cols].astype(f32), axis=-1, keepdims=True)
    scale = rstd[...]
    dots = dots * (scale * (1.0 / d))
    for i in range(PIECES):
        cols = slice(i * w, (i + 1) * w)
        dx = scale * grad[:, cols] - x[:, cols].astype(f32) * dots
        grad_o[:, cols] = (midcot[:, cols].astype(f32) + dx).astype(bf16)


def finish(x, backs, midcot, low, rstd, weights, first, number, previous):
    t, d = x.shape
    n2 = low.shape[1]
    row = lambda m: pl.BlockSpec((CHUNK, m), lambda i: (first + i, 0))
    args = [near(x), in_hbm(midcot), near(low), near(rstd), near(weights), *map(near, backs)]
    in_specs = [row(d), row(d), row(n2), row(1), pl.BlockSpec(memory_space=pltpu.VMEM)] + [row(d // PIECES)] * PIECES
    aliases = {}
    if previous is not None:
        aliases = {len(args): 0}
        args.append(previous)
        in_specs.append(pl.BlockSpec(memory_space=pltpu.HBM))
    return pl.pallas_call(
        finish_kernel,
        grid=(number,),
        in_specs=in_specs,
        out_specs=row(d),
        out_shape=pltpu.HBM((t, d), bf16),
        scratch_shapes=[pltpu.VMEM((CHUNK, d), f32)],
        input_output_aliases=aliases,
        compiler_params=params(16),
        cost_estimate=cost(2 * number * CHUNK * d * n2, 8 * number * CHUNK * d),
    )(*args)


def flip(x, bit):
    count = lax.axis_size("fsdp")
    return lax.ppermute(x, "fsdp", [(i, i ^ bit) for i in range(count)])


def gather_weights(w):
    count = lax.axis_size("fsdp")
    rows = w.shape[0]
    if count == 8:
        across, along = flip(w, 2), flip(w, 4)
        mid = rows // 2
        held = [(0, 0, w), (2, 0, across), (4, 0, along),
                (6, 0, flip(across[:mid], 4)), (6, mid, flip(along[mid:], 2))]
        held += [(k | 1, lo, flip(a, 1)) for k, lo, a in held]
    else:
        held = [(0, 0, w)]
        bit = count // 2
        while bit:
            held += [(k | bit, lo, flip(a, bit)) for k, lo, a in held]
            bit //= 2
    return [(k, lo) for k, lo, _ in held], [a for _, _, a in held]


def halve(value, away, kept_o, mine, pos):
    low = 1 << pos
    for i in range(away.shape[1]):
        base = (i // low) * 2 * low + i % low
        kept_o[:, i] = value(base + mine * low)
        away[:, i] = value(base + (1 - mine) * low)


def fold_kernel(meta, *refs, first, left, right):
    f = meta[0]
    bit = lambda b: lax.rem(lax.div(f, b), 2)
    pos = lambda b, order: sorted(order).index(b)
    if first:
        kept_i, got, al, kl, ar, kr, total = refs
        total[...] = (kept_i[...].astype(f32) + got[...].astype(f32)).astype(bf16)
        n = al.shape[-1]
        halve(lambda m: total[:, m, :, :n], al, kl, bit(left[0]), pos(left[0], left))
        halve(lambda m: total[:, m, :, n:], ar, kr, bit(right[0]), pos(right[0], right))
        return
    kl, gl, kr, gr, al_o, kl_o, ar_o, kr_o, tl, tr = refs
    tl[...] = (kl[...].astype(f32) + gl[...].astype(f32)).astype(bf16)
    tr[...] = (kr[...].astype(f32) + gr[...].astype(f32)).astype(bf16)
    halve(lambda m: tl[:, m], al_o, kl_o, bit(left[0]), pos(left[0], left))
    halve(lambda m: tr[:, m], ar_o, kr_o, bit(right[0]), pos(right[0], right))


def fold(meta, arrays, left, right, first):
    along, blocks, rows, n = arrays[0].shape
    n = n // 2 if first else n
    out = (along, blocks // 2, rows, n)
    vmem = pl.BlockSpec(memory_space=pltpu.VMEM)
    scratch = [pltpu.VMEM(arrays[0].shape, bf16)] * (1 if first else 2)
    return pl.pallas_call(
        functools.partial(fold_kernel, first=first, left=left, right=right),
        in_specs=[pl.BlockSpec(memory_space=pltpu.SMEM)] + [vmem] * len(arrays),
        out_specs=[vmem] * 4,
        out_shape=[shape(out, bf16), kept(out, bf16)] * 2,
        scratch_shapes=scratch,
        compiler_params=params(10),
        cost_estimate=cost(0, 8 * along * blocks * rows * n),
    )(meta, *arrays)


def deal_kernel(meta, kl, gl, kr, gr, own, *refs):
    along, _, _, n = kl.shape
    sends, both = refs[:-1], refs[-1]
    z = meta[1]
    both[:, :, :n] = (kl[:, 0].astype(f32) + gl[:, 0].astype(f32)).astype(bf16)
    both[:, :, n:] = (kr[:, 0].astype(f32) + gr[:, 0].astype(f32)).astype(bf16)
    own[...] = both[z]
    for k, out in enumerate(sends, 1):
        out[...] = both[lax.rem(z + k, along)]


def deal(meta, arrays):
    along, _, rows, n = arrays[0].shape
    vmem = pl.BlockSpec(memory_space=pltpu.VMEM)
    return pl.pallas_call(
        deal_kernel,
        in_specs=[pl.BlockSpec(memory_space=pltpu.SMEM)] + [vmem] * 4,
        out_specs=[vmem] * along,
        out_shape=[shape((rows, 2 * n), bf16)] * along,
        scratch_shapes=[pltpu.VMEM((along, rows, 2 * n), bf16)],
        compiler_params=params(8),
        cost_estimate=cost(0, 8 * along * rows * n),
        name="deal",
    )(meta, *arrays)


def scatter_sum(meta, away, kept_i):
    along = lax.axis_size("seq")
    count = lax.axis_size("fsdp")
    left = [1 << i for i in range(1, count.bit_length() - 1)]
    right = left[::-1]
    got = flip(away, 1)
    al, kl, ar, kr = fold(meta, [kept_i, got], left, right, True)
    for _ in range(len(left)):
        gl, gr = flip(al, left[0]), flip(ar, right[0])
        left, right = left[1:], right[1:]
        if left:
            al, kl, ar, kr = fold(meta, [kl, gl, kr, gr], left, right, False)
    own, *sends = deal(meta, [kl, gl, kr, gr])
    total = own.astype(f32)
    for k, block in enumerate(sends, 1):
        other = lax.ppermute(block, "seq", [(i, (i + k) % along) for i in range(along)])
        total = total + other.astype(f32)
    return total


def step(middle_state, newest_state, middle_cotangent, newest_cotangent, log_decay, state_weights, skip_gain):
    t, d = middle_state.shape[1:]
    heads = log_decay.shape[2]
    middle, newest, midcot, cot = middle_state[0], newest_state[0], middle_cotangent[0], newest_cotangent[0]
    meta = places()
    block = state_weights.shape[0]
    count = t // CHUNK
    keys, pieces = gather_weights(state_weights)
    x, rstd, a, b, half = normalize(meta, middle, log_decay[0])
    v, g = scale_heads(x, cot, a, b)
    p, weights = project(meta, x, keys, pieces, block)
    sl, dl, loc, dtot = states(p, v, g, half)
    inner = [inner_grad(p, v, g, sl, dl, k) for k in range(count)]
    acc, heads_done = pass_states(meta, loc, dtot, v, g, half)
    away, stays, low = weight_grad(meta, x, acc, inner)
    skip = jnp.repeat(skip_gain, d // heads)[None]
    rebuilt, backs = None, []
    for i in range(PIECES):
        sp, dp = heads_done[i]
        rebuilt, back = state_piece(
            x, v, g, cot, newest, p, sl, dl, sp, dp, half, skip, a, b, i, rebuilt)
        backs.append(back)
    gradient = None
    for i in range(2):
        gradient = finish(x, backs, midcot, low, rstd, weights,
                          i * count // 2, count // 2, gradient)
    summed = scatter_sum(meta, away, stays)
    scale = (t * lax.axis_size("seq") * lax.axis_size("fsdp")) ** (-0.5)
    return rebuilt[None], gradient[None], summed * scale


def solution(mesh):
    whole = P("fsdp", "seq", None)
    return jax.shard_map(
        step,
        mesh=mesh,
        in_specs=(whole, whole, whole, whole, whole, P("fsdp", None), P()),
        out_specs=(whole, whole, P(("seq", "fsdp"), None)),
        check_vma=False,
    )
```

profile of v0, /device:TPU:0, one launch (start us, length us, event | category | flops | bytes accessed | tf_op | source)
XLA Modules:
  0.0 154.6 jit_solution(7049018697325971791)
XLA Ops:
  0.6 3.0 %collective-permute-start = (bf16[512,256]{1,0:T(8,128)(2,1)}, bf16[512,256]{1,0:T(8,128)(2,1)S(1)}, u32[]{:S(2)}, u32[]{:S(2)}) collective-permute-start(bf16[512,256]{1,0:T(8,128)(2,1)} %refs_0_.1), channel_id=1, source_target_pairs={{0,2},{1,3},{2,0},{3,1},{4,6},{5,7},{6,4},{7,5},{8,10},{9,11},{10,... | collective-permute-start | bytes 786440 | tf_op jit(solution)/shard_map/ppermute | solution.py:511
  3.7 1.5 collective-permute-start.1
  5.2 5.0 %collective-permute-done.refs_1_ = bf16[512,256]{1,0:T(8,128)(2,1)S(1)} collective-permute-done((bf16[512,256]{1,0:T(8,128)(2,1)}, bf16[512,256]{1,0:T(8,128)(2,1)S(1)}, u32[]{:S(2)}, u32[]{:S(2)}) %collective-permute-start) | collective-permute-done | bytes 262176 | tf_op jit(solution)/shard_map/ppermute | solution.py:511
  10.2 1.8 %collective-permute-start.2 = (bf16[256,256]{1,0:T(8,128)(2,1)S(1)}, bf16[256,256]{1,0:T(8,128)(2,1)S(1)}, u32[]{:S(2)}, u32[]{:S(2)}) collective-permute-start(bf16[256,256]{1,0:T(8,128)(2,1)S(1)} %slice.8), channel_id=1, source_target_pairs={{0,4},{1,5},{2,6},{3,7},{4,0},{5,1},{6,2},{7,3},{8,12},{9,13},{10,... | collective-permute-start | bytes 393224 | tf_op jit(solution)/shard_map/ppermute | solution.py:511
  12.0 1.6 %collective-permute-start.3 = (bf16[256,256]{1,0:T(8,128)(2,1)S(1)}, bf16[256,256]{1,0:T(8,128)(2,1)S(1)}, u32[]{:S(2)}, u32[]{:S(2)}) collective-permute-start(bf16[256,256]{1,0:T(8,128)(2,1)S(1)} %slice.9), channel_id=1, source_target_pairs={{0,2},{1,3},{2,0},{3,1},{4,6},{5,7},{6,4},{7,5},{8,10},{9,11},{10,... | collective-permute-start | bytes 393224 | tf_op jit(solution)/shard_map/ppermute | solution.py:511
  15.2 1.8 %collective-permute-done.3.refs_4_ = bf16[256,256]{1,0:T(8,128)(2,1)S(1)} collective-permute-done((bf16[256,256]{1,0:T(8,128)(2,1)S(1)}, bf16[256,256]{1,0:T(8,128)(2,1)S(1)}, u32[]{:S(2)}, u32[]{:S(2)}) %collective-permute-start.3) | collective-permute-done | bytes 131104 | tf_op jit(solution)/shard_map/ppermute | solution.py:511
  18.3 4.1 %normalize.1 = (bf16[512,4096]{1,0:T(8,128)(2,1)S(1)}, f32[512,1]{1,0:T(8,128)S(1)}, f32[512,32]{1,0:T(8,128)S(1)}, f32[512,32]{1,0:T(8,128)S(1)}, f32[4,8,4096]{2,1,0:T(8,128)S(1)}) custom-call(s32[50]{0:T(128)S(1)} %pad_add_fusion.meta.ids, bf16[512,4096]{1,0:T(8,128)(2,1)} %bitcast.28, s32[512,32]{1,0:T(8,128)S(1)} %bitcast.10), custom_call_target="tpu_custom_call" | custom-call | flops 62914560 | bytes 8388608 | tf_op jit(solution)/shard_map/normalize/pallas_call | solution.py:75
  22.5 6.1 %scale_heads.1 = (bf16[512,4096]{1,0:T(8,128)(2,1)S(1)}, bf16[512,4096]{1,0:T(8,128)(2,1)S(1)}) custom-call(bf16[512,4096]{1,0:T(8,128)(2,1)S(1)} %get-tuple-element.69.x, bf16[512,4096]{1,0:T(8,128)(2,1)} %bitcast.15, f32[512,32]{1,0:T(8,128)S(1)} %get-tuple-element.70.a, f32[512,32]{1,0:T(8,128)S(1)} %get-tuple-element.71.b), custom_call_target="tpu_custom_call" | custom-call | flops 20971520 | bytes 16777216 | tf_op jit(solution)/shard_map/scale_heads/pallas_call | solution.py:100
  28.7 1.9 %project.1 = (bf16[512,256]{1,0:T(8,128)(2,1)S(1)}, bf16[4096,256]{1,0:T(8,128)(2,1)S(1)}) custom-call(s32[50]{0:T(128)S(1)} %pad_add_fusion.meta.ids, bf16[512,4096]{1,0:T(8,128)(2,1)S(1)} %get-tuple-element.69.x, bf16[512,256]{1,0:T(8,128)(2,1)S(1)} %copy-done, bf16[512,256]{1,0:T(8,128)(2,1)S(1)} %collective-permute-done.refs_1_, ...), custom_call_target="tpu_custom_call" | custom-call | flops 1073741824 | bytes 6291456 | tf_op jit(solution)/shard_map/project/pallas_call | solution.py:128
  30.6 4.9 %states.1 = (bf16[4,128,4096]{2,1,0:T(8,128)(2,1)S(1)}, bf16[4,128,4096]{2,1,0:T(8,128)(2,1)S(1)}, bf16[2,4,128,1024]{3,2,1,0:T(8,128)(2,1)S(1)}, f32[8,4096]{1,0:T(8,128)S(1)}) custom-call(bf16[512,256]{1,0:T(8,128)(2,1)S(1)} %get-tuple-element.74.p, bf16[512,4096]{1,0:T(8,128)(2,1)S(1)} %get-tuple-element.72.v, bf16[512,4096]{1,0:T(8,128)(2,1)S(1)} %get-tuple-element.73.g, ...), custom_call_target="tpu_custom_call" | custom-call | flops 1073741824 | bytes 16777216 | tf_op jit(solution)/shard_map/states/pallas_call | solution.py:172
  36.7 4.5 %collective-permute-start.9 = (bf16[128,1024]{1,0:T(8,128)(2,1)S(1)}, bf16[128,1024]{1,0:T(8,128)(2,1)S(1)}, u32[]{:S(2)}, u32[]{:S(2)}) collective-permute-start(bf16[128,1024]{1,0:T(8,128)(2,1)S(1)} %get-tuple-element.79), channel_id=1, source_target_pairs={{0,8},{8,0},{16,24},{24,16},{1,9},{9,1},{17,25},{25,17},{2,10},{10... | collective-permute-start | bytes 786440 | tf_op jit(solution)/shard_map/ppermute | solution.py:324
  41.2 6.7 %collective-permute-done.9.ra = bf16[128,1024]{1,0:T(8,128)(2,1)S(1)} collective-permute-done((bf16[128,1024]{1,0:T(8,128)(2,1)S(1)}, bf16[128,1024]{1,0:T(8,128)(2,1)S(1)}, u32[]{:S(2)}, u32[]{:S(2)}) %collective-permute-start.9) | collective-permute-done | bytes 262176 | tf_op jit(solution)/shard_map/ppermute | solution.py:324
  48.6 1.8 %collective-permute-start.11 = (bf16[128,1024]{1,0:T(8,128)(2,1)S(1)}, bf16[128,1024]{1,0:T(8,128)(2,1)S(1)}, u32[]{:S(2)}, u32[]{:S(2)}) collective-permute-start(bf16[128,1024]{1,0:T(8,128)(2,1)S(1)} %get-tuple-element.82), channel_id=1, source_target_pairs={{0,8},{8,0},{16,24},{24,16},{1,9},{9,1},{17,25},{25,17},{2,10},{10... | collective-permute-start | bytes 786440 | tf_op jit(solution)/shard_map/ppermute | solution.py:324
  51.1 5.4 %collective-permute-done.11.ra = bf16[128,1024]{1,0:T(8,128)(2,1)S(1)} collective-permute-done((bf16[128,1024]{1,0:T(8,128)(2,1)S(1)}, bf16[128,1024]{1,0:T(8,128)(2,1)S(1)}, u32[]{:S(2)}, u32[]{:S(2)}) %collective-permute-start.11) | collective-permute-done | bytes 262176 | tf_op jit(solution)/shard_map/ppermute | solution.py:324
  57.2 3.7 %collective-permute-start.13 = (bf16[128,1024]{1,0:T(8,128)(2,1)S(1)}, bf16[128,1024]{1,0:T(8,128)(2,1)S(1)}, u32[]{:S(2)}, u32[]{:S(2)}) collective-permute-start(bf16[128,1024]{1,0:T(8,128)(2,1)S(1)} %get-tuple-element.84), channel_id=1, source_target_pairs={{0,8},{8,0},{16,24},{24,16},{1,9},{9,1},{17,25},{25,17},{2,10},{10... | collective-permute-start | bytes 786440 | tf_op jit(solution)/shard_map/ppermute | solution.py:324
  61.6 4.3 %collective-permute-done.13.ra = bf16[128,1024]{1,0:T(8,128)(2,1)S(1)} collective-permute-done((bf16[128,1024]{1,0:T(8,128)(2,1)S(1)}, bf16[128,1024]{1,0:T(8,128)(2,1)S(1)}, u32[]{:S(2)}, u32[]{:S(2)}) %collective-permute-start.13) | collective-permute-done | bytes 262176 | tf_op jit(solution)/shard_map/ppermute | solution.py:324
  66.6 3.7 %collective-permute-start.15 = (bf16[128,1024]{1,0:T(8,128)(2,1)S(1)}, bf16[128,1024]{1,0:T(8,128)(2,1)S(1)}, u32[]{:S(2)}, u32[]{:S(2)}) collective-permute-start(bf16[128,1024]{1,0:T(8,128)(2,1)S(1)} %get-tuple-element.86), channel_id=1, source_target_pairs={{0,8},{8,0},{16,24},{24,16},{1,9},{9,1},{17,25},{25,17},{2,10},{10... | collective-permute-start | bytes 786440 | tf_op jit(solution)/shard_map/ppermute | solution.py:324
  71.0 3.7 %collective-permute-done.15.ra = bf16[128,1024]{1,0:T(8,128)(2,1)S(1)} collective-permute-done((bf16[128,1024]{1,0:T(8,128)(2,1)S(1)}, bf16[128,1024]{1,0:T(8,128)(2,1)S(1)}, u32[]{:S(2)}, u32[]{:S(2)}) %collective-permute-start.15) | collective-permute-done | bytes 262176 | tf_op jit(solution)/shard_map/ppermute | solution.py:324
  75.4 4.0 %collective-permute-start.17 = (bf16[128,1024]{1,0:T(8,128)(2,1)S(1)}, bf16[128,1024]{1,0:T(8,128)(2,1)S(1)}, u32[]{:S(2)}, u32[]{:S(2)}) collective-permute-start(bf16[128,1024]{1,0:T(8,128)(2,1)S(1)} %get-tuple-element.88), channel_id=1, source_target_pairs={{0,8},{8,0},{16,24},{24,16},{1,9},{9,1},{17,25},{25,17},{2,10},{10... | collective-permute-start | bytes 786440 | tf_op jit(solution)/shard_map/ppermute | solution.py:324
  84.9 3.6 %collective-permute-start.19 = (bf16[128,1024]{1,0:T(8,128)(2,1)S(1)}, bf16[128,1024]{1,0:T(8,128)(2,1)S(1)}, u32[]{:S(2)}, u32[]{:S(2)}) collective-permute-start(bf16[128,1024]{1,0:T(8,128)(2,1)S(1)} %get-tuple-element.90), channel_id=1, source_target_pairs={{0,8},{8,0},{16,24},{24,16},{1,9},{9,1},{17,25},{25,17},{2,10},{10... | collective-permute-start | bytes 786440 | tf_op jit(solution)/shard_map/ppermute | solution.py:324
  93.8 4.8 %shard_map.105 = (bf16[512,4096]{1,0:T(8,128)(2,1)}, bf16[512,1024]{1,0:T(8,128)(2,1)S(1)}) custom-call(bf16[512,4096]{1,0:T(8,128)(2,1)S(1)} %get-tuple-element.69.x, bf16[512,4096]{1,0:T(8,128)(2,1)S(1)} %get-tuple-element.72.v, bf16[512,4096]{1,0:T(8,128)(2,1)S(1)} %get-tuple-element.73.g, bf16[512,4096]{1,0:T(8,128)(2,1)} %bitcast.16, ...), custom_call_target="tpu_custom_call" | custom-call | flops 536870912 | bytes 9437184 | tf_op jit(solution)/shard_map/pallas_call | solution.py:453
  100.0 4.8 %shard_map.106 = (bf16[512,4096]{1,0:T(8,128)(2,1)}, bf16[512,1024]{1,0:T(8,128)(2,1)S(1)}) custom-call(bf16[512,4096]{1,0:T(8,128)(2,1)S(1)} %get-tuple-element.69.x, bf16[512,4096]{1,0:T(8,128)(2,1)S(1)} %get-tuple-element.72.v, bf16[512,4096]{1,0:T(8,128)(2,1)S(1)} %get-tuple-element.73.g, ...), custom_call_target="tpu_custom_call", output_to_operand_aliasing={{0}: (14, {})} | custom-call | flops 536870912 | bytes 9437184 | tf_op jit(solution)/shard_map/pallas_call | solution.py:453
  106.2 4.8 %shard_map.107 = (bf16[512,4096]{1,0:T(8,128)(2,1)}, bf16[512,1024]{1,0:T(8,128)(2,1)S(1)}) custom-call(bf16[512,4096]{1,0:T(8,128)(2,1)S(1)} %get-tuple-element.69.x, bf16[512,4096]{1,0:T(8,128)(2,1)S(1)} %get-tuple-element.72.v, bf16[512,4096]{1,0:T(8,128)(2,1)S(1)} %get-tuple-element.73.g, ...), custom_call_target="tpu_custom_call", output_to_operand_aliasing={{0}: (14, {})} | custom-call | flops 536870912 | bytes 9437184 | tf_op jit(solution)/shard_map/pallas_call | solution.py:453
  112.4 3.9 %weight_grad.1 = (bf16[4,4,128,256]{3,2,1,0:T(8,128)(2,1)S(1)}, bf16[4,4,128,256]{3,2,1,0:T(8,128)(2,1)S(1)}, bf16[512,256]{1,0:T(8,128)(2,1)S(1)}) custom-call(s32[50]{0:T(128)S(1)} %pad_add_fusion.meta.ids, bf16[512,4096]{1,0:T(8,128)(2,1)S(1)} %get-tuple-element.69.x, f32[512,256]{1,0:T(8,128)S(1)} %get-tuple-element.113.acc, ...), custom_call_target="tpu_custom_call" | custom-call | flops 1073741824 | bytes 4194304 | tf_op jit(solution)/shard_map/weight_grad/pallas_call | solution.py:388
  116.4 2.6 %collective-permute-done.21.refs_1_ = bf16[4,4,128,256]{3,2,1,0:T(8,128)(2,1)S(1)} collective-permute-done((bf16[4,4,128,256]{3,2,1,0:T(8,128)(2,1)S(1)}, bf16[4,4,128,256]{3,2,1,0:T(8,128)(2,1)S(1)}, u32[]{:S(2)}, u32[]{:S(2)}) %collective-permute-start.21) | collective-permute-done | bytes 1048608 | tf_op jit(solution)/shard_map/ppermute | solution.py:511
  120.3 1.6 %collective-permute-start.22 = (bf16[4,2,128,128]{3,2,1,0:T(8,128)(2,1)S(1)}, bf16[4,2,128,128]{3,2,1,0:T(8,128)(2,1)S(1)}, u32[]{:S(2)}, u32[]{:S(2)}) collective-permute-start(bf16[4,2,128,128]{3,2,1,0:T(8,128)(2,1)S(1)} %get-tuple-element.124), channel_id=1, source_target_pairs={{0,2},{1,3},{2,0},{3,1},{4,6},{5,7},{6,4},{7,5},{8,10},{9,11},{10,... | collective-permute-start | bytes 786440 | tf_op jit(solution)/shard_map/ppermute | solution.py:511
  122.4 6.3 %collective-permute-done.22.refs_1_ = bf16[4,2,128,128]{3,2,1,0:T(8,128)(2,1)S(1)} collective-permute-done((bf16[4,2,128,128]{3,2,1,0:T(8,128)(2,1)S(1)}, bf16[4,2,128,128]{3,2,1,0:T(8,128)(2,1)S(1)}, u32[]{:S(2)}, u32[]{:S(2)}) %collective-permute-start.22) | collective-permute-done | bytes 262176 | tf_op jit(solution)/shard_map/ppermute | solution.py:511
  132.5 4.7 %shard_map.108 = (bf16[512,4096]{1,0:T(8,128)(2,1)}, bf16[512,1024]{1,0:T(8,128)(2,1)S(1)}) custom-call(bf16[512,4096]{1,0:T(8,128)(2,1)S(1)} %get-tuple-element.69.x, bf16[512,4096]{1,0:T(8,128)(2,1)S(1)} %get-tuple-element.72.v, bf16[512,4096]{1,0:T(8,128)(2,1)S(1)} %get-tuple-element.73.g, ...), custom_call_target="tpu_custom_call", output_to_operand_aliasing={{0}: (14, {})} | custom-call | flops 536870912 | bytes 9437184 | tf_op jit(solution)/shard_map/pallas_call | solution.py:453
  137.9 1.8 %collective-permute-start.26 = (bf16[128,256]{1,0:T(8,128)(2,1)S(1)}, bf16[128,256]{1,0:T(8,128)(2,1)S(1)}, u32[]{:S(2)}, u32[]{:S(2)}) collective-permute-start(bf16[128,256]{1,0:T(8,128)(2,1)S(1)} %get-tuple-element.132), channel_id=1, source_target_pairs={{0,8},{8,16},{16,24},{24,0},{1,9},{9,17},{17,25},{25,1},{2,10},{10... | collective-permute-start | bytes 196616 | tf_op jit(solution)/shard_map/ppermute | solution.py:616
  140.7 2.8 %collective-permute-start.28 = (bf16[128,256]{1,0:T(8,128)(2,1)S(1)}, bf16[128,256]{1,0:T(8,128)(2,1)S(1)}, u32[]{:S(2)}, u32[]{:S(2)}) collective-permute-start(bf16[128,256]{1,0:T(8,128)(2,1)S(1)} %get-tuple-element.134), channel_id=1, source_target_pairs={{0,24},{8,0},{16,8},{24,16},{1,25},{9,1},{17,9},{25,17},{2,26},{10... | collective-permute-start | bytes 196616 | tf_op jit(solution)/shard_map/ppermute | solution.py:616
  143.6 5.2 %shard_map.113.refs_4_ = bf16[512,4096]{1,0:T(8,128)(2,1)} custom-call(bf16[512,4096]{1,0:T(8,128)(2,1)S(1)} %get-tuple-element.69.x, bf16[512,4096]{1,0:T(8,128)(2,1)} %bitcast.25, bf16[512,256]{1,0:T(8,128)(2,1)S(1)} %get-tuple-element.114.low, f32[512,1]{1,0:T(8,128)S(1)} %get-tuple-element.115.rstd, bf16[4096,256]{1,0:T(8,128)(2,1)S(1)} %get-tuple-element.116.weights, ...), custom_call_target="tpu_custom_call" | custom-call | flops 536870912 | bytes 8388608 | tf_op jit(solution)/shard_map/pallas_call | solution.py:496
  148.8 5.2 %shard_map.114 = bf16[512,4096]{1,0:T(8,128)(2,1)} custom-call(bf16[512,4096]{1,0:T(8,128)(2,1)S(1)} %get-tuple-element.69.x, bf16[512,4096]{1,0:T(8,128)(2,1)} %bitcast.26, bf16[512,256]{1,0:T(8,128)(2,1)S(1)} %get-tuple-element.114.low, f32[512,1]{1,0:T(8,128)S(1)} %get-tuple-element.115.rstd, ...), custom_call_target="tpu_custom_call", output_to_operand_aliasing={{}: (9, {})} | custom-call | flops 536870912 | bytes 8388608 | tf_op jit(solution)/shard_map/pallas_call | solution.py:496
  (75 shorter events, 32.0 us)
Async XLA Ops:
  0.6 9.6 %collective-permute-start = (bf16[512,256]{1,0:T(8,128)(2,1)}, bf16[512,256]{1,0:T(8,128)(2,1)S(1)}, u32[]{:S(2)}, u32[]{:S(2)}) collective-permute-start(bf16[512,256]{1,0:T(8,128)(2,1)} %refs_0_.1), channel_id=1, source_target_pairs={{0,2},{1,3},{2,0},{3,1},{4,6},{5,7},{6,4},{7,5},{8,10},{9,11},{10,... | collective-permute-start | bytes 786440 | tf_op jit(solution)/shard_map/ppermute | solution.py:511
  3.7 8.4 %collective-permute-start.1 = (bf16[512,256]{1,0:T(8,128)(2,1)}, bf16[512,256]{1,0:T(8,128)(2,1)S(1)}, u32[]{:S(2)}, u32[]{:S(2)}) collective-permute-start(bf16[512,256]{1,0:T(8,128)(2,1)} %refs_0_.1), channel_id=1, source_target_pairs={{0,4},{1,5},{2,6},{3,7},{4,0},{5,1},{6,2},{7,3},{8,12},{9,13},{10,... | collective-permute-start | bytes 786440 | tf_op jit(solution)/shard_map/ppermute | solution.py:511
  5.2 23.4 %collective-permute-start.4 = (bf16[512,256]{1,0:T(8,128)(2,1)}, bf16[512,256]{1,0:T(8,128)(2,1)S(1)}, u32[]{:S(2)}, u32[]{:S(2)}) collective-permute-start(bf16[512,256]{1,0:T(8,128)(2,1)} %refs_0_.1), channel_id=1, source_target_pairs={{0,1},{1,0},{2,3},{3,2},{4,5},{5,4},{6,7},{7,6},{8,9},{9,8},{10,11... | collective-permute-start | bytes 786440 | tf_op jit(solution)/shard_map/ppermute | solution.py:511
  10.2 5.0 %collective-permute-start.2 = (bf16[256,256]{1,0:T(8,128)(2,1)S(1)}, bf16[256,256]{1,0:T(8,128)(2,1)S(1)}, u32[]{:S(2)}, u32[]{:S(2)}) collective-permute-start(bf16[256,256]{1,0:T(8,128)(2,1)S(1)} %slice.8), channel_id=1, source_target_pairs={{0,4},{1,5},{2,6},{3,7},{4,0},{5,1},{6,2},{7,3},{8,12},{9,13},{10,... | collective-permute-start | bytes 393224 | tf_op jit(solution)/shard_map/ppermute | solution.py:511
  12.0 5.0 %collective-permute-start.3 = (bf16[256,256]{1,0:T(8,128)(2,1)S(1)}, bf16[256,256]{1,0:T(8,128)(2,1)S(1)}, u32[]{:S(2)}, u32[]{:S(2)}) collective-permute-start(bf16[256,256]{1,0:T(8,128)(2,1)S(1)} %slice.9), channel_id=1, source_target_pairs={{0,2},{1,3},{2,0},{3,1},{4,6},{5,7},{6,4},{7,5},{8,10},{9,11},{10,... | collective-permute-start | bytes 393224 | tf_op jit(solution)/shard_map/ppermute | solution.py:511
  13.6 15.0 %collective-permute-start.5 = (bf16[512,256]{1,0:T(8,128)(2,1)S(1)}, bf16[512,256]{1,0:T(8,128)(2,1)S(1)}, u32[]{:S(2)}, u32[]{:S(2)}) collective-permute-start(bf16[512,256]{1,0:T(8,128)(2,1)S(1)} %collective-permute-done.refs_1_), channel_id=1, source_target_pairs={{0,1},{1,0},{2,3},{3,2},{4,5},{5,4},{6,7},{7,6},{8,9},{9,8},{10,11... | collective-permute-start | bytes 786440 | tf_op jit(solution)/shard_map/ppermute | solution.py:511
  13.6 15.0 %collective-permute-start.6 = (bf16[512,256]{1,0:T(8,128)(2,1)S(1)}, bf16[512,256]{1,0:T(8,128)(2,1)S(1)}, u32[]{:S(2)}, u32[]{:S(2)}) collective-permute-start(bf16[512,256]{1,0:T(8,128)(2,1)S(1)} %collective-permute-done.1.refs_2_), channel_id=1, source_target_pairs={{0,1},{1,0},{2,3},{3,2},{4,5},{5,4},{6,7},{7,6},{8,9},{9,8},{10,11... | collective-permute-start | bytes 786440 | tf_op jit(solution)/shard_map/ppermute | solution.py:511
  15.2 13.4 %collective-permute-start.7 = (bf16[256,256]{1,0:T(8,128)(2,1)S(1)}, bf16[256,256]{1,0:T(8,128)(2,1)S(1)}, u32[]{:S(2)}, u32[]{:S(2)}) collective-permute-start(bf16[256,256]{1,0:T(8,128)(2,1)S(1)} %collective-permute-done.2.refs_3_), channel_id=1, source_target_pairs={{0,1},{1,0},{2,3},{3,2},{4,5},{5,4},{6,7},{7,6},{8,9},{9,8},{10,11... | collective-permute-start | bytes 393224 | tf_op jit(solution)/shard_map/ppermute | solution.py:511
  17.1 11.5 %collective-permute-start.8 = (bf16[256,256]{1,0:T(8,128)(2,1)S(1)}, bf16[256,256]{1,0:T(8,128)(2,1)S(1)}, u32[]{:S(2)}, u32[]{:S(2)}) collective-permute-start(bf16[256,256]{1,0:T(8,128)(2,1)S(1)} %collective-permute-done.3.refs_4_), channel_id=1, source_target_pairs={{0,1},{1,0},{2,3},{3,2},{4,5},{5,4},{6,7},{7,6},{8,9},{9,8},{10,11... | collective-permute-start | bytes 393224 | tf_op jit(solution)/shard_map/ppermute | solution.py:511
  22.5 6.2 %copy-start = (bf16[512,256]{1,0:T(8,128)(2,1)S(1)}, bf16[512,256]{1,0:T(8,128)(2,1)}, u32[]{:S(2)}) copy-start(bf16[512,256]{1,0:T(8,128)(2,1)} %refs_0_.1) | copy-start | bytes 786436
  36.0 5.1 %collective-permute-start.10 = (bf16[128,1024]{1,0:T(8,128)(2,1)S(1)}, bf16[128,1024]{1,0:T(8,128)(2,1)S(1)}, u32[]{:S(2)}, u32[]{:S(2)}) collective-permute-start(bf16[128,1024]{1,0:T(8,128)(2,1)S(1)} %get-tuple-element.80), channel_id=1, source_target_pairs={{8,16},{16,8},{9,17},{17,9},{10,18},{18,10},{11,19},{19,11},{12,20... | collective-permute-start | bytes 786440 | tf_op jit(solution)/shard_map/ppermute | solution.py:325
  36.7 11.1 %collective-permute-start.9 = (bf16[128,1024]{1,0:T(8,128)(2,1)S(1)}, bf16[128,1024]{1,0:T(8,128)(2,1)S(1)}, u32[]{:S(2)}, u32[]{:S(2)}) collective-permute-start(bf16[128,1024]{1,0:T(8,128)(2,1)S(1)} %get-tuple-element.79), channel_id=1, source_target_pairs={{0,8},{8,0},{16,24},{24,16},{1,9},{9,1},{17,25},{25,17},{2,10},{10... | collective-permute-start | bytes 786440 | tf_op jit(solution)/shard_map/ppermute | solution.py:324
  48.6 7.9 %collective-permute-start.11 = (bf16[128,1024]{1,0:T(8,128)(2,1)S(1)}, bf16[128,1024]{1,0:T(8,128)(2,1)S(1)}, u32[]{:S(2)}, u32[]{:S(2)}) collective-permute-start(bf16[128,1024]{1,0:T(8,128)(2,1)S(1)} %get-tuple-element.82), channel_id=1, source_target_pairs={{0,8},{8,0},{16,24},{24,16},{1,9},{9,1},{17,25},{25,17},{2,10},{10... | collective-permute-start | bytes 786440 | tf_op jit(solution)/shard_map/ppermute | solution.py:324
  50.4 6.1 %collective-permute-start.12 = (bf16[128,1024]{1,0:T(8,128)(2,1)S(1)}, bf16[128,1024]{1,0:T(8,128)(2,1)S(1)}, u32[]{:S(2)}, u32[]{:S(2)}) collective-permute-start(bf16[128,1024]{1,0:T(8,128)(2,1)S(1)} %get-tuple-element.83), channel_id=1, source_target_pairs={{8,16},{16,8},{9,17},{17,9},{10,18},{18,10},{11,19},{19,11},{12,20... | collective-permute-start | bytes 786440 | tf_op jit(solution)/shard_map/ppermute | solution.py:325
  57.2 8.7 %collective-permute-start.13 = (bf16[128,1024]{1,0:T(8,128)(2,1)S(1)}, bf16[128,1024]{1,0:T(8,128)(2,1)S(1)}, u32[]{:S(2)}, u32[]{:S(2)}) collective-permute-start(bf16[128,1024]{1,0:T(8,128)(2,1)S(1)} %get-tuple-element.84), channel_id=1, source_target_pairs={{0,8},{8,0},{16,24},{24,16},{1,9},{9,1},{17,25},{25,17},{2,10},{10... | collective-permute-start | bytes 786440 | tf_op jit(solution)/shard_map/ppermute | solution.py:324
  60.9 5.0 %collective-permute-start.14 = (bf16[128,1024]{1,0:T(8,128)(2,1)S(1)}, bf16[128,1024]{1,0:T(8,128)(2,1)S(1)}, u32[]{:S(2)}, u32[]{:S(2)}) collective-permute-start(bf16[128,1024]{1,0:T(8,128)(2,1)S(1)} %get-tuple-element.85), channel_id=1, source_target_pairs={{8,16},{16,8},{9,17},{17,9},{10,18},{18,10},{11,19},{19,11},{12,20... | collective-permute-start | bytes 786440 | tf_op jit(solution)/shard_map/ppermute | solution.py:325
  66.6 8.1 %collective-permute-start.15 = (bf16[128,1024]{1,0:T(8,128)(2,1)S(1)}, bf16[128,1024]{1,0:T(8,128)(2,1)S(1)}, u32[]{:S(2)}, u32[]{:S(2)}) collective-permute-start(bf16[128,1024]{1,0:T(8,128)(2,1)S(1)} %get-tuple-element.86), channel_id=1, source_target_pairs={{0,8},{8,0},{16,24},{24,16},{1,9},{9,1},{17,25},{25,17},{2,10},{10... | collective-permute-start | bytes 786440 | tf_op jit(solution)/shard_map/ppermute | solution.py:324
  70.3 4.4 %collective-permute-start.16 = (bf16[128,1024]{1,0:T(8,128)(2,1)S(1)}, bf16[128,1024]{1,0:T(8,128)(2,1)S(1)}, u32[]{:S(2)}, u32[]{:S(2)}) collective-permute-start(bf16[128,1024]{1,0:T(8,128)(2,1)S(1)} %get-tuple-element.87), channel_id=1, source_target_pairs={{8,16},{16,8},{9,17},{17,9},{10,18},{18,10},{11,19},{19,11},{12,20... | collective-permute-start | bytes 786440 | tf_op jit(solution)/shard_map/ppermute | solution.py:325
  75.4 8.7 %collective-permute-start.17 = (bf16[128,1024]{1,0:T(8,128)(2,1)S(1)}, bf16[128,1024]{1,0:T(8,128)(2,1)S(1)}, u32[]{:S(2)}, u32[]{:S(2)}) collective-permute-start(bf16[128,1024]{1,0:T(8,128)(2,1)S(1)} %get-tuple-element.88), channel_id=1, source_target_pairs={{0,8},{8,0},{16,24},{24,16},{1,9},{9,1},{17,25},{25,17},{2,10},{10... | collective-permute-start | bytes 786440 | tf_op jit(solution)/shard_map/ppermute | solution.py:324
  79.4 4.7 %collective-permute-start.18 = (bf16[128,1024]{1,0:T(8,128)(2,1)S(1)}, bf16[128,1024]{1,0:T(8,128)(2,1)S(1)}, u32[]{:S(2)}, u32[]{:S(2)}) collective-permute-start(bf16[128,1024]{1,0:T(8,128)(2,1)S(1)} %get-tuple-element.89), channel_id=1, source_target_pairs={{8,16},{16,8},{9,17},{17,9},{10,18},{18,10},{11,19},{19,11},{12,20... | collective-permute-start | bytes 786440 | tf_op jit(solution)/shard_map/ppermute | solution.py:325
  84.9 26.1 %collective-permute-start.19 = (bf16[128,1024]{1,0:T(8,128)(2,1)S(1)}, bf16[128,1024]{1,0:T(8,128)(2,1)S(1)}, u32[]{:S(2)}, u32[]{:S(2)}) collective-permute-start(bf16[128,1024]{1,0:T(8,128)(2,1)S(1)} %get-tuple-element.90), channel_id=1, source_target_pairs={{0,8},{8,0},{16,24},{24,16},{1,9},{9,1},{17,25},{25,17},{2,10},{10... | collective-permute-start | bytes 786440 | tf_op jit(solution)/shard_map/ppermute | solution.py:324
  88.5 22.5 %collective-permute-start.20 = (bf16[128,1024]{1,0:T(8,128)(2,1)S(1)}, bf16[128,1024]{1,0:T(8,128)(2,1)S(1)}, u32[]{:S(2)}, u32[]{:S(2)}) collective-permute-start(bf16[128,1024]{1,0:T(8,128)(2,1)S(1)} %get-tuple-element.91), channel_id=1, source_target_pairs={{8,16},{16,8},{9,17},{17,9},{10,18},{18,10},{11,19},{19,11},{12,20... | collective-permute-start | bytes 786440 | tf_op jit(solution)/shard_map/ppermute | solution.py:325
  92.3 1.4 copy-start.1
  116.3 2.7 %collective-permute-start.21 = (bf16[4,4,128,256]{3,2,1,0:T(8,128)(2,1)S(1)}, bf16[4,4,128,256]{3,2,1,0:T(8,128)(2,1)S(1)}, u32[]{:S(2)}, u32[]{:S(2)}) collective-permute-start(bf16[4,4,128,256]{3,2,1,0:T(8,128)(2,1)S(1)} %get-tuple-element.122), channel_id=1, source_target_pairs={{0,1},{1,0},{2,3},{3,2},{4,5},{5,4},{6,7},{7,6},{8,9},{9,8},{10,11... | collective-permute-start | bytes 3145736 | tf_op jit(solution)/shard_map/ppermute | solution.py:511
  120.3 8.4 %collective-permute-start.22 = (bf16[4,2,128,128]{3,2,1,0:T(8,128)(2,1)S(1)}, bf16[4,2,128,128]{3,2,1,0:T(8,128)(2,1)S(1)}, u32[]{:S(2)}, u32[]{:S(2)}) collective-permute-start(bf16[4,2,128,128]{3,2,1,0:T(8,128)(2,1)S(1)} %get-tuple-element.124), channel_id=1, source_target_pairs={{0,2},{1,3},{2,0},{3,1},{4,6},{5,7},{6,4},{7,5},{8,10},{9,11},{10,... | collective-permute-start | bytes 786440 | tf_op jit(solution)/shard_map/ppermute | solution.py:511
  121.9 8.1 %collective-permute-start.23 = (bf16[4,2,128,128]{3,2,1,0:T(8,128)(2,1)S(1)}, bf16[4,2,128,128]{3,2,1,0:T(8,128)(2,1)S(1)}, u32[]{:S(2)}, u32[]{:S(2)}) collective-permute-start(bf16[4,2,128,128]{3,2,1,0:T(8,128)(2,1)S(1)} %get-tuple-element.126), channel_id=1, source_target_pairs={{0,4},{1,5},{2,6},{3,7},{4,0},{5,1},{6,2},{7,3},{8,12},{9,13},{10,... | collective-permute-start | bytes 786440 | tf_op jit(solution)/shard_map/ppermute | solution.py:511
  130.7 6.5 %collective-permute-start.24 = (bf16[4,1,128,128]{3,2,1,0:T(8,128)(2,1)S(1)}, bf16[4,1,128,128]{3,2,1,0:T(8,128)(2,1)S(1)}, u32[]{:S(2)}, u32[]{:S(2)}) collective-permute-start(bf16[4,1,128,128]{3,2,1,0:T(8,128)(2,1)S(1)} %get-tuple-element.128), channel_id=1, source_target_pairs={{0,4},{1,5},{2,6},{3,7},{4,0},{5,1},{6,2},{7,3},{8,12},{9,13},{10,... | collective-permute-start | bytes 393224 | tf_op jit(solution)/shard_map/ppermute | solution.py:511
  131.3 5.9 %collective-permute-start.25 = (bf16[4,1,128,128]{3,2,1,0:T(8,128)(2,1)S(1)}, bf16[4,1,128,128]{3,2,1,0:T(8,128)(2,1)S(1)}, u32[]{:S(2)}, u32[]{:S(2)}) collective-permute-start(bf16[4,1,128,128]{3,2,1,0:T(8,128)(2,1)S(1)} %get-tuple-element.130), channel_id=1, source_target_pairs={{0,2},{1,3},{2,0},{3,1},{4,6},{5,7},{6,4},{7,5},{8,10},{9,11},{10,... | collective-permute-start | bytes 393224 | tf_op jit(solution)/shard_map/ppermute | solution.py:511
  137.9 16.0 %collective-permute-start.26 = (bf16[128,256]{1,0:T(8,128)(2,1)S(1)}, bf16[128,256]{1,0:T(8,128)(2,1)S(1)}, u32[]{:S(2)}, u32[]{:S(2)}) collective-permute-start(bf16[128,256]{1,0:T(8,128)(2,1)S(1)} %get-tuple-element.132), channel_id=1, source_target_pairs={{0,8},{8,16},{16,24},{24,0},{1,9},{9,17},{17,25},{25,1},{2,10},{10... | collective-permute-start | bytes 196616 | tf_op jit(solution)/shard_map/ppermute | solution.py:616
  139.7 14.3 %collective-permute-start.27 = (bf16[128,256]{1,0:T(8,128)(2,1)S(1)}, bf16[128,256]{1,0:T(8,128)(2,1)S(1)}, u32[]{:S(2)}, u32[]{:S(2)}) collective-permute-start(bf16[128,256]{1,0:T(8,128)(2,1)S(1)} %get-tuple-element.133), channel_id=1, source_target_pairs={{0,16},{8,24},{16,0},{24,8},{1,17},{9,25},{17,1},{25,9},{2,18},{10... | collective-permute-start | bytes 196616 | tf_op jit(solution)/shard_map/ppermute | solution.py:616
  140.7 13.2 %collective-permute-start.28 = (bf16[128,256]{1,0:T(8,128)(2,1)S(1)}, bf16[128,256]{1,0:T(8,128)(2,1)S(1)}, u32[]{:S(2)}, u32[]{:S(2)}) collective-permute-start(bf16[128,256]{1,0:T(8,128)(2,1)S(1)} %get-tuple-element.134), channel_id=1, source_target_pairs={{0,24},{8,0},{16,8},{24,16},{1,25},{9,1},{17,9},{25,17},{2,26},{10... | collective-permute-start | bytes 196616 | tf_op jit(solution)/shard_map/ppermute | solution.py:616
where the time goes:
time: 155 us
  Pallas kernels  69.5 us (45%)
  starting transfers between devices  43.4 us (28%)
  waiting for transfers between devices  38.3 us (25%)
    ppermute x6, starting transfers between devices, pass_states(): ra = lax.ppermute(sa, 'seq', pairs_a)  21.2 us
    ppermute x6, waiting for transfers between devices, pass_states(): ra = lax.ppermute(sa, 'seq', pairs_a)  20.1 us
    pallas_call x4, Pallas kernels, state_piece(): pl.pallas_call(functools.partial(piece_kernel, piece=piece, ps=d // heads...  19.1 us
    ppermute x14, waiting for transfers between devices, flip(): return lax.ppermute(x, 'fsdp', [(i, i ^ bit) for i in range(count)])  18.2 us
    ppermute x14, starting transfers between devices, flip(): return lax.ppermute(x, 'fsdp', [(i, i ^ bit) for i in range(count)])  12.3 us
    pallas_call x2, Pallas kernels, finish(): pl.pallas_call(finish_kernel, grid=(number,), in_specs=in_specs, out_spec...  10.3 us
    pallas_call x6, Pallas kernels, absorb(): pl.pallas_call(functools.partial(absorb_kernel, j=j), grid_spec=pltpu.Pre...  8.26 us
    pallas_call x1, Pallas kernels, scale_heads(): pl.pallas_call(functools.partial(scale_heads_kernel, heads=heads), grid=(...  6.12 us
  transfers between devices with their start and end apart: 29, of which 10 were waited for; matrix products, arithmetic and copies ran while one was open for 1% of the time, Pallas kernels for 33%

commit v1 on v0

v1 whole, which is shorter than its diff:
```python
import functools

import jax
import jax.numpy as jnp
from jax import lax
from jax.experimental import pallas as pl
from jax.experimental.pallas import tpu as pltpu
from jax.sharding import PartitionSpec as P


CHUNK = 128
PIECES = 4
MIB = 1024 * 1024

f32 = jnp.float32
bf16 = jnp.bfloat16
norm_epsilon = 1e-05
decay_unit = 1.0 / 4096.0


def dot(a, b, ca, cb):
    return lax.dot_general(a, b, (((ca,), (cb,)), ((), ())), preferred_element_type=f32)


def params(mib):
    return pltpu.CompilerParams(vmem_limit_bytes=mib * MIB)


def cost(flops, nbytes):
    return pl.CostEstimate(flops=int(flops), bytes_accessed=int(nbytes), transcendentals=0)


def shape(s, d):
    return jax.ShapeDtypeStruct(s, d)


def near(x):
    return pltpu.with_memory_space_constraint(x, pltpu.VMEM)


def kept(s, d):
    return pltpu.VMEM(s, d)


def span(i, n):
    return pl.ds(pl.multiple_of(i * n, n), n)


VM = pl.BlockSpec(memory_space=pltpu.VMEM)
SM = pl.BlockSpec(memory_space=pltpu.SMEM)


def normalize_kernel(meta, mid, decay, x_o, rstd_o, a_o, b_o, half_o, *, heads):
    del meta
    q, d = CHUNK, mid.shape[1]
    ps = d // heads
    own = span(pl.program_id(0), q)
    values = mid[own, :].astype(f32)
    rstd = lax.rsqrt(jnp.mean(values * values, axis=-1, keepdims=True) + norm_epsilon)
    i = pl.program_id(0)
    rstd_o[own, :] = rstd
    x_o[own, :] = (values * rstd).astype(bf16)
    rates = decay[...].astype(f32)
    running = (
        jnp.dot(causal(q).astype(f32), rates, precision=lax.Precision.HIGHEST, preferred_element_type=f32)
        * decay_unit
    )
    mid_log = 0.5 * running[q - 1 : q, :]
    a_o[own, :] = jnp.exp(running - mid_log) * (ps ** (-0.5))
    b_o[own, :] = jnp.exp(mid_log - running) * jnp.sqrt(1.0 - jnp.exp(2.0 * (rates * decay_unit)))
    half = jnp.exp(mid_log)
    for h in range(heads):
        half_o[i, :, h * ps : (h + 1) * ps] = jnp.broadcast_to(half[:, h : h + 1], (8, ps))


def normalize(meta, mid, decay):
    t, d = mid.shape
    heads = decay.shape[1]
    n = t // CHUNK
    row = lambda w: pl.BlockSpec((CHUNK, w), lambda i: (i, 0))
    return pl.pallas_call(
        functools.partial(normalize_kernel, heads=heads),
        grid=(n,),
        in_specs=[SM, VM, row(heads)],
        out_specs=[VM] * 5,
        out_shape=[kept((t, d), bf16), kept((t, 1), f32), kept((t, heads), f32), kept((t, heads), f32),
                   kept((n, 8, d), f32)],
        compiler_params=params(12),
        cost_estimate=cost(30 * t * d, 4 * t * d),
        name="normalize",
    )(meta, near(mid), decay)


def scale_heads_kernel(x, cot, a, b, v_o, g_o, spread):
    q, d = CHUNK, cot.shape[1]
    heads = a.shape[1]
    ps = d // heads
    i = pl.program_id(0)

    @pl.when(i == 0)
    def _():
        head = lax.rem(lax.broadcasted_iota(jnp.int32, spread.shape, 0), heads)
        col = lax.div(lax.broadcasted_iota(jnp.int32, spread.shape, 1), ps)
        spread[...] = jnp.where(head == col, 1.0, 0.0).astype(bf16)

    own = span(i, q)
    both = jnp.concatenate([a[own, :], b[own, :]], axis=0)
    high = both.astype(bf16)
    low = (both - high.astype(f32)).astype(bf16)
    parts = jnp.concatenate([high, low], axis=1)
    w = 4 * ps
    for c in range(d // w):
        cols = slice(c * w, (c + 1) * w)
        wide = dot(parts, spread[:, cols], 1, 0)
        v_o[own, cols] = (x[own, cols].astype(f32) * wide[q:]).astype(bf16)
        g_o[own, cols] = (cot[own, cols].astype(f32) * wide[:q]).astype(bf16)


def scale_heads(x, cot, a, b):
    t, d = x.shape
    return pl.pallas_call(
        scale_heads_kernel,
        grid=(t // CHUNK,),
        in_specs=[VM] * 4,
        out_specs=[VM, VM],
        out_shape=[kept((t, d), bf16)] * 2,
        scratch_shapes=[pltpu.VMEM((2 * a.shape[1], d), bf16)],
        compiler_params=params(8),
        cost_estimate=cost(10 * t * d, 8 * t * d),
        name="scale_heads",
    )(near(x), near(cot), near(a), near(b))


def project_kernel(meta, x, *refs, keys, block):
    weights, (out, full) = refs[:-2], refs[-2:]
    f = meta[0]
    total = None
    for (k, lo), w in zip(keys, weights):
        start = pl.multiple_of(jnp.bitwise_xor(f, k) * block + lo, 128)
        full[pl.ds(start, w.shape[0]), :] = w[...]
        part = dot(x[:, pl.ds(start, w.shape[0])], w[...], 1, 0)
        total = part if total is None else total + part
    out[...] = total.astype(bf16)


def project(meta, x, keys, pieces, block):
    t, d = x.shape
    n2 = pieces[0].shape[1]
    full = pl.BlockSpec(memory_space=pltpu.VMEM)
    return pl.pallas_call(
        functools.partial(project_kernel, keys=keys, block=block),
        in_specs=[pl.BlockSpec(memory_space=pltpu.SMEM), full] + [full] * len(pieces),
        out_specs=[full, full],
        out_shape=[kept((t, n2), bf16), kept((d, n2), bf16)],
        compiler_params=params(16),
        cost_estimate=cost(2 * t * d * n2, 2 * (t * d + d * n2)),
        name="project",
    )(meta, near(x), *pieces)


def states_kernel(meta, p, v, g, half, *refs, first, pieces):
    sl_o, dl_o, loc_o, dtot_o = refs[:4] if first else refs[-4:]
    t, d = v.shape
    w = d // PIECES
    n = p.shape[1] // 2
    count = t // CHUNK
    for at, piece in enumerate(pieces):
        cols = slice(piece * w, (piece + 1) * w)
        here = slice(at * w, (at + 1) * w)
        state = jnp.zeros((n, w), f32)
        total = jnp.ones((8, w), f32)
        for k in range(count):
            rows = slice(k * CHUNK, (k + 1) * CHUNK)
            hk = half[k, 0:1, cols]
            state = state * hk
            sl_o[k, :, here] = state.astype(bf16)
            state = (state + dot(p[rows, :n], v[rows, cols], 0, 0)) * hk
            total = total * half[k, :, cols] * half[k, :, cols]
        onward = state
        loc_o[0, piece] = onward.astype(bf16)
        dtot_o[:, cols] = total
        state = jnp.zeros((n, w), f32)
        for k in reversed(range(count)):
            rows = slice(k * CHUNK, (k + 1) * CHUNK)
            hk = half[k, 0:1, cols]
            state = state * hk
            dl_o[k, :, here] = state.astype(bf16)
            state = (state + dot(p[rows, n:], g[rows, cols], 0, 0)) * hk
        loc_o[1, piece] = state.astype(bf16)
        if first:
            oa, ob = refs[4:]
            odd = meta[2] == 1
            oa[...] = jnp.where(odd, state, onward).astype(bf16)
            ob[...] = jnp.where(odd, onward, state).astype(bf16)


def states(meta, p, v, g, half, previous):
    t, d = v.shape
    n = p.shape[1] // 2
    count = t // CHUNK
    w = d // PIECES
    first = previous is None
    pieces = range(1) if first else range(1, PIECES)
    number = len(pieces)
    args = [meta, near(p), near(v), near(g), near(half)]
    out_shape = [kept((count, n, number * w), bf16)] * 2 + [kept((2, PIECES, n, w), bf16), kept((8, d), f32)]
    aliases = {}
    if first:
        out_shape += [shape((n, w), bf16)] * 2
    else:
        aliases = {5: 2, 6: 3}
        args += [near(previous[0]), near(previous[1])]
    return pl.pallas_call(
        functools.partial(states_kernel, first=first, pieces=pieces),
        in_specs=[SM] + [VM] * (len(args) - 1),
        out_specs=[VM] * len(out_shape),
        out_shape=out_shape,
        input_output_aliases=aliases,
        compiler_params=params(8),
        cost_estimate=cost(4 * t * w * n * number, 8 * t * w * number),
    )(*args)


def hop_kernel(ids, ra, rb, loc, dtot, oa, ob, *, j):
    w = ra.shape[1]
    base = 2 + 8 * j
    for c, came, out in ((0, rb, oa), (2, ra, ob)):
        at = ids[base + c + 1]
        decay = dtot[0:1, span(at, w)]
        out[...] = (loc[ids[base + c], at].astype(f32) + decay * came[...].astype(f32)).astype(bf16)


def hop(ids, j, ra, rb, loc, dtot):
    n, w = ra.shape
    return pl.pallas_call(
        functools.partial(hop_kernel, j=j),
        in_specs=[SM] + [VM] * 4,
        out_specs=[VM, VM],
        out_shape=[shape((n, w), bf16)] * 2,
        compiler_params=params(4),
        cost_estimate=cost(4 * n * w, 12 * n * w),
    )(ids, ra, rb, near(loc), near(dtot))


def absorb_kernel(ids, ra, rb, v, g, half, *refs, j, fresh):
    si_o, di_o, acc = refs[-3:]
    t = v.shape[0]
    n, w = ra.shape
    count = t // CHUNK
    base = 2 + 8 * j
    odd = ids[base] == 1
    fa = ra[...].astype(f32)
    fb = rb[...].astype(f32)
    ahead = jnp.where(odd, fa, fb)
    behind = jnp.where(odd, fb, fa)
    if fresh:
        si_o[...] = jnp.zeros_like(si_o)
        di_o[...] = jnp.zeros_like(di_o)
        acc[...] = jnp.zeros_like(acc)
    si_o[ids[base + 5]] = ahead.astype(bf16)
    di_o[ids[base + 7]] = behind.astype(bf16)
    for c, state, order, other, part in ((4, ahead, range(count), g, slice(n, 2 * n)),
                                         (6, behind, reversed(range(count)), v, slice(0, n))):
        at = ids[base + c]

        @pl.when(at == ids[base + c + 1])
        def _():
            cols = span(at, w)
            carry = jnp.ones((1, w), f32)
            for k in order:
                rows = slice(k * CHUNK, (k + 1) * CHUNK)
                hk = half[k, 0:1, cols]
                acc[rows, part] += dot(other[rows, cols], (state * (carry * hk)).astype(bf16), 1, 1)
                carry = carry * hk * hk


def absorb(ids, j, ra, rb, v, g, half, held):
    t, _ = v.shape
    n, w = ra.shape
    args = [ids, ra, rb, near(v), near(g), near(half)]
    aliases = {}
    if held is not None:
        aliases = {6: 0, 7: 1, 8: 2}
        args += map(near, held)
    return pl.pallas_call(
        functools.partial(absorb_kernel, j=j, fresh=held is None),
        in_specs=[SM] + [VM] * (len(args) - 1),
        out_specs=[VM] * 3,
        out_shape=[kept((PIECES + 1, n, w), bf16)] * 2 + [kept((t, 2 * n), f32)],
        input_output_aliases=aliases,
        compiler_params=params(6),
        cost_estimate=cost(4 * t * w * n, 4 * t * w),
    )(*args)


def places():
    count = lax.axis_size("seq")
    z = lax.axis_index("seq")
    j = jnp.arange(PIECES + count - 2, dtype=jnp.int32)
    odd = jnp.zeros_like(j) + z % 2
    clip = lambda at: jnp.clip(at, 0, PIECES - 1)
    slot = lambda at: jnp.where((at >= 0) & (at < PIECES), at, PIECES)
    ahead, behind = j - z, j - (count - 1 - z)
    first = jnp.where(odd == 1, behind, ahead)
    second = jnp.where(odd == 1, ahead, behind)
    ids = jnp.stack(
        [odd, clip(first), 1 - odd, clip(second),
         clip(ahead + 1), slot(ahead + 1), clip(behind + 1), slot(behind + 1)], axis=1).reshape(-1)
    own = jnp.stack([lax.axis_index("fsdp"), z]).astype(jnp.int32)
    return jnp.concatenate([own, ids])


def pass_states(ids, sa, sb, loc, dtot, v, g, half):
    count = lax.axis_size("seq")
    steps = PIECES + count - 2
    pairs_a = [(i, i ^ 1) for i in range(count) if i ^ 1 < count]
    pairs_b = [p for i in range(1, count - 1, 2) for p in ((i, i + 1), (i + 1, i))]
    held = None
    done = []
    for step in range(steps):
        if step:
            sa, sb = hop(ids, step, ra, rb, loc, dtot)
        ra = lax.ppermute(sa, "seq", pairs_a)
        rb = lax.ppermute(sb, "seq", pairs_b)
        held = absorb(ids, step, ra, rb, v, g, half, held)
        if step >= count - 2:
            done.append(held[:2])
    return held[2], done


def causal(q):
    return lax.broadcasted_iota(jnp.int32, (q, q), 0) >= lax.broadcasted_iota(jnp.int32, (q, q), 1)


def inner_grad_kernel(p, v, g, sa, da, sb, db, out, *, k):
    n = p.shape[1] // 2
    w = sa.shape[2]
    rows = slice(k * CHUNK, (k + 1) * CHUNK)
    entry, readout = p[rows, :n], p[rows, n:]
    scores = jnp.where(causal(CHUNK), dot(g[rows, :], v[rows, :], 1, 1), 0.0).astype(bf16)
    out[:, :n] = dot(scores, readout, 0, 0) + dot(v[rows, :w], da[k], 1, 1) + dot(v[rows, w:], db[k], 1, 1)
    out[:, n:] = dot(scores, entry, 1, 0) + dot(g[rows, :w], sa[k], 1, 1) + dot(g[rows, w:], sb[k], 1, 1)


def inner_grad(p, v, g, sa, da, sb, db, k):
    _, d = v.shape
    n2 = p.shape[1]
    return pl.pallas_call(
        functools.partial(inner_grad_kernel, k=k),
        in_specs=[VM] * 7,
        out_specs=VM,
        out_shape=kept((CHUNK, n2), f32),
        compiler_params=params(6),
        cost_estimate=cost(6 * CHUNK * d * CHUNK, 8 * CHUNK * d),
    )(*map(near, (p, v, g, sa, da, sb, db)))


def weight_grad_kernel(meta, x, *refs, first):
    if first:
        acc, inner, (away, kept_o, low, term) = refs[0], refs[1:-4], refs[-4:]
        for k, part in enumerate(inner):
            rows = slice(k * CHUNK, (k + 1) * CHUNK)
            low[rows, :] = (acc[rows, :] + part[...]).astype(bf16)
    else:
        low, away, kept_o, term = refs
    number, half, rows, _ = away.shape
    w = term.shape[0]
    mine = lax.rem(meta[0], 2)
    for j in range(number):
        at = j if first else j + number
        term[...] = dot(x[:, at * w : (at + 1) * w], low[...], 0, 0)
        for i in range(half):
            kept_o[j, i] = term[span(2 * i + mine, rows), :].astype(bf16)
            away[j, i] = term[span(2 * i + 1 - mine, rows), :].astype(bf16)


def weight_grad(meta, x, sources, first):
    t, d = x.shape
    n2 = sources[0].shape[1]
    along, count = lax.axis_size("seq"), lax.axis_size("fsdp")
    w = d // along
    number = along // 2
    blocks = (number, count // 2, w // count, n2)
    out_shape = [shape(blocks, bf16), kept(blocks, bf16)] + ([kept((t, n2), bf16)] if first else [])
    return pl.pallas_call(
        functools.partial(weight_grad_kernel, first=first),
        in_specs=[SM, VM] + [VM] * len(sources),
        out_specs=[VM] * len(out_shape),
        out_shape=out_shape,
        scratch_shapes=[pltpu.VMEM((w, n2), f32)],
        compiler_params=params(8),
        cost_estimate=cost(2 * t * w * number * n2, 2 * t * w * number),
    )(meta, near(x), *map(near, sources))


def piece_kernel(x, v, g, cot, newest, p, sl, dl, si, di, half, skip, a, b, *refs, piece, at, ps):
    rebuilt_o, back_o, rhs, lhs = refs[-4:]
    q, w = rebuilt_o.shape
    n = p.shape[1] // 2
    per = w // ps
    k = pl.program_id(0)
    rows = span(k, q)
    cols = slice(piece * w, (piece + 1) * w)
    here = slice(at * w, (at + 1) * w)
    ahead = jnp.ones((1, w), f32)
    behind = ahead
    for j in range(half.shape[0]):
        hj = half[j, 0:1, cols]
        sq = hj * hj
        own = jnp.where(j == k, hj, 1.0)
        ahead = ahead * jnp.where(j < k, sq, own)
        behind = behind * jnp.where(j > k, sq, own)
    entry, readout = p[rows, :n], p[rows, n:]
    scores = jnp.where(causal(q), dot(readout, entry, 1, 1), 0.0)
    lhs[:, :q] = scores.astype(bf16)
    lhs[:, q:] = readout
    rhs[:q, :] = v[rows, cols]
    rhs[q:, :] = (sl[k, :, here].astype(f32) + si[piece].astype(f32) * ahead).astype(bf16)
    mixed = dot(lhs[...], rhs[...], 1, 0)
    av, bv = a[rows, :], b[rows, :]
    for h in range(per):
        hh = piece * per + h
        own = slice(h * ps, (h + 1) * ps)
        wide = slice(hh * ps, (hh + 1) * ps)
        y = mixed[:, own] * av[:, hh : hh + 1] + skip[0:1, wide] * x[rows, wide].astype(f32)
        rebuilt_o[:, own] = (newest[rows, wide].astype(f32) - y).astype(bf16)
    lhs[:, :q] = scores.T.astype(bf16)
    lhs[:, q:] = entry
    rhs[:q, :] = g[rows, cols]
    rhs[q:, :] = (dl[k, :, here].astype(f32) + di[piece].astype(f32) * behind).astype(bf16)
    back = dot(lhs[...], rhs[...], 1, 0)
    for h in range(per):
        hh = piece * per + h
        own = slice(h * ps, (h + 1) * ps)
        wide = slice(hh * ps, (hh + 1) * ps)
        gr = back[:, own] * bv[:, hh : hh + 1] + skip[0:1, wide] * cot[rows, wide].astype(f32)
        back_o[rows, own] = gr.astype(bf16)


def state_piece(x, v, g, cot, newest, p, sl, dl, si, di, half, skip, a, b, piece, previous):
    t, d = x.shape
    n2 = p.shape[1]
    n = n2 // 2
    heads = a.shape[1]
    w = d // PIECES
    cols = pl.BlockSpec((CHUNK, w), lambda i: (i, piece))
    args = [near(x), near(v), near(g), near(cot), near(newest),
            *map(near, (p, sl, dl, si, di, half)), skip, near(a), near(b)]
    in_specs = [VM] * 14
    aliases = {}
    if previous is not None:
        aliases = {len(args): 0}
        args.append(previous)
        in_specs.append(pl.BlockSpec(memory_space=pltpu.HBM))
    return pl.pallas_call(
        functools.partial(piece_kernel, piece=piece, at=max(piece - 1, 0), ps=d // heads),
        grid=(t // CHUNK,),
        in_specs=in_specs,
        out_specs=[cols, VM],
        out_shape=[pltpu.HBM((t, d), bf16), kept((t, w), bf16)],
        scratch_shapes=[pltpu.VMEM((CHUNK + n, w), bf16), pltpu.VMEM((CHUNK, CHUNK + n), bf16)],
        input_output_aliases=aliases,
        compiler_params=params(8),
        cost_estimate=cost(8 * t * w * n, 18 * t * w),
    )(*args)


def finish_kernel(x, midcot, low, rstd, weights, *refs, first):
    backs = refs[:PIECES]
    grad_o, grad = refs[-2:]
    q, d = grad_o.shape
    rows = span(first + pl.program_id(0), q)
    lhs = low[rows, :]
    w = d // PIECES
    step = 256
    sums = jnp.zeros((q, 128), f32)
    for i in range(d // step):
        cols = slice(i * step, (i + 1) * step)
        inside = slice(i * step % w, i * step % w + step)
        gr = dot(lhs, weights[cols, :], 1, 1) + backs[i * step // w][rows, inside].astype(f32)
        grad[:, cols] = gr
        prod = gr * x[rows, cols].astype(f32)
        for c in range(step // 128):
            sums = sums + prod[:, c * 128 : (c + 1) * 128]
    scale = jnp.broadcast_to(rstd[rows, :], (q, 128))
    dots = jnp.broadcast_to(jnp.sum(sums, axis=-1, keepdims=True), (q, 128)) * (scale * (1.0 / d))
    for i in range(d // 128):
        cols = slice(i * 128, (i + 1) * 128)
        dx = scale * grad[:, cols] - x[rows, cols].astype(f32) * dots
        grad_o[:, cols] = (midcot[rows, cols].astype(f32) + dx).astype(bf16)


def finish(x, backs, midcot, low, rstd, weights, first, number, previous):
    t, d = x.shape
    n2 = low.shape[1]
    row = pl.BlockSpec((CHUNK, d), lambda i: (first + i, 0))
    args = [near(x), near(midcot), near(low), near(rstd), near(weights), *map(near, backs)]
    in_specs = [VM] * (5 + PIECES)
    aliases = {}
    if previous is not None:
        aliases = {len(args): 0}
        args.append(previous)
        in_specs.append(pl.BlockSpec(memory_space=pltpu.HBM))
    return pl.pallas_call(
        functools.partial(finish_kernel, first=first),
        grid=(number,),
        in_specs=in_specs,
        out_specs=row,
        out_shape=pltpu.HBM((t, d), bf16),
        scratch_shapes=[pltpu.VMEM((CHUNK, d), f32)],
        input_output_aliases=aliases,
        compiler_params=params(12),
        cost_estimate=cost(2 * number * CHUNK * d * n2, 8 * number * CHUNK * d),
    )(*args)


def flip(x, bit):
    count = lax.axis_size("fsdp")
    return lax.ppermute(x, "fsdp", [(i, i ^ bit) for i in range(count)])


def gather_weights(w):
    count = lax.axis_size("fsdp")
    rows = w.shape[0]
    if count == 8:
        across, along = flip(w, 2), flip(w, 4)
        mid = rows // 2
        held = [(0, 0, w), (2, 0, across), (4, 0, along),
                (6, 0, flip(across[:mid], 4)), (6, mid, flip(along[mid:], 2))]
        held += [(k | 1, lo, flip(a, 1)) for k, lo, a in held]
    else:
        held = [(0, 0, w)]
        bit = count // 2
        while bit:
            held += [(k | bit, lo, flip(a, bit)) for k, lo, a in held]
            bit //= 2
    return [(k, lo) for k, lo, _ in held], [a for _, _, a in held]


def halve(value, away, kept_o, mine, pos):
    low = 1 << pos
    for i in range(away.shape[1]):
        base = (i // low) * 2 * low + i % low
        kept_o[:, i] = value(base + mine * low)
        away[:, i] = value(base + (1 - mine) * low)


def fold_kernel(meta, *refs, first, left, right):
    f = meta[0]
    bit = lambda b: lax.rem(lax.div(f, b), 2)
    pos = lambda b, order: sorted(order).index(b)
    if first:
        k0, g0, k1, g1, al, kl, ar, kr, total = refs
        part = k0.shape[0]
        total[:part] = (k0[...].astype(f32) + g0[...].astype(f32)).astype(bf16)
        total[part:] = (k1[...].astype(f32) + g1[...].astype(f32)).astype(bf16)
        n = al.shape[-1]
        halve(lambda m: total[:, m, :, :n], al, kl, bit(left[0]), pos(left[0], left))
        halve(lambda m: total[:, m, :, n:], ar, kr, bit(right[0]), pos(right[0], right))
        return
    kl, gl, kr, gr, al_o, kl_o, ar_o, kr_o, tl, tr = refs
    tl[...] = (kl[...].astype(f32) + gl[...].astype(f32)).astype(bf16)
    tr[...] = (kr[...].astype(f32) + gr[...].astype(f32)).astype(bf16)
    halve(lambda m: tl[:, m], al_o, kl_o, bit(left[0]), pos(left[0], left))
    halve(lambda m: tr[:, m], ar_o, kr_o, bit(right[0]), pos(right[0], right))


def fold(meta, arrays, left, right, first):
    along, blocks, rows, n = arrays[0].shape
    if first:
        along, n = 2 * along, n // 2
    out = (along, blocks // 2, rows, n)
    vmem = pl.BlockSpec(memory_space=pltpu.VMEM)
    scratch = [pltpu.VMEM((along, blocks, rows, 2 * n), bf16)] if first else [pltpu.VMEM(arrays[0].shape, bf16)] * 2
    return pl.pallas_call(
        functools.partial(fold_kernel, first=first, left=left, right=right),
        in_specs=[pl.BlockSpec(memory_space=pltpu.SMEM)] + [vmem] * len(arrays),
        out_specs=[vmem] * 4,
        out_shape=[shape(out, bf16), kept(out, bf16)] * 2,
        scratch_shapes=scratch,
        compiler_params=params(10),
        cost_estimate=cost(0, 8 * along * blocks * rows * n),
    )(meta, *arrays)


def deal_kernel(meta, kl, gl, kr, gr, own, *refs):
    _, _, _, n = kl.shape
    sends, both = refs[:-1], refs[-1]
    z = meta[1]
    both[:, :, :n] = (kl[:, 0].astype(f32) + gl[:, 0].astype(f32)).astype(bf16)
    both[:, :, n:] = (kr[:, 0].astype(f32) + gr[:, 0].astype(f32)).astype(bf16)
    own[...] = both[z]
    for k, out in enumerate(sends, 1):
        out[...] = both[jnp.bitwise_xor(z, k)]


def deal(meta, arrays):
    along, _, rows, n = arrays[0].shape
    vmem = pl.BlockSpec(memory_space=pltpu.VMEM)
    return pl.pallas_call(
        deal_kernel,
        in_specs=[pl.BlockSpec(memory_space=pltpu.SMEM)] + [vmem] * 4,
        out_specs=[vmem] * along,
        out_shape=[shape((rows, 2 * n), bf16)] * along,
        scratch_shapes=[pltpu.VMEM((along, rows, 2 * n), bf16)],
        compiler_params=params(8),
        cost_estimate=cost(0, 8 * along * rows * n),
        name="deal",
    )(meta, *arrays)


def scatter_sum(meta, halves):
    along = lax.axis_size("seq")
    count = lax.axis_size("fsdp")
    left = [1 << i for i in range(1, count.bit_length() - 1)]
    right = left[::-1]
    arrays = []
    for away, stays in halves:
        arrays += [stays, flip(away, 1)]
    al, kl, ar, kr = fold(meta, arrays, left, right, True)
    for _ in range(len(left)):
        gl, gr = flip(al, left[0]), flip(ar, right[0])
        left, right = left[1:], right[1:]
        if left:
            al, kl, ar, kr = fold(meta, [kl, gl, kr, gr], left, right, False)
    own, *sends = deal(meta, [kl, gl, kr, gr])
    total = own.astype(f32)
    for k, block in enumerate(sends, 1):
        other = lax.ppermute(block, "seq", [(i, i ^ k) for i in range(along)])
        total = total + other.astype(f32)
    return total


def step(middle_state, newest_state, middle_cotangent, newest_cotangent, log_decay, state_weights, skip_gain):
    t, d = middle_state.shape[1:]
    heads = log_decay.shape[2]
    middle, newest, midcot, cot = middle_state[0], newest_state[0], middle_cotangent[0], newest_cotangent[0]
    meta = places()
    block = state_weights.shape[0]
    count = t // CHUNK
    keys, pieces = gather_weights(state_weights)
    x, rstd, a, b, half = normalize(meta, middle, log_decay[0])
    v, g = scale_heads(x, cot, a, b)
    p, weights = project(meta, x, keys, pieces, block)
    s0, d0, loc, dtot, sa, sb = states(meta, p, v, g, half, None)
    s1, d1, loc, dtot = states(meta, p, v, g, half, (loc, dtot))
    inner = [inner_grad(p, v, g, s0, d0, s1, d1, k) for k in range(count)]
    acc, heads_done = pass_states(meta, sa, sb, loc, dtot, v, g, half)
    *half0, low = weight_grad(meta, x, [acc, *inner], True)
    half1 = weight_grad(meta, x, [low], False)
    skip = jnp.repeat(skip_gain, d // heads)[None]
    rebuilt, backs = None, []
    for i in range(PIECES):
        sp, dp = heads_done[i]
        rebuilt, back = state_piece(
            x, v, g, cot, newest, p, s1 if i else s0, d1 if i else d0, sp, dp, half, skip, a, b, i, rebuilt)
        backs.append(back)
    gradient = None
    for i in range(2):
        gradient = finish(x, backs, midcot, low, rstd, weights,
                          i * count // 2, count // 2, gradient)
    summed = scatter_sum(meta, [half0, half1])
    scale = (t * lax.axis_size("seq") * lax.axis_size("fsdp")) ** (-0.5)
    return rebuilt[None], gradient[None], summed * scale


def solution(mesh):
    whole = P("fsdp", "seq", None)
    return jax.shard_map(
        step,
        mesh=mesh,
        in_specs=(whole, whole, whole, whole, whole, P("fsdp", None), P()),
        out_specs=(whole, whole, P(("seq", "fsdp"), None)),
        check_vma=False,
    )
```

time: 155 us -> 141 us (0.910)
  Pallas kernels: 69.5 us -> 56.8 us
  waiting for transfers between devices: 38.3 us -> 35.6 us
  local copies, waits for them, and re-layouts: 1.54 us -> 4.09 us
    pallas_call x25 -> x26, Pallas kernels: 60.7 us -> 49.5 us  [the longest x4 12.1 us: state_piece(): pl.pallas_call(functools.partial(piece_kernel, piece=piece, at=max(piece...]
    ppermute x6, waiting for transfers between devices: 20.1 us -> 17.1 us  [pass_states(): ra = lax.ppermute(sa, 'seq', pairs_a)]
    unnamed x5 -> x13, local copies, waits for them, and re-layouts: 0.98 us -> 3.83 us
    ppermute x6, starting transfers between devices: 21.2 us -> 19.4 us  [pass_states(): ra = lax.ppermute(sa, 'seq', pairs_a)]
    ppermute x14 -> x15, starting transfers between devices: 12.3 us -> 12.8 us  [flip(): return lax.ppermute(x, 'fsdp', [(i, i ^ bit) for i in range(count)])]
    ppermute x14 -> x15, waiting for transfers between devices: 18.2 us -> 18.4 us  [flip(): return lax.ppermute(x, 'fsdp', [(i, i ^ bit) for i in range(count)])]
  transfers between devices with their start and end apart: 29 -> 30, of which waited for: 10 -> 13; matrix products, arithmetic and copies ran while one was open for 1% -> 1% of each run, Pallas kernels for 33% -> 30%
where the time goes in v1:
time: 141 us; the launch traced here: 140 us
  Pallas kernels  56.8 us (40%)
  starting transfers between devices  42.2 us (30%)
  waiting for transfers between devices  35.6 us (25%)
  local copies, waits for them, and re-layouts  4.09 us (3%)
    ppermute x6, starting transfers between devices, pass_states(): ra = lax.ppermute(sa, 'seq', pairs_a)  19.4 us
    ppermute x15, waiting for transfers between devices, flip(): return lax.ppermute(x, 'fsdp', [(i, i ^ bit) for i in range(count)])  18.4 us
    ppermute x6, waiting for transfers between devices, pass_states(): ra = lax.ppermute(sa, 'seq', pairs_a)  17.1 us
    ppermute x15, starting transfers between devices, flip(): return lax.ppermute(x, 'fsdp', [(i, i ^ bit) for i in range(count)])  12.8 us
    pallas_call x4, Pallas kernels, state_piece(): pl.pallas_call(functools.partial(piece_kernel, piece=piece, at=max(piece...  12.1 us
    pallas_call x2, Pallas kernels, finish(): pl.pallas_call(functools.partial(finish_kernel, first=first), grid=(numbe...  8.21 us
    pallas_call x6, Pallas kernels, absorb(): pl.pallas_call(functools.partial(absorb_kernel, j=j, fresh=held is None),...  7.73 us
    pallas_call x4, Pallas kernels, inner_grad(): pl.pallas_call(functools.partial(inner_grad_kernel, k=k), in_specs=[VM] *...  6.78 us
  transfers between devices with their start and end apart: 30, of which 13 were waited for; matrix products, arithmetic and copies ran while one was open for 1% of the time, Pallas kernels for 30%

profile of v1, /device:TPU:0, one launch (start us, length us, event | category | flops | bytes accessed | tf_op | source)
XLA Modules:
  0.0 140.5 jit_solution(15866703877008950942)
XLA Ops:
  0.6 3.0 %collective-permute-start = (bf16[512,256]{1,0:T(8,128)(2,1)}, bf16[512,256]{1,0:T(8,128)(2,1)S(1)}, u32[]{:S(2)}, u32[]{:S(2)}) collective-permute-start(bf16[512,256]{1,0:T(8,128)(2,1)} %refs_0_.1), channel_id=1, source_target_pairs={{0,2},{1,3},{2,0},{3,1},{4,6},{5,7},{6,4},{7,5},{8,10},{9,11},{10,... | collective-permute-start | bytes 786440 | tf_op jit(solution)/shard_map/ppermute | solution.py:519
  5.2 5.0 %collective-permute-done.refs_1_ = bf16[512,256]{1,0:T(8,128)(2,1)S(1)} collective-permute-done((bf16[512,256]{1,0:T(8,128)(2,1)}, bf16[512,256]{1,0:T(8,128)(2,1)S(1)}, u32[]{:S(2)}, u32[]{:S(2)}) %collective-permute-start) | collective-permute-done | bytes 262176 | tf_op jit(solution)/shard_map/ppermute | solution.py:519
  10.2 1.8 %collective-permute-start.2 = (bf16[256,256]{1,0:T(8,128)(2,1)S(1)}, bf16[256,256]{1,0:T(8,128)(2,1)S(1)}, u32[]{:S(2)}, u32[]{:S(2)}) collective-permute-start(bf16[256,256]{1,0:T(8,128)(2,1)S(1)} %slice.8), channel_id=1, source_target_pairs={{0,4},{1,5},{2,6},{3,7},{4,0},{5,1},{6,2},{7,3},{8,12},{9,13},{10,... | collective-permute-start | bytes 393224 | tf_op jit(solution)/shard_map/ppermute | solution.py:519
  15.2 1.8 %collective-permute-done.3.refs_4_ = bf16[256,256]{1,0:T(8,128)(2,1)S(1)} collective-permute-done((bf16[256,256]{1,0:T(8,128)(2,1)S(1)}, bf16[256,256]{1,0:T(8,128)(2,1)S(1)}, u32[]{:S(2)}, u32[]{:S(2)}) %collective-permute-start.3) | collective-permute-done | bytes 131104 | tf_op jit(solution)/shard_map/ppermute | solution.py:519
  18.3 2.3 %copy-done.3 = bf16[1,512,4096]{2,1,0:T(8,128)(2,1)S(1)} copy-done((bf16[1,512,4096]{2,1,0:T(8,128)(2,1)S(1)}, bf16[1,512,4096]{2,1,0:T(8,128)(2,1)}, u32[]{:S(2)}) %copy-start.3) | copy-done | bytes 4194328
  20.7 2.7 %normalize.1 = (bf16[512,4096]{1,0:T(8,128)(2,1)S(1)}, f32[512,1]{1,0:T(8,128)S(1)}, f32[512,32]{1,0:T(8,128)S(1)}, f32[512,32]{1,0:T(8,128)S(1)}, f32[4,8,4096]{2,1,0:T(8,128)S(1)}) custom-call(s32[50]{0:T(128)S(1)} %pad_add_fusion.meta.ids, bf16[512,4096]{1,0:T(8,128)(2,1)S(1)} %bitcast.21, s32[512,32]{1,0:T(8,128)S(1)} %bitcast.22), custom_call_target="tpu_custom_call" | custom-call | flops 62914560 | bytes 8388608 | tf_op jit(solution)/shard_map/normalize/pallas_call | solution.py:81
  23.4 3.1 %scale_heads.1 = (bf16[512,4096]{1,0:T(8,128)(2,1)S(1)}, bf16[512,4096]{1,0:T(8,128)(2,1)S(1)}) custom-call(bf16[512,4096]{1,0:T(8,128)(2,1)S(1)} %get-tuple-element.75.x, bf16[512,4096]{1,0:T(8,128)(2,1)S(1)} %bitcast.10, f32[512,32]{1,0:T(8,128)S(1)} %get-tuple-element.76.a, f32[512,32]{1,0:T(8,128)S(1)} %get-tuple-element.77.b), custom_call_target="tpu_custom_call" | custom-call | flops 20971520 | bytes 16777216 | tf_op jit(solution)/shard_map/scale_heads/pallas_call | solution.py:121
  26.5 1.9 %project.1 = (bf16[512,256]{1,0:T(8,128)(2,1)S(1)}, bf16[4096,256]{1,0:T(8,128)(2,1)S(1)}) custom-call(s32[50]{0:T(128)S(1)} %pad_add_fusion.meta.ids, bf16[512,4096]{1,0:T(8,128)(2,1)S(1)} %get-tuple-element.75.x, bf16[512,256]{1,0:T(8,128)(2,1)S(1)} %copy-done.4, bf16[512,256]{1,0:T(8,128)(2,1)S(1)} %collective-permute-done.refs_1_, ...), custom_call_target="tpu_custom_call" | custom-call | flops 1073741824 | bytes 6291456 | tf_op jit(solution)/shard_map/project/pallas_call | solution.py:150
  30.6 4.5 %collective-permute-start.9 = (bf16[128,1024]{1,0:T(8,128)(2,1)S(1)}, bf16[128,1024]{1,0:T(8,128)(2,1)S(1)}, u32[]{:S(2)}, u32[]{:S(2)}) collective-permute-start(bf16[128,1024]{1,0:T(8,128)(2,1)S(1)} %get-tuple-element.86), channel_id=1, source_target_pairs={{0,8},{8,0},{16,24},{24,16},{1,9},{9,1},{17,25},{25,17},{2,10},{10... | collective-permute-start | bytes 786440 | tf_op jit(solution)/shard_map/ppermute | solution.py:323
  35.1 2.9 %shard_map.95 = (bf16[4,128,3072]{2,1,0:T(8,128)(2,1)S(1)}, bf16[4,128,3072]{2,1,0:T(8,128)(2,1)S(1)}, bf16[2,4,128,1024]{3,2,1,0:T(8,128)(2,1)S(1)}, f32[8,4096]{1,0:T(8,128)S(1)}) custom-call(s32[50]{0:T(128)S(1)} %pad_add_fusion.meta.ids, bf16[512,256]{1,0:T(8,128)(2,1)S(1)} %get-tuple-element.80.p, ...), custom_call_target="tpu_custom_call", output_to_operand_aliasing={{2}: (5, {}), {3}: (6, {})} | custom-call | flops 805306368 | bytes 12582912 | tf_op jit(solution)/shard_map/pallas_call | solution.py:213
  38.0 3.7 %collective-permute-done.9.ra = bf16[128,1024]{1,0:T(8,128)(2,1)S(1)} collective-permute-done((bf16[128,1024]{1,0:T(8,128)(2,1)S(1)}, bf16[128,1024]{1,0:T(8,128)(2,1)S(1)}, u32[]{:S(2)}, u32[]{:S(2)}) %collective-permute-start.9) | collective-permute-done | bytes 262176 | tf_op jit(solution)/shard_map/ppermute | solution.py:323
  42.5 1.8 %collective-permute-start.11 = (bf16[128,1024]{1,0:T(8,128)(2,1)S(1)}, bf16[128,1024]{1,0:T(8,128)(2,1)S(1)}, u32[]{:S(2)}, u32[]{:S(2)}) collective-permute-start(bf16[128,1024]{1,0:T(8,128)(2,1)S(1)} %get-tuple-element.90), channel_id=1, source_target_pairs={{0,8},{8,0},{16,24},{24,16},{1,9},{9,1},{17,25},{25,17},{2,10},{10... | collective-permute-start | bytes 786440 | tf_op jit(solution)/shard_map/ppermute | solution.py:323
  45.0 5.4 %collective-permute-done.11.ra = bf16[128,1024]{1,0:T(8,128)(2,1)S(1)} collective-permute-done((bf16[128,1024]{1,0:T(8,128)(2,1)S(1)}, bf16[128,1024]{1,0:T(8,128)(2,1)S(1)}, u32[]{:S(2)}, u32[]{:S(2)}) %collective-permute-start.11) | collective-permute-done | bytes 262176 | tf_op jit(solution)/shard_map/ppermute | solution.py:323
  51.1 3.7 %collective-permute-start.13 = (bf16[128,1024]{1,0:T(8,128)(2,1)S(1)}, bf16[128,1024]{1,0:T(8,128)(2,1)S(1)}, u32[]{:S(2)}, u32[]{:S(2)}) collective-permute-start(bf16[128,1024]{1,0:T(8,128)(2,1)S(1)} %get-tuple-element.92), channel_id=1, source_target_pairs={{0,8},{8,0},{16,24},{24,16},{1,9},{9,1},{17,25},{25,17},{2,10},{10... | collective-permute-start | bytes 786440 | tf_op jit(solution)/shard_map/ppermute | solution.py:323
  55.5 4.3 %collective-permute-done.13.ra = bf16[128,1024]{1,0:T(8,128)(2,1)S(1)} collective-permute-done((bf16[128,1024]{1,0:T(8,128)(2,1)S(1)}, bf16[128,1024]{1,0:T(8,128)(2,1)S(1)}, u32[]{:S(2)}, u32[]{:S(2)}) %collective-permute-start.13) | collective-permute-done | bytes 262176 | tf_op jit(solution)/shard_map/ppermute | solution.py:323
  60.5 3.7 %collective-permute-start.15 = (bf16[128,1024]{1,0:T(8,128)(2,1)S(1)}, bf16[128,1024]{1,0:T(8,128)(2,1)S(1)}, u32[]{:S(2)}, u32[]{:S(2)}) collective-permute-start(bf16[128,1024]{1,0:T(8,128)(2,1)S(1)} %get-tuple-element.94), channel_id=1, source_target_pairs={{0,8},{8,0},{16,24},{24,16},{1,9},{9,1},{17,25},{25,17},{2,10},{10... | collective-permute-start | bytes 786440 | tf_op jit(solution)/shard_map/ppermute | solution.py:323
  64.9 3.7 %collective-permute-done.15.ra = bf16[128,1024]{1,0:T(8,128)(2,1)S(1)} collective-permute-done((bf16[128,1024]{1,0:T(8,128)(2,1)S(1)}, bf16[128,1024]{1,0:T(8,128)(2,1)S(1)}, u32[]{:S(2)}, u32[]{:S(2)}) %collective-permute-start.15) | collective-permute-done | bytes 262176 | tf_op jit(solution)/shard_map/ppermute | solution.py:323
  69.2 4.0 %collective-permute-start.17 = (bf16[128,1024]{1,0:T(8,128)(2,1)S(1)}, bf16[128,1024]{1,0:T(8,128)(2,1)S(1)}, u32[]{:S(2)}, u32[]{:S(2)}) collective-permute-start(bf16[128,1024]{1,0:T(8,128)(2,1)S(1)} %get-tuple-element.96), channel_id=1, source_target_pairs={{0,8},{8,0},{16,24},{24,16},{1,9},{9,1},{17,25},{25,17},{2,10},{10... | collective-permute-start | bytes 786440 | tf_op jit(solution)/shard_map/ppermute | solution.py:323
  74.1 1.7 %shard_map.114.refs_4_ = f32[128,256]{1,0:T(8,128)S(1)} custom-call(bf16[512,256]{1,0:T(8,128)(2,1)S(1)} %get-tuple-element.80.p, bf16[512,4096]{1,0:T(8,128)(2,1)S(1)} %get-tuple-element.78.v, bf16[512,4096]{1,0:T(8,128)(2,1)S(1)} %get-tuple-element.79.g, bf16[4,128,1024]{2,1,0:T(8,128)(2,1)S(1)} %get-tuple-element.117.sl.sa, ...), custom_call_target="tpu_custom_call" | custom-call | flops 402653184 | bytes 4194304 | tf_op jit(solution)/shard_map/pallas_call | solution.py:348
  75.8 1.7 %shard_map.113.refs_3_ = f32[128,256]{1,0:T(8,128)S(1)} custom-call(bf16[512,256]{1,0:T(8,128)(2,1)S(1)} %get-tuple-element.80.p, bf16[512,4096]{1,0:T(8,128)(2,1)S(1)} %get-tuple-element.78.v, bf16[512,4096]{1,0:T(8,128)(2,1)S(1)} %get-tuple-element.79.g, bf16[4,128,1024]{2,1,0:T(8,128)(2,1)S(1)} %get-tuple-element.117.sl.sa, ...), custom_call_target="tpu_custom_call" | custom-call | flops 402653184 | bytes 4194304 | tf_op jit(solution)/shard_map/pallas_call | solution.py:348
  81.6 1.8 %collective-permute-start.19 = (bf16[128,1024]{1,0:T(8,128)(2,1)S(1)}, bf16[128,1024]{1,0:T(8,128)(2,1)S(1)}, u32[]{:S(2)}, u32[]{:S(2)}) collective-permute-start(bf16[128,1024]{1,0:T(8,128)(2,1)S(1)} %get-tuple-element.98), channel_id=1, source_target_pairs={{0,8},{8,0},{16,24},{24,16},{1,9},{9,1},{17,25},{25,17},{2,10},{10... | collective-permute-start | bytes 786440 | tf_op jit(solution)/shard_map/ppermute | solution.py:323
  88.8 3.0 %shard_map.107 = (bf16[512,4096]{1,0:T(8,128)(2,1)}, bf16[512,1024]{1,0:T(8,128)(2,1)S(1)}) custom-call(bf16[512,4096]{1,0:T(8,128)(2,1)S(1)} %get-tuple-element.75.x, bf16[512,4096]{1,0:T(8,128)(2,1)S(1)} %get-tuple-element.78.v, bf16[512,4096]{1,0:T(8,128)(2,1)S(1)} %get-tuple-element.79.g, bf16[512,4096]{1,0:T(8,128)(2,1)S(1)} %bitcast.11, ...), custom_call_target="tpu_custom_call" | custom-call | flops 536870912 | bytes 9437184 | tf_op jit(solution)/shard_map/pallas_call | solution.py:455
  93.0 3.0 %shard_map.108 = (bf16[512,4096]{1,0:T(8,128)(2,1)}, bf16[512,1024]{1,0:T(8,128)(2,1)S(1)}) custom-call(bf16[512,4096]{1,0:T(8,128)(2,1)S(1)} %get-tuple-element.75.x, bf16[512,4096]{1,0:T(8,128)(2,1)S(1)} %get-tuple-element.78.v, bf16[512,4096]{1,0:T(8,128)(2,1)S(1)} %get-tuple-element.79.g, ...), custom_call_target="tpu_custom_call", output_to_operand_aliasing={{0}: (14, {})} | custom-call | flops 536870912 | bytes 9437184 | tf_op jit(solution)/shard_map/pallas_call | solution.py:455
  97.2 3.0 %shard_map.109 = (bf16[512,4096]{1,0:T(8,128)(2,1)}, bf16[512,1024]{1,0:T(8,128)(2,1)S(1)}) custom-call(bf16[512,4096]{1,0:T(8,128)(2,1)S(1)} %get-tuple-element.75.x, bf16[512,4096]{1,0:T(8,128)(2,1)S(1)} %get-tuple-element.78.v, bf16[512,4096]{1,0:T(8,128)(2,1)S(1)} %get-tuple-element.79.g, ...), custom_call_target="tpu_custom_call", output_to_operand_aliasing={{0}: (14, {})} | custom-call | flops 536870912 | bytes 9437184 | tf_op jit(solution)/shard_map/pallas_call | solution.py:455
  101.6 1.8 %shard_map.115 = (bf16[2,4,128,256]{3,2,1,0:T(8,128)(2,1)S(1)}, bf16[2,4,128,256]{3,2,1,0:T(8,128)(2,1)S(1)}, bf16[512,256]{1,0:T(8,128)(2,1)S(1)}) custom-call(s32[50]{0:T(128)S(1)} %pad_add_fusion.meta.ids, bf16[512,4096]{1,0:T(8,128)(2,1)S(1)} %get-tuple-element.75.x, f32[512,256]{1,0:T(8,128)S(1)} %get-tuple-element.123.refs_0_, ...), custom_call_target="tpu_custom_call" | custom-call | flops 536870912 | bytes 2097152 | tf_op jit(solution)/shard_map/pallas_call | solution.py:385
  103.4 1.8 %shard_map.118 = (bf16[2,4,128,256]{3,2,1,0:T(8,128)(2,1)S(1)}, bf16[2,4,128,256]{3,2,1,0:T(8,128)(2,1)S(1)}) custom-call(s32[50]{0:T(128)S(1)} %pad_add_fusion.meta.ids, bf16[512,4096]{1,0:T(8,128)(2,1)S(1)} %get-tuple-element.75.x, bf16[512,256]{1,0:T(8,128)(2,1)S(1)} %get-tuple-element.124.low.refs_0_), custom_call_target="tpu_custom_call" | custom-call | flops 536870912 | bytes 2097152 | tf_op jit(solution)/shard_map/pallas_call | solution.py:385
  111.2 6.4 %collective-permute-done.23.refs_1_ = bf16[4,2,128,128]{3,2,1,0:T(8,128)(2,1)S(1)} collective-permute-done((bf16[4,2,128,128]{3,2,1,0:T(8,128)(2,1)S(1)}, bf16[4,2,128,128]{3,2,1,0:T(8,128)(2,1)S(1)}, u32[]{:S(2)}, u32[]{:S(2)}) %collective-permute-start.23) | collective-permute-done | bytes 262176 | tf_op jit(solution)/shard_map/ppermute | solution.py:519
  121.3 3.0 %shard_map.110 = (bf16[512,4096]{1,0:T(8,128)(2,1)}, bf16[512,1024]{1,0:T(8,128)(2,1)S(1)}) custom-call(bf16[512,4096]{1,0:T(8,128)(2,1)S(1)} %get-tuple-element.75.x, bf16[512,4096]{1,0:T(8,128)(2,1)S(1)} %get-tuple-element.78.v, bf16[512,4096]{1,0:T(8,128)(2,1)S(1)} %get-tuple-element.79.g, ...), custom_call_target="tpu_custom_call", output_to_operand_aliasing={{0}: (14, {})} | custom-call | flops 536870912 | bytes 9437184 | tf_op jit(solution)/shard_map/pallas_call | solution.py:455
  125.8 3.3 %collective-permute-start.27 = (bf16[128,256]{1,0:T(8,128)(2,1)S(1)}, bf16[128,256]{1,0:T(8,128)(2,1)S(1)}, u32[]{:S(2)}, u32[]{:S(2)}) collective-permute-start(bf16[128,256]{1,0:T(8,128)(2,1)S(1)} %get-tuple-element.144), channel_id=1, source_target_pairs={{0,8},{8,0},{16,24},{24,16},{1,9},{9,1},{17,25},{25,17},{2,10},{10... | collective-permute-start | bytes 196616 | tf_op jit(solution)/shard_map/ppermute | solution.py:629
  129.4 2.2 %collective-permute-start.29 = (bf16[128,256]{1,0:T(8,128)(2,1)S(1)}, bf16[128,256]{1,0:T(8,128)(2,1)S(1)}, u32[]{:S(2)}, u32[]{:S(2)}) collective-permute-start(bf16[128,256]{1,0:T(8,128)(2,1)S(1)} %get-tuple-element.146), channel_id=1, source_target_pairs={{0,24},{8,16},{16,8},{24,0},{1,25},{9,17},{17,9},{25,1},{2,26},{10... | collective-permute-start | bytes 196616 | tf_op jit(solution)/shard_map/ppermute | solution.py:629
  131.6 4.1 %shard_map.116.refs_4_ = bf16[512,4096]{1,0:T(8,128)(2,1)} custom-call(bf16[512,4096]{1,0:T(8,128)(2,1)S(1)} %get-tuple-element.75.x, bf16[512,4096]{1,0:T(8,128)(2,1)S(1)} %bitcast.19, bf16[512,256]{1,0:T(8,128)(2,1)S(1)} %get-tuple-element.124.low.refs_0_, f32[512,1]{1,0:T(8,128)S(1)} %get-tuple-element.125.rstd, ...), custom_call_target="tpu_custom_call" | custom-call | flops 536870912 | bytes 8388608 | tf_op jit(solution)/shard_map/pallas_call | solution.py:504
  135.7 4.1 %shard_map.117 = bf16[512,4096]{1,0:T(8,128)(2,1)} custom-call(bf16[512,4096]{1,0:T(8,128)(2,1)S(1)} %get-tuple-element.75.x, bf16[512,4096]{1,0:T(8,128)(2,1)S(1)} %bitcast.20, bf16[512,256]{1,0:T(8,128)(2,1)S(1)} %get-tuple-element.124.low.refs_0_, f32[512,1]{1,0:T(8,128)S(1)} %get-tuple-element.125.rstd, ...), custom_call_target="tpu_custom_call", output_to_operand_aliasing={{}: (9, {})} | custom-call | flops 536870912 | bytes 8388608 | tf_op jit(solution)/shard_map/pallas_call | solution.py:504
  (84 shorter events, 39.0 us)
Async XLA Ops:
  0.6 9.6 %collective-permute-start = (bf16[512,256]{1,0:T(8,128)(2,1)}, bf16[512,256]{1,0:T(8,128)(2,1)S(1)}, u32[]{:S(2)}, u32[]{:S(2)}) collective-permute-start(bf16[512,256]{1,0:T(8,128)(2,1)} %refs_0_.1), channel_id=1, source_target_pairs={{0,2},{1,3},{2,0},{3,1},{4,6},{5,7},{6,4},{7,5},{8,10},{9,11},{10,... | collective-permute-start | bytes 786440 | tf_op jit(solution)/shard_map/ppermute | solution.py:519
  3.7 8.4 %collective-permute-start.1 = (bf16[512,256]{1,0:T(8,128)(2,1)}, bf16[512,256]{1,0:T(8,128)(2,1)S(1)}, u32[]{:S(2)}, u32[]{:S(2)}) collective-permute-start(bf16[512,256]{1,0:T(8,128)(2,1)} %refs_0_.1), channel_id=1, source_target_pairs={{0,4},{1,5},{2,6},{3,7},{4,0},{5,1},{6,2},{7,3},{8,12},{9,13},{10,... | collective-permute-start | bytes 786440 | tf_op jit(solution)/shard_map/ppermute | solution.py:519
  5.2 21.3 %collective-permute-start.4 = (bf16[512,256]{1,0:T(8,128)(2,1)}, bf16[512,256]{1,0:T(8,128)(2,1)S(1)}, u32[]{:S(2)}, u32[]{:S(2)}) collective-permute-start(bf16[512,256]{1,0:T(8,128)(2,1)} %refs_0_.1), channel_id=1, source_target_pairs={{0,1},{1,0},{2,3},{3,2},{4,5},{5,4},{6,7},{7,6},{8,9},{9,8},{10,11... | collective-permute-start | bytes 786440 | tf_op jit(solution)/shard_map/ppermute | solution.py:519
  10.2 5.0 %collective-permute-start.2 = (bf16[256,256]{1,0:T(8,128)(2,1)S(1)}, bf16[256,256]{1,0:T(8,128)(2,1)S(1)}, u32[]{:S(2)}, u32[]{:S(2)}) collective-permute-start(bf16[256,256]{1,0:T(8,128)(2,1)S(1)} %slice.8), channel_id=1, source_target_pairs={{0,4},{1,5},{2,6},{3,7},{4,0},{5,1},{6,2},{7,3},{8,12},{9,13},{10,... | collective-permute-start | bytes 393224 | tf_op jit(solution)/shard_map/ppermute | solution.py:519
  12.0 5.0 %collective-permute-start.3 = (bf16[256,256]{1,0:T(8,128)(2,1)S(1)}, bf16[256,256]{1,0:T(8,128)(2,1)S(1)}, u32[]{:S(2)}, u32[]{:S(2)}) collective-permute-start(bf16[256,256]{1,0:T(8,128)(2,1)S(1)} %slice.9), channel_id=1, source_target_pairs={{0,2},{1,3},{2,0},{3,1},{4,6},{5,7},{6,4},{7,5},{8,10},{9,11},{10,... | collective-permute-start | bytes 393224 | tf_op jit(solution)/shard_map/ppermute | solution.py:519
  13.6 12.9 %collective-permute-start.5 = (bf16[512,256]{1,0:T(8,128)(2,1)S(1)}, bf16[512,256]{1,0:T(8,128)(2,1)S(1)}, u32[]{:S(2)}, u32[]{:S(2)}) collective-permute-start(bf16[512,256]{1,0:T(8,128)(2,1)S(1)} %collective-permute-done.refs_1_), channel_id=1, source_target_pairs={{0,1},{1,0},{2,3},{3,2},{4,5},{5,4},{6,7},{7,6},{8,9},{9,8},{10,11... | collective-permute-start | bytes 786440 | tf_op jit(solution)/shard_map/ppermute | solution.py:519
  13.6 12.9 %collective-permute-start.6 = (bf16[512,256]{1,0:T(8,128)(2,1)S(1)}, bf16[512,256]{1,0:T(8,128)(2,1)S(1)}, u32[]{:S(2)}, u32[]{:S(2)}) collective-permute-start(bf16[512,256]{1,0:T(8,128)(2,1)S(1)} %collective-permute-done.1.refs_2_), channel_id=1, source_target_pairs={{0,1},{1,0},{2,3},{3,2},{4,5},{5,4},{6,7},{7,6},{8,9},{9,8},{10,11... | collective-permute-start | bytes 786440 | tf_op jit(solution)/shard_map/ppermute | solution.py:519
  15.2 11.3 %collective-permute-start.7 = (bf16[256,256]{1,0:T(8,128)(2,1)S(1)}, bf16[256,256]{1,0:T(8,128)(2,1)S(1)}, u32[]{:S(2)}, u32[]{:S(2)}) collective-permute-start(bf16[256,256]{1,0:T(8,128)(2,1)S(1)} %collective-permute-done.2.refs_3_), channel_id=1, source_target_pairs={{0,1},{1,0},{2,3},{3,2},{4,5},{5,4},{6,7},{7,6},{8,9},{9,8},{10,11... | collective-permute-start | bytes 393224 | tf_op jit(solution)/shard_map/ppermute | solution.py:519
  17.1 9.4 %collective-permute-start.8 = (bf16[256,256]{1,0:T(8,128)(2,1)S(1)}, bf16[256,256]{1,0:T(8,128)(2,1)S(1)}, u32[]{:S(2)}, u32[]{:S(2)}) collective-permute-start(bf16[256,256]{1,0:T(8,128)(2,1)S(1)} %collective-permute-done.3.refs_4_), channel_id=1, source_target_pairs={{0,1},{1,0},{2,3},{3,2},{4,5},{5,4},{6,7},{7,6},{8,9},{9,8},{10,11... | collective-permute-start | bytes 393224 | tf_op jit(solution)/shard_map/ppermute | solution.py:519
  18.2 5.1 %copy-start = (bf16[1,512,4096]{2,1,0:T(8,128)(2,1)S(1)}, bf16[1,512,4096]{2,1,0:T(8,128)(2,1)}, u32[]{:S(2)}) copy-start(bf16[1,512,4096]{2,1,0:T(8,128)(2,1)} %param.10) | copy-start | bytes 12582916
  30.0 8.1 %collective-permute-start.10 = (bf16[128,1024]{1,0:T(8,128)(2,1)S(1)}, bf16[128,1024]{1,0:T(8,128)(2,1)S(1)}, u32[]{:S(2)}, u32[]{:S(2)}) collective-permute-start(bf16[128,1024]{1,0:T(8,128)(2,1)S(1)} %get-tuple-element.87), channel_id=1, source_target_pairs={{8,16},{16,8},{9,17},{17,9},{10,18},{18,10},{11,19},{19,11},{12,20... | collective-permute-start | bytes 786440 | tf_op jit(solution)/shard_map/ppermute | solution.py:324
  30.6 11.1 %collective-permute-start.9 = (bf16[128,1024]{1,0:T(8,128)(2,1)S(1)}, bf16[128,1024]{1,0:T(8,128)(2,1)S(1)}, u32[]{:S(2)}, u32[]{:S(2)}) collective-permute-start(bf16[128,1024]{1,0:T(8,128)(2,1)S(1)} %get-tuple-element.86), channel_id=1, source_target_pairs={{0,8},{8,0},{16,24},{24,16},{1,9},{9,1},{17,25},{25,17},{2,10},{10... | collective-permute-start | bytes 786440 | tf_op jit(solution)/shard_map/ppermute | solution.py:323
  42.5 7.9 %collective-permute-start.11 = (bf16[128,1024]{1,0:T(8,128)(2,1)S(1)}, bf16[128,1024]{1,0:T(8,128)(2,1)S(1)}, u32[]{:S(2)}, u32[]{:S(2)}) collective-permute-start(bf16[128,1024]{1,0:T(8,128)(2,1)S(1)} %get-tuple-element.90), channel_id=1, source_target_pairs={{0,8},{8,0},{16,24},{24,16},{1,9},{9,1},{17,25},{25,17},{2,10},{10... | collective-permute-start | bytes 786440 | tf_op jit(solution)/shard_map/ppermute | solution.py:323
  44.3 6.1 %collective-permute-start.12 = (bf16[128,1024]{1,0:T(8,128)(2,1)S(1)}, bf16[128,1024]{1,0:T(8,128)(2,1)S(1)}, u32[]{:S(2)}, u32[]{:S(2)}) collective-permute-start(bf16[128,1024]{1,0:T(8,128)(2,1)S(1)} %get-tuple-element.91), channel_id=1, source_target_pairs={{8,16},{16,8},{9,17},{17,9},{10,18},{18,10},{11,19},{19,11},{12,20... | collective-permute-start | bytes 786440 | tf_op jit(solution)/shard_map/ppermute | solution.py:324
  51.1 8.7 %collective-permute-start.13 = (bf16[128,1024]{1,0:T(8,128)(2,1)S(1)}, bf16[128,1024]{1,0:T(8,128)(2,1)S(1)}, u32[]{:S(2)}, u32[]{:S(2)}) collective-permute-start(bf16[128,1024]{1,0:T(8,128)(2,1)S(1)} %get-tuple-element.92), channel_id=1, source_target_pairs={{0,8},{8,0},{16,24},{24,16},{1,9},{9,1},{17,25},{25,17},{2,10},{10... | collective-permute-start | bytes 786440 | tf_op jit(solution)/shard_map/ppermute | solution.py:323
  54.8 5.0 %collective-permute-start.14 = (bf16[128,1024]{1,0:T(8,128)(2,1)S(1)}, bf16[128,1024]{1,0:T(8,128)(2,1)S(1)}, u32[]{:S(2)}, u32[]{:S(2)}) collective-permute-start(bf16[128,1024]{1,0:T(8,128)(2,1)S(1)} %get-tuple-element.93), channel_id=1, source_target_pairs={{8,16},{16,8},{9,17},{17,9},{10,18},{18,10},{11,19},{19,11},{12,20... | collective-permute-start | bytes 786440 | tf_op jit(solution)/shard_map/ppermute | solution.py:324
  60.5 8.1 %collective-permute-start.15 = (bf16[128,1024]{1,0:T(8,128)(2,1)S(1)}, bf16[128,1024]{1,0:T(8,128)(2,1)S(1)}, u32[]{:S(2)}, u32[]{:S(2)}) collective-permute-start(bf16[128,1024]{1,0:T(8,128)(2,1)S(1)} %get-tuple-element.94), channel_id=1, source_target_pairs={{0,8},{8,0},{16,24},{24,16},{1,9},{9,1},{17,25},{25,17},{2,10},{10... | collective-permute-start | bytes 786440 | tf_op jit(solution)/shard_map/ppermute | solution.py:323
  64.2 4.4 %collective-permute-start.16 = (bf16[128,1024]{1,0:T(8,128)(2,1)S(1)}, bf16[128,1024]{1,0:T(8,128)(2,1)S(1)}, u32[]{:S(2)}, u32[]{:S(2)}) collective-permute-start(bf16[128,1024]{1,0:T(8,128)(2,1)S(1)} %get-tuple-element.95), channel_id=1, source_target_pairs={{8,16},{16,8},{9,17},{17,9},{10,18},{18,10},{11,19},{19,11},{12,20... | collective-permute-start | bytes 786440 | tf_op jit(solution)/shard_map/ppermute | solution.py:324
  69.2 11.7 %collective-permute-start.17 = (bf16[128,1024]{1,0:T(8,128)(2,1)S(1)}, bf16[128,1024]{1,0:T(8,128)(2,1)S(1)}, u32[]{:S(2)}, u32[]{:S(2)}) collective-permute-start(bf16[128,1024]{1,0:T(8,128)(2,1)S(1)} %get-tuple-element.96), channel_id=1, source_target_pairs={{0,8},{8,0},{16,24},{24,16},{1,9},{9,1},{17,25},{25,17},{2,10},{10... | collective-permute-start | bytes 786440 | tf_op jit(solution)/shard_map/ppermute | solution.py:323
  73.2 7.7 %collective-permute-start.18 = (bf16[128,1024]{1,0:T(8,128)(2,1)S(1)}, bf16[128,1024]{1,0:T(8,128)(2,1)S(1)}, u32[]{:S(2)}, u32[]{:S(2)}) collective-permute-start(bf16[128,1024]{1,0:T(8,128)(2,1)S(1)} %get-tuple-element.97), channel_id=1, source_target_pairs={{8,16},{16,8},{9,17},{17,9},{10,18},{18,10},{11,19},{19,11},{12,20... | collective-permute-start | bytes 786440 | tf_op jit(solution)/shard_map/ppermute | solution.py:324
  81.6 18.6 %collective-permute-start.19 = (bf16[128,1024]{1,0:T(8,128)(2,1)S(1)}, bf16[128,1024]{1,0:T(8,128)(2,1)S(1)}, u32[]{:S(2)}, u32[]{:S(2)}) collective-permute-start(bf16[128,1024]{1,0:T(8,128)(2,1)S(1)} %get-tuple-element.98), channel_id=1, source_target_pairs={{0,8},{8,0},{16,24},{24,16},{1,9},{9,1},{17,25},{25,17},{2,10},{10... | collective-permute-start | bytes 786440 | tf_op jit(solution)/shard_map/ppermute | solution.py:323
  83.4 16.8 %collective-permute-start.20 = (bf16[128,1024]{1,0:T(8,128)(2,1)S(1)}, bf16[128,1024]{1,0:T(8,128)(2,1)S(1)}, u32[]{:S(2)}, u32[]{:S(2)}) collective-permute-start(bf16[128,1024]{1,0:T(8,128)(2,1)S(1)} %get-tuple-element.99), channel_id=1, source_target_pairs={{8,16},{16,8},{9,17},{17,9},{10,18},{18,10},{11,19},{19,11},{12,20... | collective-permute-start | bytes 786440 | tf_op jit(solution)/shard_map/ppermute | solution.py:324
  105.3 2.0 %collective-permute-start.22 = (bf16[2,4,128,256]{3,2,1,0:T(8,128)(2,1)S(1)}, bf16[2,4,128,256]{3,2,1,0:T(8,128)(2,1)S(1)}, u32[]{:S(2)}, u32[]{:S(2)}) collective-permute-start(bf16[2,4,128,256]{3,2,1,0:T(8,128)(2,1)S(1)} %get-tuple-element.134), channel_id=1, source_target_pairs={{0,1},{1,0},{2,3},{3,2},{4,5},{5,4},{6,7},{7,6},{8,9},{9,8},{10,11... | collective-permute-start | bytes 1572872 | tf_op jit(solution)/shard_map/ppermute | solution.py:519
  105.3 2.6 %collective-permute-start.21 = (bf16[2,4,128,256]{3,2,1,0:T(8,128)(2,1)S(1)}, bf16[2,4,128,256]{3,2,1,0:T(8,128)(2,1)S(1)}, u32[]{:S(2)}, u32[]{:S(2)}) collective-permute-start(bf16[2,4,128,256]{3,2,1,0:T(8,128)(2,1)S(1)} %get-tuple-element.132), channel_id=1, source_target_pairs={{0,1},{1,0},{2,3},{3,2},{4,5},{5,4},{6,7},{7,6},{8,9},{9,8},{10,11... | collective-permute-start | bytes 1572872 | tf_op jit(solution)/shard_map/ppermute | solution.py:519
  109.2 8.4 %collective-permute-start.23 = (bf16[4,2,128,128]{3,2,1,0:T(8,128)(2,1)S(1)}, bf16[4,2,128,128]{3,2,1,0:T(8,128)(2,1)S(1)}, u32[]{:S(2)}, u32[]{:S(2)}) collective-permute-start(bf16[4,2,128,128]{3,2,1,0:T(8,128)(2,1)S(1)} %get-tuple-element.136), channel_id=1, source_target_pairs={{0,2},{1,3},{2,0},{3,1},{4,6},{5,7},{6,4},{7,5},{8,10},{9,11},{10,... | collective-permute-start | bytes 786440 | tf_op jit(solution)/shard_map/ppermute | solution.py:519
  110.7 8.1 %collective-permute-start.24 = (bf16[4,2,128,128]{3,2,1,0:T(8,128)(2,1)S(1)}, bf16[4,2,128,128]{3,2,1,0:T(8,128)(2,1)S(1)}, u32[]{:S(2)}, u32[]{:S(2)}) collective-permute-start(bf16[4,2,128,128]{3,2,1,0:T(8,128)(2,1)S(1)} %get-tuple-element.138), channel_id=1, source_target_pairs={{0,4},{1,5},{2,6},{3,7},{4,0},{5,1},{6,2},{7,3},{8,12},{9,13},{10,... | collective-permute-start | bytes 786440 | tf_op jit(solution)/shard_map/ppermute | solution.py:519
  119.6 5.0 %collective-permute-start.25 = (bf16[4,1,128,128]{3,2,1,0:T(8,128)(2,1)S(1)}, bf16[4,1,128,128]{3,2,1,0:T(8,128)(2,1)S(1)}, u32[]{:S(2)}, u32[]{:S(2)}) collective-permute-start(bf16[4,1,128,128]{3,2,1,0:T(8,128)(2,1)S(1)} %get-tuple-element.140), channel_id=1, source_target_pairs={{0,4},{1,5},{2,6},{3,7},{4,0},{5,1},{6,2},{7,3},{8,12},{9,13},{10,... | collective-permute-start | bytes 393224 | tf_op jit(solution)/shard_map/ppermute | solution.py:519
  120.2 5.0 %collective-permute-start.26 = (bf16[4,1,128,128]{3,2,1,0:T(8,128)(2,1)S(1)}, bf16[4,1,128,128]{3,2,1,0:T(8,128)(2,1)S(1)}, u32[]{:S(2)}, u32[]{:S(2)}) collective-permute-start(bf16[4,1,128,128]{3,2,1,0:T(8,128)(2,1)S(1)} %get-tuple-element.142), channel_id=1, source_target_pairs={{0,2},{1,3},{2,0},{3,1},{4,6},{5,7},{6,4},{7,5},{8,10},{9,11},{10,... | collective-permute-start | bytes 393224 | tf_op jit(solution)/shard_map/ppermute | solution.py:519
  121.3 10.2 %copy-start.2 = (bf16[1,512,4096]{2,1,0:T(8,128)(2,1)S(1)}, bf16[1,512,4096]{2,1,0:T(8,128)(2,1)}, u32[]{:S(2)}) copy-start(bf16[1,512,4096]{2,1,0:T(8,128)(2,1)} %param.9) | copy-start | bytes 12582916
  125.8 14.0 %collective-permute-start.27 = (bf16[128,256]{1,0:T(8,128)(2,1)S(1)}, bf16[128,256]{1,0:T(8,128)(2,1)S(1)}, u32[]{:S(2)}, u32[]{:S(2)}) collective-permute-start(bf16[128,256]{1,0:T(8,128)(2,1)S(1)} %get-tuple-element.144), channel_id=1, source_target_pairs={{0,8},{8,0},{16,24},{24,16},{1,9},{9,1},{17,25},{25,17},{2,10},{10... | collective-permute-start | bytes 196616 | tf_op jit(solution)/shard_map/ppermute | solution.py:629
  129.1 10.7 %collective-permute-start.28 = (bf16[128,256]{1,0:T(8,128)(2,1)S(1)}, bf16[128,256]{1,0:T(8,128)(2,1)S(1)}, u32[]{:S(2)}, u32[]{:S(2)}) collective-permute-start(bf16[128,256]{1,0:T(8,128)(2,1)S(1)} %get-tuple-element.145), channel_id=1, source_target_pairs={{0,16},{8,24},{16,0},{24,8},{1,17},{9,25},{17,1},{25,9},{2,18},{10... | collective-permute-start | bytes 196616 | tf_op jit(solution)/shard_map/ppermute | solution.py:629
  129.4 10.4 %collective-permute-start.29 = (bf16[128,256]{1,0:T(8,128)(2,1)S(1)}, bf16[128,256]{1,0:T(8,128)(2,1)S(1)}, u32[]{:S(2)}, u32[]{:S(2)}) collective-permute-start(bf16[128,256]{1,0:T(8,128)(2,1)S(1)} %get-tuple-element.146), channel_id=1, source_target_pairs={{0,24},{8,16},{16,8},{24,0},{1,25},{9,17},{17,9},{25,1},{2,26},{10... | collective-permute-start | bytes 196616 | tf_op jit(solution)/shard_map/ppermute | solution.py:629
  (4 other events, 9.3 us)

commit v2 on v1

--- a/solution.py
+++ b/solution.py
@@ -221,6 +221,32 @@
     )(*args)
 
 
+def turn_kernel(meta, x, away, kept_o, held, *, rows):
+    g = held.shape[0]
+    mine = lax.rem(meta[0], 2)
+    for i in range(x.shape[1] // g):
+        held[...] = x[:, i * g : (i + 1) * g].T
+        for b in range(g // (2 * rows)):
+            at = i * g // (2 * rows) + b
+            kept_o[at * rows : (at + 1) * rows, :] = held[span(2 * b + mine, rows), :]
+            away[at * rows : (at + 1) * rows, :] = held[span(2 * b + 1 - mine, rows), :]
+
+
+def turn(meta, x):
+    t, d = x.shape
+    rows = d // (lax.axis_size("seq") * lax.axis_size("fsdp"))
+    return pl.pallas_call(
+        functools.partial(turn_kernel, rows=rows),
+        in_specs=[SM, VM],
+        out_specs=[VM, VM],
+        out_shape=[shape((d // 2, t), bf16), kept((d // 2, t), bf16)],
+        scratch_shapes=[pltpu.VMEM((4 * CHUNK, t), bf16)],
+        compiler_params=params(6),
+        cost_estimate=cost(0, 4 * t * d),
+        name="turn",
+    )(meta, near(x))
+
+
 def hop_kernel(ids, ra, rb, loc, dtot, oa, ob, *, j):
     w = ra.shape[1]
     base = 2 + 8 * j
@@ -355,42 +381,78 @@
     )(*map(near, (p, v, g, sa, da, sb, db)))
 
 
-def weight_grad_kernel(meta, x, *refs, first):
-    if first:
-        acc, inner, (away, kept_o, low, term) = refs[0], refs[1:-4], refs[-4:]
-        for k, part in enumerate(inner):
-            rows = slice(k * CHUNK, (k + 1) * CHUNK)
-            low[rows, :] = (acc[rows, :] + part[...]).astype(bf16)
-    else:
-        low, away, kept_o, term = refs
-    number, half, rows, _ = away.shape
-    w = term.shape[0]
-    mine = lax.rem(meta[0], 2)
-    for j in range(number):
-        at = j if first else j + number
-        term[...] = dot(x[:, at * w : (at + 1) * w], low[...], 0, 0)
-        for i in range(half):
-            kept_o[j, i] = term[span(2 * i + mine, rows), :].astype(bf16)
-            away[j, i] = term[span(2 * i + 1 - mine, rows), :].astype(bf16)
-
-
-def weight_grad(meta, x, sources, first):
-    t, d = x.shape
-    n2 = sources[0].shape[1]
+def lower_kernel(acc, *refs):
+    inner, low = refs[:-1], refs[-1]
+    for k, part in enumerate(inner):
+        rows = slice(k * CHUNK, (k + 1) * CHUNK)
+        low[rows, :] = (acc[rows, :] + part[...]).astype(bf16)
+
+
+def lower(acc, inner):
+    return pl.pallas_call(
+        lower_kernel,
+        in_specs=[VM] * (1 + len(inner)),
+        out_specs=VM,
+        out_shape=kept(acc.shape, bf16),
+        compiler_params=params(4),
+        cost_estimate=cost(0, 10 * acc.size),
+        name="lower",
+    )(near(acc), *map(near, inner))
+
+
+def own_term_kernel(x, low, out):
+    w = 4 * CHUNK
+    for i in range(x.shape[0] // w):
+        rows = slice(i * w, (i + 1) * w)
+        out[rows, :] = dot(x[rows, :], low[...], 1, 0)
+
+
+def own_term(x, low):
+    d, t = x.shape
+    n2 = low.shape[1]
+    return pl.pallas_call(
+        own_term_kernel,
+        in_specs=[VM, VM],
+        out_specs=VM,
+        out_shape=kept((d, n2), f32),
+        compiler_params=params(6),
+        cost_estimate=cost(2 * t * d * n2, 2 * t * d),
+        name="own_term",
+    )(near(x), near(low))
+
+
+def chip_term_kernel(meta, x, low, term, al, kl, ar, kr, total, *, left, right):
+    along, blocks, rows, n2 = total.shape
+    w = blocks * rows
+    for s in range(along):
+        own = slice(s * w, (s + 1) * w)
+        value = (term[own, :] + dot(x[own, :], low[...], 1, 0)).astype(bf16)
+        for i in range(blocks):
+            total[s, i] = value[i * rows : (i + 1) * rows, :]
+    n = n2 // 2
+    f = meta[0]
+    bit = lambda b: lax.rem(lax.div(f, b), 2)
+    halve(lambda m: total[:, m, :, :n], al, kl, bit(left[0]), sorted(left).index(left[0]))
+    halve(lambda m: total[:, m, :, n:], ar, kr, bit(right[0]), sorted(right).index(right[0]))
+
+
+def chip_term(meta, x, low, term, left, right):
+    d, t = x.shape
+    n2 = low.shape[1]
     along, count = lax.axis_size("seq"), lax.axis_size("fsdp")
-    w = d // along
-    number = along // 2
-    blocks = (number, count // 2, w // count, n2)
-    out_shape = [shape(blocks, bf16), kept(blocks, bf16)] + ([kept((t, n2), bf16)] if first else [])
-    return pl.pallas_call(
-        functools.partial(weight_grad_kernel, first=first),
-        in_specs=[SM, VM] + [VM] * len(sources),
-        out_specs=[VM] * len(out_shape),
-        out_shape=out_shape,
-        scratch_shapes=[pltpu.VMEM((w, n2), f32)],
+    blocks = count // 2
+    rows = d // (along * blocks)
+    out = (along, blocks // 2, rows, n2 // 2)
+    return pl.pallas_call(
+        functools.partial(chip_term_kernel, left=left, right=right),
+        in_specs=[SM] + [VM] * 3,
+        out_specs=[VM] * 4,
+        out_shape=[shape(out, bf16), kept(out, bf16)] * 2,
+        scratch_shapes=[pltpu.VMEM((along, blocks, rows, n2), bf16)],
         compiler_params=params(8),
-        cost_estimate=cost(2 * t * w * number * n2, 2 * t * w * number),
-    )(meta, near(x), *map(near, sources))
+        cost_estimate=cost(2 * t * d * n2, 2 * t * d),
+        name="chip_term",
+    )(meta, near(x), near(low), near(term))
 
 
 def piece_kernel(x, v, g, cot, newest, p, sl, dl, si, di, half, skip, a, b, *refs, piece, at, ps):
@@ -545,39 +607,24 @@
         away[:, i] = value(base + (1 - mine) * low)
 
 
-def fold_kernel(meta, *refs, first, left, right):
+def fold_kernel(meta, kl, gl, kr, gr, al_o, kl_o, ar_o, kr_o, tl, tr, *, left, right):
     f = meta[0]
     bit = lambda b: lax.rem(lax.div(f, b), 2)
-    pos = lambda b, order: sorted(order).index(b)
-    if first:
-        k0, g0, k1, g1, al, kl, ar, kr, total = refs
-        part = k0.shape[0]
-        total[:part] = (k0[...].astype(f32) + g0[...].astype(f32)).astype(bf16)
-        total[part:] = (k1[...].astype(f32) + g1[...].astype(f32)).astype(bf16)
-        n = al.shape[-1]
-        halve(lambda m: total[:, m, :, :n], al, kl, bit(left[0]), pos(left[0], left))
-        halve(lambda m: total[:, m, :, n:], ar, kr, bit(right[0]), pos(right[0], right))
-        return
-    kl, gl, kr, gr, al_o, kl_o, ar_o, kr_o, tl, tr = refs
     tl[...] = (kl[...].astype(f32) + gl[...].astype(f32)).astype(bf16)
     tr[...] = (kr[...].astype(f32) + gr[...].astype(f32)).astype(bf16)
-    halve(lambda m: tl[:, m], al_o, kl_o, bit(left[0]), pos(left[0], left))
-    halve(lambda m: tr[:, m], ar_o, kr_o, bit(right[0]), pos(right[0], right))
-
-
-def fold(meta, arrays, left, right, first):
+    halve(lambda m: tl[:, m], al_o, kl_o, bit(left[0]), sorted(left).index(left[0]))
+    halve(lambda m: tr[:, m], ar_o, kr_o, bit(right[0]), sorted(right).index(right[0]))
+
+
+def fold(meta, arrays, left, right):
     along, blocks, rows, n = arrays[0].shape
-    if first:
-        along, n = 2 * along, n // 2
     out = (along, blocks // 2, rows, n)
-    vmem = pl.BlockSpec(memory_space=pltpu.VMEM)
-    scratch = [pltpu.VMEM((along, blocks, rows, 2 * n), bf16)] if first else [pltpu.VMEM(arrays[0].shape, bf16)] * 2
-    return pl.pallas_call(
-        functools.partial(fold_kernel, first=first, left=left, right=right),
-        in_specs=[pl.BlockSpec(memory_space=pltpu.SMEM)] + [vmem] * len(arrays),
-        out_specs=[vmem] * 4,
+    return pl.pallas_call(
+        functools.partial(fold_kernel, left=left, right=right),
+        in_specs=[SM] + [VM] * 4,
+        out_specs=[VM] * 4,
         out_shape=[shape(out, bf16), kept(out, bf16)] * 2,
-        scratch_shapes=scratch,
+        scratch_shapes=[pltpu.VMEM(arrays[0].shape, bf16)] * 2,
         compiler_params=params(10),
         cost_estimate=cost(0, 8 * along * blocks * rows * n),
     )(meta, *arrays)
@@ -609,20 +656,19 @@
     )(meta, *arrays)
 
 
-def scatter_sum(meta, halves):
+def scatter_sum(meta, own, other, low):
     along = lax.axis_size("seq")
     count = lax.axis_size("fsdp")
     left = [1 << i for i in range(1, count.bit_length() - 1)]
     right = left[::-1]
-    arrays = []
-    for away, stays in halves:
-        arrays += [stays, flip(away, 1)]
-    al, kl, ar, kr = fold(meta, arrays, left, right, True)
+    low_other = flip(low, 1)
+    term = own_term(own, low)
+    al, kl, ar, kr = chip_term(meta, other, low_other, term, left, right)
     for _ in range(len(left)):
         gl, gr = flip(al, left[0]), flip(ar, right[0])
         left, right = left[1:], right[1:]
         if left:
-            al, kl, ar, kr = fold(meta, [kl, gl, kr, gr], left, right, False)
+            al, kl, ar, kr = fold(meta, [kl, gl, kr, gr], left, right)
     own, *sends = deal(meta, [kl, gl, kr, gr])
     total = own.astype(f32)
     for k, block in enumerate(sends, 1):
@@ -644,10 +690,11 @@
     p, weights = project(meta, x, keys, pieces, block)
     s0, d0, loc, dtot, sa, sb = states(meta, p, v, g, half, None)
     s1, d1, loc, dtot = states(meta, p, v, g, half, (loc, dtot))
+    away, own = turn(meta, x)
+    other = flip(away, 1)
     inner = [inner_grad(p, v, g, s0, d0, s1, d1, k) for k in range(count)]
     acc, heads_done = pass_states(meta, sa, sb, loc, dtot, v, g, half)
-    *half0, low = weight_grad(meta, x, [acc, *inner], True)
-    half1 = weight_grad(meta, x, [low], False)
+    low = lower(acc, inner)
     skip = jnp.repeat(skip_gain, d // heads)[None]
     rebuilt, backs = None, []
     for i in range(PIECES):
@@ -656,10 +703,12 @@
             x, v, g, cot, newest, p, s1 if i else s0, d1 if i else d0, sp, dp, half, skip, a, b, i, rebuilt)
         backs.append(back)
     gradient = None
-    for i in range(2):
-        gradient = finish(x, backs, midcot, low, rstd, weights,
-                          i * count // 2, count // 2, gradient)
-    summed = scatter_sum(meta, [half0, half1])
+    cuts = [0, count // 4, count // 2, count]
+    for first, last in zip(cuts, cuts[1:]):
+        if last > first:
+            gradient = finish(x, backs, midcot, low, rstd, weights, first, last - first,
+                              gradient)
+    summed = scatter_sum(meta, own, other, low)
     scale = (t * lax.axis_size("seq") * lax.axis_size("fsdp")) ** (-0.5)
     return rebuilt[None], gradient[None], summed * scale
 

time: 141 us -> 138 us (0.979)
  waiting for transfers between devices: 35.6 us -> 32.1 us
    ppermute x15, waiting for transfers between devices: 18.4 us -> 16.1 us  [flip(): return lax.ppermute(x, 'fsdp', [(i, i ^ bit) for i in range(count)])]
    pallas_call x2 -> x3, Pallas kernels: 8.21 us -> 9.21 us  [finish(): pl.pallas_call(functools.partial(finish_kernel, first=first), grid=(numbe...]
    pallas_call x4 -> x5, Pallas kernels: 5.64 us -> 5.03 us  [the longest x1 1.99 us: turn(): pl.pallas_call(functools.partial(turn_kernel, rows=rows), in_specs=[SM, V...]
  transfers between devices with their start and end apart: 30 -> 30, of which waited for: 13 -> 10; matrix products, arithmetic and copies ran while one was open for 1% -> 1% of each run, Pallas kernels for 30% -> 40%
where the time goes in v2:
time: 138 us
  Pallas kernels  57.4 us (42%)
  starting transfers between devices  42.3 us (31%)
  waiting for transfers between devices  32.1 us (23%)
  local copies, waits for them, and re-layouts  3.93 us (3%)
    ppermute x6, starting transfers between devices, pass_states(): ra = lax.ppermute(sa, 'seq', pairs_a)  19.5 us
    ppermute x15, waiting for transfers between devices, flip(): return lax.ppermute(x, 'fsdp', [(i, i ^ bit) for i in range(count)])  16.1 us
    ppermute x6, waiting for transfers between devices, pass_states(): ra = lax.ppermute(sa, 'seq', pairs_a)  16 us
    ppermute x15, starting transfers between devices, flip(): return lax.ppermute(x, 'fsdp', [(i, i ^ bit) for i in range(count)])  12.9 us
    pallas_call x4, Pallas kernels, state_piece(): pl.pallas_call(functools.partial(piece_kernel, piece=piece, at=max(piece...  12.3 us
    pallas_call x3, Pallas kernels, finish(): pl.pallas_call(functools.partial(finish_kernel, first=first), grid=(numbe...  9.21 us
    pallas_call x6, Pallas kernels, absorb(): pl.pallas_call(functools.partial(absorb_kernel, j=j, fresh=held is None),...  7.74 us
    pallas_call x4, Pallas kernels, inner_grad(): pl.pallas_call(functools.partial(inner_grad_kernel, k=k), in_specs=[VM] *...  6.78 us
  transfers between devices with their start and end apart: 30, of which 10 were waited for; matrix products, arithmetic and copies ran while one was open for 1% of the time, Pallas kernels for 40%

profile of v2, /device:TPU:0, one launch (start us, length us, event | category | flops | bytes accessed | tf_op | source)
XLA Modules:
  0.0 137.6 jit_solution(9254244384072039656)
XLA Ops:
  0.6 3.0 %collective-permute-start = (bf16[512,256]{1,0:T(8,128)(2,1)}, bf16[512,256]{1,0:T(8,128)(2,1)S(1)}, u32[]{:S(2)}, u32[]{:S(2)}) collective-permute-start(bf16[512,256]{1,0:T(8,128)(2,1)} %refs_0_.1), channel_id=1, source_target_pairs={{0,2},{1,3},{2,0},{3,1},{4,6},{5,7},{6,4},{7,5},{8,10},{9,11},{10,... | collective-permute-start | bytes 786440 | tf_op jit(solution)/shard_map/ppermute | solution.py:581
  5.2 5.0 %collective-permute-done.refs_1_ = bf16[512,256]{1,0:T(8,128)(2,1)S(1)} collective-permute-done((bf16[512,256]{1,0:T(8,128)(2,1)}, bf16[512,256]{1,0:T(8,128)(2,1)S(1)}, u32[]{:S(2)}, u32[]{:S(2)}) %collective-permute-start) | collective-permute-done | bytes 262176 | tf_op jit(solution)/shard_map/ppermute | solution.py:581
  10.2 1.8 %collective-permute-start.2 = (bf16[256,256]{1,0:T(8,128)(2,1)S(1)}, bf16[256,256]{1,0:T(8,128)(2,1)S(1)}, u32[]{:S(2)}, u32[]{:S(2)}) collective-permute-start(bf16[256,256]{1,0:T(8,128)(2,1)S(1)} %slice.8), channel_id=1, source_target_pairs={{0,4},{1,5},{2,6},{3,7},{4,0},{5,1},{6,2},{7,3},{8,12},{9,13},{10,... | collective-permute-start | bytes 393224 | tf_op jit(solution)/shard_map/ppermute | solution.py:581
  15.2 1.8 %collective-permute-done.3.refs_4_ = bf16[256,256]{1,0:T(8,128)(2,1)S(1)} collective-permute-done((bf16[256,256]{1,0:T(8,128)(2,1)S(1)}, bf16[256,256]{1,0:T(8,128)(2,1)S(1)}, u32[]{:S(2)}, u32[]{:S(2)}) %collective-permute-start.3) | collective-permute-done | bytes 131104 | tf_op jit(solution)/shard_map/ppermute | solution.py:581
  18.1 2.2 %copy-done.3 = bf16[1,512,4096]{2,1,0:T(8,128)(2,1)S(1)} copy-done((bf16[1,512,4096]{2,1,0:T(8,128)(2,1)S(1)}, bf16[1,512,4096]{2,1,0:T(8,128)(2,1)}, u32[]{:S(2)}) %copy-start.3) | copy-done | bytes 4194328
  20.3 2.7 %normalize.1 = (bf16[512,4096]{1,0:T(8,128)(2,1)S(1)}, f32[512,1]{1,0:T(8,128)S(1)}, f32[512,32]{1,0:T(8,128)S(1)}, f32[512,32]{1,0:T(8,128)S(1)}, f32[4,8,4096]{2,1,0:T(8,128)S(1)}) custom-call(s32[50]{0:T(128)S(1)} %pad_add_fusion.meta.ids, bf16[512,4096]{1,0:T(8,128)(2,1)S(1)} %bitcast.22, s32[512,32]{1,0:T(8,128)S(1)} %bitcast.23), custom_call_target="tpu_custom_call" | custom-call | flops 62914560 | bytes 8388608 | tf_op jit(solution)/shard_map/normalize/pallas_call | solution.py:81
  23.0 2.0 %turn.1 = (bf16[2048,512]{1,0:T(8,128)(2,1)S(1)}, bf16[2048,512]{1,0:T(8,128)(2,1)S(1)}) custom-call(s32[50]{0:T(128)S(1)} %pad_add_fusion.meta.ids, bf16[512,4096]{1,0:T(8,128)(2,1)S(1)} %get-tuple-element.72.x), custom_call_target="tpu_custom_call" | custom-call | bytes 8388608 | tf_op jit(solution)/shard_map/turn/pallas_call | solution.py:238
  25.6 3.1 %scale_heads.1 = (bf16[512,4096]{1,0:T(8,128)(2,1)S(1)}, bf16[512,4096]{1,0:T(8,128)(2,1)S(1)}) custom-call(bf16[512,4096]{1,0:T(8,128)(2,1)S(1)} %get-tuple-element.72.x, bf16[512,4096]{1,0:T(8,128)(2,1)S(1)} %bitcast.10, f32[512,32]{1,0:T(8,128)S(1)} %get-tuple-element.73.a, f32[512,32]{1,0:T(8,128)S(1)} %get-tuple-element.74.b), custom_call_target="tpu_custom_call" | custom-call | flops 20971520 | bytes 16777216 | tf_op jit(solution)/shard_map/scale_heads/pallas_call | solution.py:121
  28.7 1.9 %project.1 = (bf16[512,256]{1,0:T(8,128)(2,1)S(1)}, bf16[4096,256]{1,0:T(8,128)(2,1)S(1)}) custom-call(s32[50]{0:T(128)S(1)} %pad_add_fusion.meta.ids, bf16[512,4096]{1,0:T(8,128)(2,1)S(1)} %get-tuple-element.72.x, bf16[512,256]{1,0:T(8,128)(2,1)S(1)} %copy-done.4, bf16[512,256]{1,0:T(8,128)(2,1)S(1)} %collective-permute-done.refs_1_, ...), custom_call_target="tpu_custom_call" | custom-call | flops 1073741824 | bytes 6291456 | tf_op jit(solution)/shard_map/project/pallas_call | solution.py:150
  32.8 4.5 %collective-permute-start.9 = (bf16[128,1024]{1,0:T(8,128)(2,1)S(1)}, bf16[128,1024]{1,0:T(8,128)(2,1)S(1)}, u32[]{:S(2)}, u32[]{:S(2)}) collective-permute-start(bf16[128,1024]{1,0:T(8,128)(2,1)S(1)} %get-tuple-element.83), channel_id=1, source_target_pairs={{0,8},{8,0},{16,24},{24,16},{1,9},{9,1},{17,25},{25,17},{2,10},{10... | collective-permute-start | bytes 786440 | tf_op jit(solution)/shard_map/ppermute | solution.py:349
  37.3 2.9 %shard_map.95 = (bf16[4,128,3072]{2,1,0:T(8,128)(2,1)S(1)}, bf16[4,128,3072]{2,1,0:T(8,128)(2,1)S(1)}, bf16[2,4,128,1024]{3,2,1,0:T(8,128)(2,1)S(1)}, f32[8,4096]{1,0:T(8,128)S(1)}) custom-call(s32[50]{0:T(128)S(1)} %pad_add_fusion.meta.ids, bf16[512,256]{1,0:T(8,128)(2,1)S(1)} %get-tuple-element.77.p, ...), custom_call_target="tpu_custom_call", output_to_operand_aliasing={{2}: (5, {}), {3}: (6, {})} | custom-call | flops 805306368 | bytes 12582912 | tf_op jit(solution)/shard_map/pallas_call | solution.py:213
  40.2 3.3 %collective-permute-done.9.ra = bf16[128,1024]{1,0:T(8,128)(2,1)S(1)} collective-permute-done((bf16[128,1024]{1,0:T(8,128)(2,1)S(1)}, bf16[128,1024]{1,0:T(8,128)(2,1)S(1)}, u32[]{:S(2)}, u32[]{:S(2)}) %collective-permute-start.9) | collective-permute-done | bytes 262176 | tf_op jit(solution)/shard_map/ppermute | solution.py:349
  44.3 1.8 %collective-permute-start.11 = (bf16[128,1024]{1,0:T(8,128)(2,1)S(1)}, bf16[128,1024]{1,0:T(8,128)(2,1)S(1)}, u32[]{:S(2)}, u32[]{:S(2)}) collective-permute-start(bf16[128,1024]{1,0:T(8,128)(2,1)S(1)} %get-tuple-element.87), channel_id=1, source_target_pairs={{0,8},{8,0},{16,24},{24,16},{1,9},{9,1},{17,25},{25,17},{2,10},{10... | collective-permute-start | bytes 786440 | tf_op jit(solution)/shard_map/ppermute | solution.py:349
  46.8 5.0 %collective-permute-done.11.ra = bf16[128,1024]{1,0:T(8,128)(2,1)S(1)} collective-permute-done((bf16[128,1024]{1,0:T(8,128)(2,1)S(1)}, bf16[128,1024]{1,0:T(8,128)(2,1)S(1)}, u32[]{:S(2)}, u32[]{:S(2)}) %collective-permute-start.11) | collective-permute-done | bytes 262176 | tf_op jit(solution)/shard_map/ppermute | solution.py:349
  52.5 3.7 %collective-permute-start.13 = (bf16[128,1024]{1,0:T(8,128)(2,1)S(1)}, bf16[128,1024]{1,0:T(8,128)(2,1)S(1)}, u32[]{:S(2)}, u32[]{:S(2)}) collective-permute-start(bf16[128,1024]{1,0:T(8,128)(2,1)S(1)} %get-tuple-element.89), channel_id=1, source_target_pairs={{0,8},{8,0},{16,24},{24,16},{1,9},{9,1},{17,25},{25,17},{2,10},{10... | collective-permute-start | bytes 786440 | tf_op jit(solution)/shard_map/ppermute | solution.py:349
  56.9 3.9 %collective-permute-done.13.ra = bf16[128,1024]{1,0:T(8,128)(2,1)S(1)} collective-permute-done((bf16[128,1024]{1,0:T(8,128)(2,1)S(1)}, bf16[128,1024]{1,0:T(8,128)(2,1)S(1)}, u32[]{:S(2)}, u32[]{:S(2)}) %collective-permute-start.13) | collective-permute-done | bytes 262176 | tf_op jit(solution)/shard_map/ppermute | solution.py:349
  61.5 3.8 %collective-permute-start.15 = (bf16[128,1024]{1,0:T(8,128)(2,1)S(1)}, bf16[128,1024]{1,0:T(8,128)(2,1)S(1)}, u32[]{:S(2)}, u32[]{:S(2)}) collective-permute-start(bf16[128,1024]{1,0:T(8,128)(2,1)S(1)} %get-tuple-element.91), channel_id=1, source_target_pairs={{0,8},{8,0},{16,24},{24,16},{1,9},{9,1},{17,25},{25,17},{2,10},{10... | collective-permute-start | bytes 786440 | tf_op jit(solution)/shard_map/ppermute | solution.py:349
  65.9 3.7 %collective-permute-done.15.ra = bf16[128,1024]{1,0:T(8,128)(2,1)S(1)} collective-permute-done((bf16[128,1024]{1,0:T(8,128)(2,1)S(1)}, bf16[128,1024]{1,0:T(8,128)(2,1)S(1)}, u32[]{:S(2)}, u32[]{:S(2)}) %collective-permute-start.15) | collective-permute-done | bytes 262176 | tf_op jit(solution)/shard_map/ppermute | solution.py:349
  70.3 4.0 %collective-permute-start.17 = (bf16[128,1024]{1,0:T(8,128)(2,1)S(1)}, bf16[128,1024]{1,0:T(8,128)(2,1)S(1)}, u32[]{:S(2)}, u32[]{:S(2)}) collective-permute-start(bf16[128,1024]{1,0:T(8,128)(2,1)S(1)} %get-tuple-element.93), channel_id=1, source_target_pairs={{0,8},{8,0},{16,24},{24,16},{1,9},{9,1},{17,25},{25,17},{2,10},{10... | collective-permute-start | bytes 786440 | tf_op jit(solution)/shard_map/ppermute | solution.py:349
  75.2 1.7 %shard_map.114.refs_3_ = f32[128,256]{1,0:T(8,128)S(1)} custom-call(bf16[512,256]{1,0:T(8,128)(2,1)S(1)} %get-tuple-element.77.p, bf16[512,4096]{1,0:T(8,128)(2,1)S(1)} %get-tuple-element.75.v, bf16[512,4096]{1,0:T(8,128)(2,1)S(1)} %get-tuple-element.76.g, bf16[4,128,1024]{2,1,0:T(8,128)(2,1)S(1)} %get-tuple-element.114.sl.sa, ...), custom_call_target="tpu_custom_call" | custom-call | flops 402653184 | bytes 4194304 | tf_op jit(solution)/shard_map/pallas_call | solution.py:374
  80.3 1.7 %shard_map.111.refs_0_ = f32[128,256]{1,0:T(8,128)S(1)} custom-call(bf16[512,256]{1,0:T(8,128)(2,1)S(1)} %get-tuple-element.77.p, bf16[512,4096]{1,0:T(8,128)(2,1)S(1)} %get-tuple-element.75.v, bf16[512,4096]{1,0:T(8,128)(2,1)S(1)} %get-tuple-element.76.g, bf16[4,128,1024]{2,1,0:T(8,128)(2,1)S(1)} %get-tuple-element.114.sl.sa, ...), custom_call_target="tpu_custom_call" | custom-call | flops 402653184 | bytes 4194304 | tf_op jit(solution)/shard_map/pallas_call | solution.py:374
  82.7 1.8 %collective-permute-start.19 = (bf16[128,1024]{1,0:T(8,128)(2,1)S(1)}, bf16[128,1024]{1,0:T(8,128)(2,1)S(1)}, u32[]{:S(2)}, u32[]{:S(2)}) collective-permute-start(bf16[128,1024]{1,0:T(8,128)(2,1)S(1)} %get-tuple-element.95), channel_id=1, source_target_pairs={{0,8},{8,0},{16,24},{24,16},{1,9},{9,1},{17,25},{25,17},{2,10},{10... | collective-permute-start | bytes 786440 | tf_op jit(solution)/shard_map/ppermute | solution.py:349
  89.9 3.1 %shard_map.107 = (bf16[512,4096]{1,0:T(8,128)(2,1)}, bf16[512,1024]{1,0:T(8,128)(2,1)S(1)}) custom-call(bf16[512,4096]{1,0:T(8,128)(2,1)S(1)} %get-tuple-element.72.x, bf16[512,4096]{1,0:T(8,128)(2,1)S(1)} %get-tuple-element.75.v, bf16[512,4096]{1,0:T(8,128)(2,1)S(1)} %get-tuple-element.76.g, bf16[512,4096]{1,0:T(8,128)(2,1)S(1)} %bitcast.11, ...), custom_call_target="tpu_custom_call" | custom-call | flops 536870912 | bytes 9437184 | tf_op jit(solution)/shard_map/pallas_call | solution.py:517
  94.1 3.1 %shard_map.108 = (bf16[512,4096]{1,0:T(8,128)(2,1)}, bf16[512,1024]{1,0:T(8,128)(2,1)S(1)}) custom-call(bf16[512,4096]{1,0:T(8,128)(2,1)S(1)} %get-tuple-element.72.x, bf16[512,4096]{1,0:T(8,128)(2,1)S(1)} %get-tuple-element.75.v, bf16[512,4096]{1,0:T(8,128)(2,1)S(1)} %get-tuple-element.76.g, ...), custom_call_target="tpu_custom_call", output_to_operand_aliasing={{0}: (14, {})} | custom-call | flops 536870912 | bytes 9437184 | tf_op jit(solution)/shard_map/pallas_call | solution.py:517
  98.4 3.1 %shard_map.109 = (bf16[512,4096]{1,0:T(8,128)(2,1)}, bf16[512,1024]{1,0:T(8,128)(2,1)S(1)}) custom-call(bf16[512,4096]{1,0:T(8,128)(2,1)S(1)} %get-tuple-element.72.x, bf16[512,4096]{1,0:T(8,128)(2,1)S(1)} %get-tuple-element.75.v, bf16[512,4096]{1,0:T(8,128)(2,1)S(1)} %get-tuple-element.76.g, ...), custom_call_target="tpu_custom_call", output_to_operand_aliasing={{0}: (14, {})} | custom-call | flops 536870912 | bytes 9437184 | tf_op jit(solution)/shard_map/pallas_call | solution.py:517
  108.0 6.3 %collective-permute-done.23.gl = bf16[4,2,128,128]{3,2,1,0:T(8,128)(2,1)S(1)} collective-permute-done((bf16[4,2,128,128]{3,2,1,0:T(8,128)(2,1)S(1)}, bf16[4,2,128,128]{3,2,1,0:T(8,128)(2,1)S(1)}, u32[]{:S(2)}, u32[]{:S(2)}) %collective-permute-start.23) | collective-permute-done | bytes 262176 | tf_op jit(solution)/shard_map/ppermute | solution.py:581
  118.1 3.1 %shard_map.110 = (bf16[512,4096]{1,0:T(8,128)(2,1)}, bf16[512,1024]{1,0:T(8,128)(2,1)S(1)}) custom-call(bf16[512,4096]{1,0:T(8,128)(2,1)S(1)} %get-tuple-element.72.x, bf16[512,4096]{1,0:T(8,128)(2,1)S(1)} %get-tuple-element.75.v, bf16[512,4096]{1,0:T(8,128)(2,1)S(1)} %get-tuple-element.76.g, ...), custom_call_target="tpu_custom_call", output_to_operand_aliasing={{0}: (14, {})} | custom-call | flops 536870912 | bytes 9437184 | tf_op jit(solution)/shard_map/pallas_call | solution.py:517
  121.2 2.6 %shard_map.115.refs_4_ = bf16[512,4096]{1,0:T(8,128)(2,1)} custom-call(bf16[512,4096]{1,0:T(8,128)(2,1)S(1)} %get-tuple-element.72.x, bf16[512,4096]{1,0:T(8,128)(2,1)S(1)} %bitcast.19, bf16[512,256]{1,0:T(8,128)(2,1)S(1)} %lower.1.low, f32[512,1]{1,0:T(8,128)S(1)} %get-tuple-element.121.rstd, bf16[4096,256]{1,0:T(8,128)(2,1)S(1)} %get-tuple-element.122.weights, ...), custom_call_target="tpu_custom_call" | custom-call | flops 268435456 | bytes 4194304 | tf_op jit(solution)/shard_map/pallas_call | solution.py:566
  124.4 3.3 %collective-permute-start.27 = (bf16[128,256]{1,0:T(8,128)(2,1)S(1)}, bf16[128,256]{1,0:T(8,128)(2,1)S(1)}, u32[]{:S(2)}, u32[]{:S(2)}) collective-permute-start(bf16[128,256]{1,0:T(8,128)(2,1)S(1)} %get-tuple-element.138), channel_id=1, source_target_pairs={{0,8},{8,0},{16,24},{24,16},{1,9},{9,1},{17,25},{25,17},{2,10},{10... | collective-permute-start | bytes 196616 | tf_op jit(solution)/shard_map/ppermute | solution.py:675
  128.0 2.2 %collective-permute-start.29 = (bf16[128,256]{1,0:T(8,128)(2,1)S(1)}, bf16[128,256]{1,0:T(8,128)(2,1)S(1)}, u32[]{:S(2)}, u32[]{:S(2)}) collective-permute-start(bf16[128,256]{1,0:T(8,128)(2,1)S(1)} %get-tuple-element.140), channel_id=1, source_target_pairs={{0,24},{8,16},{16,8},{24,0},{1,25},{9,17},{17,9},{25,1},{2,26},{10... | collective-permute-start | bytes 196616 | tf_op jit(solution)/shard_map/ppermute | solution.py:675
  130.2 2.6 %shard_map.116.refs_4_ = bf16[512,4096]{1,0:T(8,128)(2,1)} custom-call(bf16[512,4096]{1,0:T(8,128)(2,1)S(1)} %get-tuple-element.72.x, bf16[512,4096]{1,0:T(8,128)(2,1)S(1)} %bitcast.20, bf16[512,256]{1,0:T(8,128)(2,1)S(1)} %lower.1.low, f32[512,1]{1,0:T(8,128)S(1)} %get-tuple-element.121.rstd, ...), custom_call_target="tpu_custom_call", output_to_operand_aliasing={{}: (9, {})} | custom-call | flops 268435456 | bytes 4194304 | tf_op jit(solution)/shard_map/pallas_call | solution.py:566
  132.8 4.1 %shard_map.117 = bf16[512,4096]{1,0:T(8,128)(2,1)} custom-call(bf16[512,4096]{1,0:T(8,128)(2,1)S(1)} %get-tuple-element.72.x, bf16[512,4096]{1,0:T(8,128)(2,1)S(1)} %bitcast.21, bf16[512,256]{1,0:T(8,128)(2,1)S(1)} %lower.1.low, f32[512,1]{1,0:T(8,128)S(1)} %get-tuple-element.121.rstd, ...), custom_call_target="tpu_custom_call", output_to_operand_aliasing={{}: (9, {})} | custom-call | flops 536870912 | bytes 8388608 | tf_op jit(solution)/shard_map/pallas_call | solution.py:566
  (86 shorter events, 37.9 us)
Async XLA Ops:
  0.6 9.6 %collective-permute-start = (bf16[512,256]{1,0:T(8,128)(2,1)}, bf16[512,256]{1,0:T(8,128)(2,1)S(1)}, u32[]{:S(2)}, u32[]{:S(2)}) collective-permute-start(bf16[512,256]{1,0:T(8,128)(2,1)} %refs_0_.1), channel_id=1, source_target_pairs={{0,2},{1,3},{2,0},{3,1},{4,6},{5,7},{6,4},{7,5},{8,10},{9,11},{10,... | collective-permute-start | bytes 786440 | tf_op jit(solution)/shard_map/ppermute | solution.py:581
  3.7 8.4 %collective-permute-start.1 = (bf16[512,256]{1,0:T(8,128)(2,1)}, bf16[512,256]{1,0:T(8,128)(2,1)S(1)}, u32[]{:S(2)}, u32[]{:S(2)}) collective-permute-start(bf16[512,256]{1,0:T(8,128)(2,1)} %refs_0_.1), channel_id=1, source_target_pairs={{0,4},{1,5},{2,6},{3,7},{4,0},{5,1},{6,2},{7,3},{8,12},{9,13},{10,... | collective-permute-start | bytes 786440 | tf_op jit(solution)/shard_map/ppermute | solution.py:581
  5.2 19.8 %collective-permute-start.4 = (bf16[512,256]{1,0:T(8,128)(2,1)}, bf16[512,256]{1,0:T(8,128)(2,1)S(1)}, u32[]{:S(2)}, u32[]{:S(2)}) collective-permute-start(bf16[512,256]{1,0:T(8,128)(2,1)} %refs_0_.1), channel_id=1, source_target_pairs={{0,1},{1,0},{2,3},{3,2},{4,5},{5,4},{6,7},{7,6},{8,9},{9,8},{10,11... | collective-permute-start | bytes 786440 | tf_op jit(solution)/shard_map/ppermute | solution.py:581
  10.2 5.0 %collective-permute-start.2 = (bf16[256,256]{1,0:T(8,128)(2,1)S(1)}, bf16[256,256]{1,0:T(8,128)(2,1)S(1)}, u32[]{:S(2)}, u32[]{:S(2)}) collective-permute-start(bf16[256,256]{1,0:T(8,128)(2,1)S(1)} %slice.8), channel_id=1, source_target_pairs={{0,4},{1,5},{2,6},{3,7},{4,0},{5,1},{6,2},{7,3},{8,12},{9,13},{10,... | collective-permute-start | bytes 393224 | tf_op jit(solution)/shard_map/ppermute | solution.py:581
  12.0 5.0 %collective-permute-start.3 = (bf16[256,256]{1,0:T(8,128)(2,1)S(1)}, bf16[256,256]{1,0:T(8,128)(2,1)S(1)}, u32[]{:S(2)}, u32[]{:S(2)}) collective-permute-start(bf16[256,256]{1,0:T(8,128)(2,1)S(1)} %slice.9), channel_id=1, source_target_pairs={{0,2},{1,3},{2,0},{3,1},{4,6},{5,7},{6,4},{7,5},{8,10},{9,11},{10,... | collective-permute-start | bytes 393224 | tf_op jit(solution)/shard_map/ppermute | solution.py:581
  13.6 15.1 %collective-permute-start.5 = (bf16[512,256]{1,0:T(8,128)(2,1)S(1)}, bf16[512,256]{1,0:T(8,128)(2,1)S(1)}, u32[]{:S(2)}, u32[]{:S(2)}) collective-permute-start(bf16[512,256]{1,0:T(8,128)(2,1)S(1)} %collective-permute-done.refs_1_), channel_id=1, source_target_pairs={{0,1},{1,0},{2,3},{3,2},{4,5},{5,4},{6,7},{7,6},{8,9},{9,8},{10,11... | collective-permute-start | bytes 786440 | tf_op jit(solution)/shard_map/ppermute | solution.py:581
  13.6 15.1 %collective-permute-start.6 = (bf16[512,256]{1,0:T(8,128)(2,1)S(1)}, bf16[512,256]{1,0:T(8,128)(2,1)S(1)}, u32[]{:S(2)}, u32[]{:S(2)}) collective-permute-start(bf16[512,256]{1,0:T(8,128)(2,1)S(1)} %collective-permute-done.1.refs_2_), channel_id=1, source_target_pairs={{0,1},{1,0},{2,3},{3,2},{4,5},{5,4},{6,7},{7,6},{8,9},{9,8},{10,11... | collective-permute-start | bytes 786440 | tf_op jit(solution)/shard_map/ppermute | solution.py:581
  15.2 13.4 %collective-permute-start.7 = (bf16[256,256]{1,0:T(8,128)(2,1)S(1)}, bf16[256,256]{1,0:T(8,128)(2,1)S(1)}, u32[]{:S(2)}, u32[]{:S(2)}) collective-permute-start(bf16[256,256]{1,0:T(8,128)(2,1)S(1)} %collective-permute-done.2.refs_3_), channel_id=1, source_target_pairs={{0,1},{1,0},{2,3},{3,2},{4,5},{5,4},{6,7},{7,6},{8,9},{9,8},{10,11... | collective-permute-start | bytes 393224 | tf_op jit(solution)/shard_map/ppermute | solution.py:581
  17.1 11.6 %collective-permute-start.8 = (bf16[256,256]{1,0:T(8,128)(2,1)S(1)}, bf16[256,256]{1,0:T(8,128)(2,1)S(1)}, u32[]{:S(2)}, u32[]{:S(2)}) collective-permute-start(bf16[256,256]{1,0:T(8,128)(2,1)S(1)} %collective-permute-done.3.refs_4_), channel_id=1, source_target_pairs={{0,1},{1,0},{2,3},{3,2},{4,5},{5,4},{6,7},{7,6},{8,9},{9,8},{10,11... | collective-permute-start | bytes 393224 | tf_op jit(solution)/shard_map/ppermute | solution.py:581
  25.0 78.7 %collective-permute-start.21 = (bf16[2048,512]{1,0:T(8,128)(2,1)S(1)}, bf16[2048,512]{1,0:T(8,128)(2,1)S(1)}, u32[]{:S(2)}, u32[]{:S(2)}) collective-permute-start(bf16[2048,512]{1,0:T(8,128)(2,1)S(1)} %get-tuple-element.127), channel_id=1, source_target_pairs={{0,1},{1,0},{2,3},{3,2},{4,5},{5,4},{6,7},{7,6},{8,9},{9,8},{10,11... | collective-permute-start | bytes 6291464 | tf_op jit(solution)/shard_map/ppermute | solution.py:581
  25.6 3.1 %copy-start.4 = (bf16[512,256]{1,0:T(8,128)(2,1)S(1)}, bf16[512,256]{1,0:T(8,128)(2,1)}, u32[]{:S(2)}) copy-start(bf16[512,256]{1,0:T(8,128)(2,1)} %refs_0_.1) | copy-start | bytes 786436
  32.1 8.1 %collective-permute-start.10 = (bf16[128,1024]{1,0:T(8,128)(2,1)S(1)}, bf16[128,1024]{1,0:T(8,128)(2,1)S(1)}, u32[]{:S(2)}, u32[]{:S(2)}) collective-permute-start(bf16[128,1024]{1,0:T(8,128)(2,1)S(1)} %get-tuple-element.84), channel_id=1, source_target_pairs={{8,16},{16,8},{9,17},{17,9},{10,18},{18,10},{11,19},{19,11},{12,20... | collective-permute-start | bytes 786440 | tf_op jit(solution)/shard_map/ppermute | solution.py:350
  32.8 10.7 %collective-permute-start.9 = (bf16[128,1024]{1,0:T(8,128)(2,1)S(1)}, bf16[128,1024]{1,0:T(8,128)(2,1)S(1)}, u32[]{:S(2)}, u32[]{:S(2)}) collective-permute-start(bf16[128,1024]{1,0:T(8,128)(2,1)S(1)} %get-tuple-element.83), channel_id=1, source_target_pairs={{0,8},{8,0},{16,24},{24,16},{1,9},{9,1},{17,25},{25,17},{2,10},{10... | collective-permute-start | bytes 786440 | tf_op jit(solution)/shard_map/ppermute | solution.py:349
  44.3 7.5 %collective-permute-start.11 = (bf16[128,1024]{1,0:T(8,128)(2,1)S(1)}, bf16[128,1024]{1,0:T(8,128)(2,1)S(1)}, u32[]{:S(2)}, u32[]{:S(2)}) collective-permute-start(bf16[128,1024]{1,0:T(8,128)(2,1)S(1)} %get-tuple-element.87), channel_id=1, source_target_pairs={{0,8},{8,0},{16,24},{24,16},{1,9},{9,1},{17,25},{25,17},{2,10},{10... | collective-permute-start | bytes 786440 | tf_op jit(solution)/shard_map/ppermute | solution.py:349
  46.1 5.7 %collective-permute-start.12 = (bf16[128,1024]{1,0:T(8,128)(2,1)S(1)}, bf16[128,1024]{1,0:T(8,128)(2,1)S(1)}, u32[]{:S(2)}, u32[]{:S(2)}) collective-permute-start(bf16[128,1024]{1,0:T(8,128)(2,1)S(1)} %get-tuple-element.88), channel_id=1, source_target_pairs={{8,16},{16,8},{9,17},{17,9},{10,18},{18,10},{11,19},{19,11},{12,20... | collective-permute-start | bytes 786440 | tf_op jit(solution)/shard_map/ppermute | solution.py:350
  52.5 8.3 %collective-permute-start.13 = (bf16[128,1024]{1,0:T(8,128)(2,1)S(1)}, bf16[128,1024]{1,0:T(8,128)(2,1)S(1)}, u32[]{:S(2)}, u32[]{:S(2)}) collective-permute-start(bf16[128,1024]{1,0:T(8,128)(2,1)S(1)} %get-tuple-element.89), channel_id=1, source_target_pairs={{0,8},{8,0},{16,24},{24,16},{1,9},{9,1},{17,25},{25,17},{2,10},{10... | collective-permute-start | bytes 786440 | tf_op jit(solution)/shard_map/ppermute | solution.py:349
  56.2 4.6 %collective-permute-start.14 = (bf16[128,1024]{1,0:T(8,128)(2,1)S(1)}, bf16[128,1024]{1,0:T(8,128)(2,1)S(1)}, u32[]{:S(2)}, u32[]{:S(2)}) collective-permute-start(bf16[128,1024]{1,0:T(8,128)(2,1)S(1)} %get-tuple-element.90), channel_id=1, source_target_pairs={{8,16},{16,8},{9,17},{17,9},{10,18},{18,10},{11,19},{19,11},{12,20... | collective-permute-start | bytes 786440 | tf_op jit(solution)/shard_map/ppermute | solution.py:350
  61.5 8.1 %collective-permute-start.15 = (bf16[128,1024]{1,0:T(8,128)(2,1)S(1)}, bf16[128,1024]{1,0:T(8,128)(2,1)S(1)}, u32[]{:S(2)}, u32[]{:S(2)}) collective-permute-start(bf16[128,1024]{1,0:T(8,128)(2,1)S(1)} %get-tuple-element.91), channel_id=1, source_target_pairs={{0,8},{8,0},{16,24},{24,16},{1,9},{9,1},{17,25},{25,17},{2,10},{10... | collective-permute-start | bytes 786440 | tf_op jit(solution)/shard_map/ppermute | solution.py:349
  65.3 4.4 %collective-permute-start.16 = (bf16[128,1024]{1,0:T(8,128)(2,1)S(1)}, bf16[128,1024]{1,0:T(8,128)(2,1)S(1)}, u32[]{:S(2)}, u32[]{:S(2)}) collective-permute-start(bf16[128,1024]{1,0:T(8,128)(2,1)S(1)} %get-tuple-element.92), channel_id=1, source_target_pairs={{8,16},{16,8},{9,17},{17,9},{10,18},{18,10},{11,19},{19,11},{12,20... | collective-permute-start | bytes 786440 | tf_op jit(solution)/shard_map/ppermute | solution.py:350
  70.3 11.7 %collective-permute-start.17 = (bf16[128,1024]{1,0:T(8,128)(2,1)S(1)}, bf16[128,1024]{1,0:T(8,128)(2,1)S(1)}, u32[]{:S(2)}, u32[]{:S(2)}) collective-permute-start(bf16[128,1024]{1,0:T(8,128)(2,1)S(1)} %get-tuple-element.93), channel_id=1, source_target_pairs={{0,8},{8,0},{16,24},{24,16},{1,9},{9,1},{17,25},{25,17},{2,10},{10... | collective-permute-start | bytes 786440 | tf_op jit(solution)/shard_map/ppermute | solution.py:349
  74.3 7.7 %collective-permute-start.18 = (bf16[128,1024]{1,0:T(8,128)(2,1)S(1)}, bf16[128,1024]{1,0:T(8,128)(2,1)S(1)}, u32[]{:S(2)}, u32[]{:S(2)}) collective-permute-start(bf16[128,1024]{1,0:T(8,128)(2,1)S(1)} %get-tuple-element.94), channel_id=1, source_target_pairs={{8,16},{16,8},{9,17},{17,9},{10,18},{18,10},{11,19},{19,11},{12,20... | collective-permute-start | bytes 786440 | tf_op jit(solution)/shard_map/ppermute | solution.py:350
  82.7 18.7 %collective-permute-start.19 = (bf16[128,1024]{1,0:T(8,128)(2,1)S(1)}, bf16[128,1024]{1,0:T(8,128)(2,1)S(1)}, u32[]{:S(2)}, u32[]{:S(2)}) collective-permute-start(bf16[128,1024]{1,0:T(8,128)(2,1)S(1)} %get-tuple-element.95), channel_id=1, source_target_pairs={{0,8},{8,0},{16,24},{24,16},{1,9},{9,1},{17,25},{25,17},{2,10},{10... | collective-permute-start | bytes 786440 | tf_op jit(solution)/shard_map/ppermute | solution.py:349
  84.5 17.0 %collective-permute-start.20 = (bf16[128,1024]{1,0:T(8,128)(2,1)S(1)}, bf16[128,1024]{1,0:T(8,128)(2,1)S(1)}, u32[]{:S(2)}, u32[]{:S(2)}) collective-permute-start(bf16[128,1024]{1,0:T(8,128)(2,1)S(1)} %get-tuple-element.96), channel_id=1, source_target_pairs={{8,16},{16,8},{9,17},{17,9},{10,18},{18,10},{11,19},{19,11},{12,20... | collective-permute-start | bytes 786440 | tf_op jit(solution)/shard_map/ppermute | solution.py:350
  102.9 1.6 %collective-permute-start.22 = (bf16[512,256]{1,0:T(8,128)(2,1)S(1)}, bf16[512,256]{1,0:T(8,128)(2,1)S(1)}, u32[]{:S(2)}, u32[]{:S(2)}) collective-permute-start(bf16[512,256]{1,0:T(8,128)(2,1)S(1)} %lower.1.low), channel_id=1, source_target_pairs={{0,1},{1,0},{2,3},{3,2},{4,5},{5,4},{6,7},{7,6},{8,9},{9,8},{10,11... | collective-permute-start | bytes 786440 | tf_op jit(solution)/shard_map/ppermute | solution.py:581
  106.0 8.4 %collective-permute-start.23 = (bf16[4,2,128,128]{3,2,1,0:T(8,128)(2,1)S(1)}, bf16[4,2,128,128]{3,2,1,0:T(8,128)(2,1)S(1)}, u32[]{:S(2)}, u32[]{:S(2)}) collective-permute-start(bf16[4,2,128,128]{3,2,1,0:T(8,128)(2,1)S(1)} %get-tuple-element.130), channel_id=1, source_target_pairs={{0,2},{1,3},{2,0},{3,1},{4,6},{5,7},{6,4},{7,5},{8,10},{9,11},{10,... | collective-permute-start | bytes 786440 | tf_op jit(solution)/shard_map/ppermute | solution.py:581
  107.5 8.1 %collective-permute-start.24 = (bf16[4,2,128,128]{3,2,1,0:T(8,128)(2,1)S(1)}, bf16[4,2,128,128]{3,2,1,0:T(8,128)(2,1)S(1)}, u32[]{:S(2)}, u32[]{:S(2)}) collective-permute-start(bf16[4,2,128,128]{3,2,1,0:T(8,128)(2,1)S(1)} %get-tuple-element.132), channel_id=1, source_target_pairs={{0,4},{1,5},{2,6},{3,7},{4,0},{5,1},{6,2},{7,3},{8,12},{9,13},{10,... | collective-permute-start | bytes 786440 | tf_op jit(solution)/shard_map/ppermute | solution.py:581
  116.4 7.4 %collective-permute-start.25 = (bf16[4,1,128,128]{3,2,1,0:T(8,128)(2,1)S(1)}, bf16[4,1,128,128]{3,2,1,0:T(8,128)(2,1)S(1)}, u32[]{:S(2)}, u32[]{:S(2)}) collective-permute-start(bf16[4,1,128,128]{3,2,1,0:T(8,128)(2,1)S(1)} %get-tuple-element.134), channel_id=1, source_target_pairs={{0,4},{1,5},{2,6},{3,7},{4,0},{5,1},{6,2},{7,3},{8,12},{9,13},{10,... | collective-permute-start | bytes 393224 | tf_op jit(solution)/shard_map/ppermute | solution.py:581
  117.0 6.8 %collective-permute-start.26 = (bf16[4,1,128,128]{3,2,1,0:T(8,128)(2,1)S(1)}, bf16[4,1,128,128]{3,2,1,0:T(8,128)(2,1)S(1)}, u32[]{:S(2)}, u32[]{:S(2)}) collective-permute-start(bf16[4,1,128,128]{3,2,1,0:T(8,128)(2,1)S(1)} %get-tuple-element.136), channel_id=1, source_target_pairs={{0,2},{1,3},{2,0},{3,1},{4,6},{5,7},{6,4},{7,5},{8,10},{9,11},{10,... | collective-permute-start | bytes 393224 | tf_op jit(solution)/shard_map/ppermute | solution.py:581
  118.1 3.1 %copy-start.2 = (bf16[1,512,4096]{2,1,0:T(8,128)(2,1)S(1)}, bf16[1,512,4096]{2,1,0:T(8,128)(2,1)}, u32[]{:S(2)}) copy-start(bf16[1,512,4096]{2,1,0:T(8,128)(2,1)} %param.9) | copy-start | bytes 12582916
  124.4 12.4 %collective-permute-start.27 = (bf16[128,256]{1,0:T(8,128)(2,1)S(1)}, bf16[128,256]{1,0:T(8,128)(2,1)S(1)}, u32[]{:S(2)}, u32[]{:S(2)}) collective-permute-start(bf16[128,256]{1,0:T(8,128)(2,1)S(1)} %get-tuple-element.138), channel_id=1, source_target_pairs={{0,8},{8,0},{16,24},{24,16},{1,9},{9,1},{17,25},{25,17},{2,10},{10... | collective-permute-start | bytes 196616 | tf_op jit(solution)/shard_map/ppermute | solution.py:675
  127.8 9.1 %collective-permute-start.28 = (bf16[128,256]{1,0:T(8,128)(2,1)S(1)}, bf16[128,256]{1,0:T(8,128)(2,1)S(1)}, u32[]{:S(2)}, u32[]{:S(2)}) collective-permute-start(bf16[128,256]{1,0:T(8,128)(2,1)S(1)} %get-tuple-element.139), channel_id=1, source_target_pairs={{0,16},{8,24},{16,0},{24,8},{1,17},{9,25},{17,1},{25,9},{2,18},{10... | collective-permute-start | bytes 196616 | tf_op jit(solution)/shard_map/ppermute | solution.py:675
  128.0 8.8 %collective-permute-start.29 = (bf16[128,256]{1,0:T(8,128)(2,1)S(1)}, bf16[128,256]{1,0:T(8,128)(2,1)S(1)}, u32[]{:S(2)}, u32[]{:S(2)}) collective-permute-start(bf16[128,256]{1,0:T(8,128)(2,1)S(1)} %get-tuple-element.140), channel_id=1, source_target_pairs={{0,24},{8,16},{16,8},{24,0},{1,25},{9,17},{17,9},{25,1},{2,26},{10... | collective-permute-start | bytes 196616 | tf_op jit(solution)/shard_map/ppermute | solution.py:675
  (4 other events, 8.6 us)

commit v3 on v2

--- a/solution.py
+++ b/solution.py
@@ -456,7 +456,7 @@
 
 
 def piece_kernel(x, v, g, cot, newest, p, sl, dl, si, di, half, skip, a, b, *refs, piece, at, ps):
-    rebuilt_o, back_o, rhs, lhs = refs[-4:]
+    rebuilt_o, back_o, dots_o, rhs, lhs = refs[-5:]
     q, w = rebuilt_o.shape
     n = p.shape[1] // 2
     per = w // ps
@@ -497,6 +497,9 @@
         wide = slice(hh * ps, (hh + 1) * ps)
         gr = back[:, own] * bv[:, hh : hh + 1] + skip[0:1, wide] * cot[rows, wide].astype(f32)
         back_o[rows, own] = gr.astype(bf16)
+        prod = gr * x[rows, wide].astype(f32)
+        sums = prod if h == 0 else sums + prod
+    dots_o[rows, :] = sums
 
 
 def state_piece(x, v, g, cot, newest, p, sl, dl, si, di, half, skip, a, b, piece, previous):
@@ -518,8 +521,8 @@
         functools.partial(piece_kernel, piece=piece, at=max(piece - 1, 0), ps=d // heads),
         grid=(t // CHUNK,),
         in_specs=in_specs,
-        out_specs=[cols, VM],
-        out_shape=[pltpu.HBM((t, d), bf16), kept((t, w), bf16)],
+        out_specs=[cols, VM, VM],
+        out_shape=[pltpu.HBM((t, d), bf16), kept((t, w), bf16), kept((t, d // heads), f32)],
         scratch_shapes=[pltpu.VMEM((CHUNK + n, w), bf16), pltpu.VMEM((CHUNK, CHUNK + n), bf16)],
         input_output_aliases=aliases,
         compiler_params=params(8),
@@ -527,37 +530,35 @@
     )(*args)
 
 
-def finish_kernel(x, midcot, low, rstd, weights, *refs, first):
-    backs = refs[:PIECES]
-    grad_o, grad = refs[-2:]
-    q, d = grad_o.shape
+def finish_kernel(x, midcot, low, p, rstd, weights, *refs, first):
+    backs, sums = refs[:PIECES], refs[PIECES : 2 * PIECES]
+    grad_o = refs[-1]
+    q, d = CHUNK, x.shape[1]
     rows = span(first + pl.program_id(0), q)
     lhs = low[rows, :]
     w = d // PIECES
     step = 256
-    sums = jnp.zeros((q, 128), f32)
+    both = lhs.astype(f32) * p[rows, :].astype(f32)
+    total = sums[0][rows, :]
+    for other in sums[1:]:
+        total = total + other[rows, :]
+    dots = jnp.sum(total, axis=-1, keepdims=True) + jnp.sum(both, axis=-1, keepdims=True)
+    scale = jnp.broadcast_to(rstd[rows, :], (q, step))
+    dots = jnp.broadcast_to(dots, (q, step)) * (scale * (1.0 / d))
     for i in range(d // step):
         cols = slice(i * step, (i + 1) * step)
         inside = slice(i * step % w, i * step % w + step)
         gr = dot(lhs, weights[cols, :], 1, 1) + backs[i * step // w][rows, inside].astype(f32)
-        grad[:, cols] = gr
-        prod = gr * x[rows, cols].astype(f32)
-        for c in range(step // 128):
-            sums = sums + prod[:, c * 128 : (c + 1) * 128]
-    scale = jnp.broadcast_to(rstd[rows, :], (q, 128))
-    dots = jnp.broadcast_to(jnp.sum(sums, axis=-1, keepdims=True), (q, 128)) * (scale * (1.0 / d))
-    for i in range(d // 128):
-        cols = slice(i * 128, (i + 1) * 128)
-        dx = scale * grad[:, cols] - x[rows, cols].astype(f32) * dots
+        dx = scale * gr - x[rows, cols].astype(f32) * dots
         grad_o[:, cols] = (midcot[rows, cols].astype(f32) + dx).astype(bf16)
 
 
-def finish(x, backs, midcot, low, rstd, weights, first, number, previous):
+def finish(x, backs, sums, midcot, low, p, rstd, weights, first, number, previous):
     t, d = x.shape
     n2 = low.shape[1]
     row = pl.BlockSpec((CHUNK, d), lambda i: (first + i, 0))
-    args = [near(x), near(midcot), near(low), near(rstd), near(weights), *map(near, backs)]
-    in_specs = [VM] * (5 + PIECES)
+    args = [*map(near, (x, midcot, low, p, rstd, weights)), *map(near, backs), *map(near, sums)]
+    in_specs = [VM] * (6 + 2 * PIECES)
     aliases = {}
     if previous is not None:
         aliases = {len(args): 0}
@@ -569,9 +570,8 @@
         in_specs=in_specs,
         out_specs=row,
         out_shape=pltpu.HBM((t, d), bf16),
-        scratch_shapes=[pltpu.VMEM((CHUNK, d), f32)],
         input_output_aliases=aliases,
-        compiler_params=params(12),
+        compiler_params=params(8),
         cost_estimate=cost(2 * number * CHUNK * d * n2, 8 * number * CHUNK * d),
     )(*args)
 
@@ -696,17 +696,18 @@
     acc, heads_done = pass_states(meta, sa, sb, loc, dtot, v, g, half)
     low = lower(acc, inner)
     skip = jnp.repeat(skip_gain, d // heads)[None]
-    rebuilt, backs = None, []
+    rebuilt, backs, sums = None, [], []
     for i in range(PIECES):
         sp, dp = heads_done[i]
-        rebuilt, back = state_piece(
+        rebuilt, back, dots = state_piece(
             x, v, g, cot, newest, p, s1 if i else s0, d1 if i else d0, sp, dp, half, skip, a, b, i, rebuilt)
         backs.append(back)
+        sums.append(dots)
     gradient = None
     cuts = [0, count // 4, count // 2, count]
     for first, last in zip(cuts, cuts[1:]):
         if last > first:
-            gradient = finish(x, backs, midcot, low, rstd, weights, first, last - first,
+            gradient = finish(x, backs, sums, midcot, low, p, rstd, weights, first, last - first,
                               gradient)
     summed = scatter_sum(meta, own, other, low)
     scale = (t * lax.axis_size("seq") * lax.axis_size("fsdp")) ** (-0.5)

time: 138 us -> 136 us (0.986)
  Pallas kernels: 57.4 us -> 55.3 us
    pallas_call x3, Pallas kernels: 9.21 us -> 6.77 us  [finish(): pl.pallas_call(functools.partial(finish_kernel, first=first), grid=(numbe...]
  transfers between devices with their start and end apart: 30 -> 30, of which waited for: 10 -> 10; matrix products, arithmetic and copies ran while one was open for 1% -> 1% of each run, Pallas kernels for 40% -> 39%
where the time goes in v3:
time: 136 us
  Pallas kernels  55.3 us (41%)
  starting transfers between devices  42.4 us (31%)
  waiting for transfers between devices  32.1 us (24%)
  local copies, waits for them, and re-layouts  3.93 us (3%)
    ppermute x6, starting transfers between devices, pass_states(): ra = lax.ppermute(sa, 'seq', pairs_a)  19.5 us
    ppermute x15, waiting for transfers between devices, flip(): return lax.ppermute(x, 'fsdp', [(i, i ^ bit) for i in range(count)])  16.1 us
    ppermute x6, waiting for transfers between devices, pass_states(): ra = lax.ppermute(sa, 'seq', pairs_a)  16 us
    ppermute x15, starting transfers between devices, flip(): return lax.ppermute(x, 'fsdp', [(i, i ^ bit) for i in range(count)])  12.9 us
    pallas_call x4, Pallas kernels, state_piece(): pl.pallas_call(functools.partial(piece_kernel, piece=piece, at=max(piece...  12.7 us
    pallas_call x6, Pallas kernels, absorb(): pl.pallas_call(functools.partial(absorb_kernel, j=j, fresh=held is None),...  7.75 us
    pallas_call x4, Pallas kernels, inner_grad(): pl.pallas_call(functools.partial(inner_grad_kernel, k=k), in_specs=[VM] *...  6.79 us
    pallas_call x3, Pallas kernels, finish(): pl.pallas_call(functools.partial(finish_kernel, first=first), grid=(numbe...  6.77 us
  transfers between devices with their start and end apart: 30, of which 10 were waited for; matrix products, arithmetic and copies ran while one was open for 1% of the time, Pallas kernels for 39%

profile of v3, /device:TPU:0, one launch (start us, length us, event | category | flops | bytes accessed | tf_op | source)
XLA Modules:
  0.0 135.5 jit_solution(5416360867348725264)
XLA Ops:
  0.6 3.0 %collective-permute-start = (bf16[512,256]{1,0:T(8,128)(2,1)}, bf16[512,256]{1,0:T(8,128)(2,1)S(1)}, u32[]{:S(2)}, u32[]{:S(2)}) collective-permute-start(bf16[512,256]{1,0:T(8,128)(2,1)} %refs_0_.1), channel_id=1, source_target_pairs={{0,2},{1,3},{2,0},{3,1},{4,6},{5,7},{6,4},{7,5},{8,10},{9,11},{10,... | collective-permute-start | bytes 786440 | tf_op jit(solution)/shard_map/ppermute | solution.py:581
  5.2 5.0 %collective-permute-done.refs_1_ = bf16[512,256]{1,0:T(8,128)(2,1)S(1)} collective-permute-done((bf16[512,256]{1,0:T(8,128)(2,1)}, bf16[512,256]{1,0:T(8,128)(2,1)S(1)}, u32[]{:S(2)}, u32[]{:S(2)}) %collective-permute-start) | collective-permute-done | bytes 262176 | tf_op jit(solution)/shard_map/ppermute | solution.py:581
  10.2 1.8 %collective-permute-start.2 = (bf16[256,256]{1,0:T(8,128)(2,1)S(1)}, bf16[256,256]{1,0:T(8,128)(2,1)S(1)}, u32[]{:S(2)}, u32[]{:S(2)}) collective-permute-start(bf16[256,256]{1,0:T(8,128)(2,1)S(1)} %slice.8), channel_id=1, source_target_pairs={{0,4},{1,5},{2,6},{3,7},{4,0},{5,1},{6,2},{7,3},{8,12},{9,13},{10,... | collective-permute-start | bytes 393224 | tf_op jit(solution)/shard_map/ppermute | solution.py:581
  15.2 1.8 %collective-permute-done.3.refs_4_ = bf16[256,256]{1,0:T(8,128)(2,1)S(1)} collective-permute-done((bf16[256,256]{1,0:T(8,128)(2,1)S(1)}, bf16[256,256]{1,0:T(8,128)(2,1)S(1)}, u32[]{:S(2)}, u32[]{:S(2)}) %collective-permute-start.3) | collective-permute-done | bytes 131104 | tf_op jit(solution)/shard_map/ppermute | solution.py:581
  18.1 2.2 %copy-done.3 = bf16[1,512,4096]{2,1,0:T(8,128)(2,1)S(1)} copy-done((bf16[1,512,4096]{2,1,0:T(8,128)(2,1)S(1)}, bf16[1,512,4096]{2,1,0:T(8,128)(2,1)}, u32[]{:S(2)}) %copy-start.3) | copy-done | bytes 4194328
  20.3 2.7 %normalize.1 = (bf16[512,4096]{1,0:T(8,128)(2,1)S(1)}, f32[512,1]{1,0:T(8,128)S(1)}, f32[512,32]{1,0:T(8,128)S(1)}, f32[512,32]{1,0:T(8,128)S(1)}, f32[4,8,4096]{2,1,0:T(8,128)S(1)}) custom-call(s32[50]{0:T(128)S(1)} %pad_add_fusion.meta.ids, bf16[512,4096]{1,0:T(8,128)(2,1)S(1)} %bitcast.22, s32[512,32]{1,0:T(8,128)S(1)} %bitcast.23), custom_call_target="tpu_custom_call" | custom-call | flops 62914560 | bytes 8388608 | tf_op jit(solution)/shard_map/normalize/pallas_call | solution.py:81
  23.0 2.0 %turn.1 = (bf16[2048,512]{1,0:T(8,128)(2,1)S(1)}, bf16[2048,512]{1,0:T(8,128)(2,1)S(1)}) custom-call(s32[50]{0:T(128)S(1)} %pad_add_fusion.meta.ids, bf16[512,4096]{1,0:T(8,128)(2,1)S(1)} %get-tuple-element.76.x), custom_call_target="tpu_custom_call" | custom-call | bytes 8388608 | tf_op jit(solution)/shard_map/turn/pallas_call | solution.py:238
  25.6 3.1 %scale_heads.1 = (bf16[512,4096]{1,0:T(8,128)(2,1)S(1)}, bf16[512,4096]{1,0:T(8,128)(2,1)S(1)}) custom-call(bf16[512,4096]{1,0:T(8,128)(2,1)S(1)} %get-tuple-element.76.x, bf16[512,4096]{1,0:T(8,128)(2,1)S(1)} %bitcast.10, f32[512,32]{1,0:T(8,128)S(1)} %get-tuple-element.77.a, f32[512,32]{1,0:T(8,128)S(1)} %get-tuple-element.78.b), custom_call_target="tpu_custom_call" | custom-call | flops 20971520 | bytes 16777216 | tf_op jit(solution)/shard_map/scale_heads/pallas_call | solution.py:121
  28.7 1.9 %project.1 = (bf16[512,256]{1,0:T(8,128)(2,1)S(1)}, bf16[4096,256]{1,0:T(8,128)(2,1)S(1)}) custom-call(s32[50]{0:T(128)S(1)} %pad_add_fusion.meta.ids, bf16[512,4096]{1,0:T(8,128)(2,1)S(1)} %get-tuple-element.76.x, bf16[512,256]{1,0:T(8,128)(2,1)S(1)} %copy-done.4, bf16[512,256]{1,0:T(8,128)(2,1)S(1)} %collective-permute-done.refs_1_, ...), custom_call_target="tpu_custom_call" | custom-call | flops 1073741824 | bytes 6291456 | tf_op jit(solution)/shard_map/project/pallas_call | solution.py:150
  32.8 4.5 %collective-permute-start.9 = (bf16[128,1024]{1,0:T(8,128)(2,1)S(1)}, bf16[128,1024]{1,0:T(8,128)(2,1)S(1)}, u32[]{:S(2)}, u32[]{:S(2)}) collective-permute-start(bf16[128,1024]{1,0:T(8,128)(2,1)S(1)} %get-tuple-element.87), channel_id=1, source_target_pairs={{0,8},{8,0},{16,24},{24,16},{1,9},{9,1},{17,25},{25,17},{2,10},{10... | collective-permute-start | bytes 786440 | tf_op jit(solution)/shard_map/ppermute | solution.py:349
  37.3 2.9 %shard_map.95 = (bf16[4,128,3072]{2,1,0:T(8,128)(2,1)S(1)}, bf16[4,128,3072]{2,1,0:T(8,128)(2,1)S(1)}, bf16[2,4,128,1024]{3,2,1,0:T(8,128)(2,1)S(1)}, f32[8,4096]{1,0:T(8,128)S(1)}) custom-call(s32[50]{0:T(128)S(1)} %pad_add_fusion.meta.ids, bf16[512,256]{1,0:T(8,128)(2,1)S(1)} %get-tuple-element.81.p, ...), custom_call_target="tpu_custom_call", output_to_operand_aliasing={{2}: (5, {}), {3}: (6, {})} | custom-call | flops 805306368 | bytes 12582912 | tf_op jit(solution)/shard_map/pallas_call | solution.py:213
  40.2 3.3 %collective-permute-done.9.ra = bf16[128,1024]{1,0:T(8,128)(2,1)S(1)} collective-permute-done((bf16[128,1024]{1,0:T(8,128)(2,1)S(1)}, bf16[128,1024]{1,0:T(8,128)(2,1)S(1)}, u32[]{:S(2)}, u32[]{:S(2)}) %collective-permute-start.9) | collective-permute-done | bytes 262176 | tf_op jit(solution)/shard_map/ppermute | solution.py:349
  44.3 1.8 %collective-permute-start.11 = (bf16[128,1024]{1,0:T(8,128)(2,1)S(1)}, bf16[128,1024]{1,0:T(8,128)(2,1)S(1)}, u32[]{:S(2)}, u32[]{:S(2)}) collective-permute-start(bf16[128,1024]{1,0:T(8,128)(2,1)S(1)} %get-tuple-element.91), channel_id=1, source_target_pairs={{0,8},{8,0},{16,24},{24,16},{1,9},{9,1},{17,25},{25,17},{2,10},{10... | collective-permute-start | bytes 786440 | tf_op jit(solution)/shard_map/ppermute | solution.py:349
  46.8 5.0 %collective-permute-done.11.ra = bf16[128,1024]{1,0:T(8,128)(2,1)S(1)} collective-permute-done((bf16[128,1024]{1,0:T(8,128)(2,1)S(1)}, bf16[128,1024]{1,0:T(8,128)(2,1)S(1)}, u32[]{:S(2)}, u32[]{:S(2)}) %collective-permute-start.11) | collective-permute-done | bytes 262176 | tf_op jit(solution)/shard_map/ppermute | solution.py:349
  52.5 3.7 %collective-permute-start.13 = (bf16[128,1024]{1,0:T(8,128)(2,1)S(1)}, bf16[128,1024]{1,0:T(8,128)(2,1)S(1)}, u32[]{:S(2)}, u32[]{:S(2)}) collective-permute-start(bf16[128,1024]{1,0:T(8,128)(2,1)S(1)} %get-tuple-element.93), channel_id=1, source_target_pairs={{0,8},{8,0},{16,24},{24,16},{1,9},{9,1},{17,25},{25,17},{2,10},{10... | collective-permute-start | bytes 786440 | tf_op jit(solution)/shard_map/ppermute | solution.py:349
  56.9 3.9 %collective-permute-done.13.ra = bf16[128,1024]{1,0:T(8,128)(2,1)S(1)} collective-permute-done((bf16[128,1024]{1,0:T(8,128)(2,1)S(1)}, bf16[128,1024]{1,0:T(8,128)(2,1)S(1)}, u32[]{:S(2)}, u32[]{:S(2)}) %collective-permute-start.13) | collective-permute-done | bytes 262176 | tf_op jit(solution)/shard_map/ppermute | solution.py:349
  61.5 3.8 %collective-permute-start.15 = (bf16[128,1024]{1,0:T(8,128)(2,1)S(1)}, bf16[128,1024]{1,0:T(8,128)(2,1)S(1)}, u32[]{:S(2)}, u32[]{:S(2)}) collective-permute-start(bf16[128,1024]{1,0:T(8,128)(2,1)S(1)} %get-tuple-element.95), channel_id=1, source_target_pairs={{0,8},{8,0},{16,24},{24,16},{1,9},{9,1},{17,25},{25,17},{2,10},{10... | collective-permute-start | bytes 786440 | tf_op jit(solution)/shard_map/ppermute | solution.py:349
  65.9 3.7 %collective-permute-done.15.ra = bf16[128,1024]{1,0:T(8,128)(2,1)S(1)} collective-permute-done((bf16[128,1024]{1,0:T(8,128)(2,1)S(1)}, bf16[128,1024]{1,0:T(8,128)(2,1)S(1)}, u32[]{:S(2)}, u32[]{:S(2)}) %collective-permute-start.15) | collective-permute-done | bytes 262176 | tf_op jit(solution)/shard_map/ppermute | solution.py:349
  70.3 4.0 %collective-permute-start.17 = (bf16[128,1024]{1,0:T(8,128)(2,1)S(1)}, bf16[128,1024]{1,0:T(8,128)(2,1)S(1)}, u32[]{:S(2)}, u32[]{:S(2)}) collective-permute-start(bf16[128,1024]{1,0:T(8,128)(2,1)S(1)} %get-tuple-element.97), channel_id=1, source_target_pairs={{0,8},{8,0},{16,24},{24,16},{1,9},{9,1},{17,25},{25,17},{2,10},{10... | collective-permute-start | bytes 786440 | tf_op jit(solution)/shard_map/ppermute | solution.py:349
  75.2 1.7 %shard_map.114.refs_3_ = f32[128,256]{1,0:T(8,128)S(1)} custom-call(bf16[512,256]{1,0:T(8,128)(2,1)S(1)} %get-tuple-element.81.p, bf16[512,4096]{1,0:T(8,128)(2,1)S(1)} %get-tuple-element.79.v, bf16[512,4096]{1,0:T(8,128)(2,1)S(1)} %get-tuple-element.80.g, bf16[4,128,1024]{2,1,0:T(8,128)(2,1)S(1)} %get-tuple-element.118.sl.sa, ...), custom_call_target="tpu_custom_call" | custom-call | flops 402653184 | bytes 4194304 | tf_op jit(solution)/shard_map/pallas_call | solution.py:374
  78.6 1.7 %shard_map.112.refs_1_ = f32[128,256]{1,0:T(8,128)S(1)} custom-call(bf16[512,256]{1,0:T(8,128)(2,1)S(1)} %get-tuple-element.81.p, bf16[512,4096]{1,0:T(8,128)(2,1)S(1)} %get-tuple-element.79.v, bf16[512,4096]{1,0:T(8,128)(2,1)S(1)} %get-tuple-element.80.g, bf16[4,128,1024]{2,1,0:T(8,128)(2,1)S(1)} %get-tuple-element.118.sl.sa, ...), custom_call_target="tpu_custom_call" | custom-call | flops 402653184 | bytes 4194304 | tf_op jit(solution)/shard_map/pallas_call | solution.py:374
  82.7 1.8 %collective-permute-start.19 = (bf16[128,1024]{1,0:T(8,128)(2,1)S(1)}, bf16[128,1024]{1,0:T(8,128)(2,1)S(1)}, u32[]{:S(2)}, u32[]{:S(2)}) collective-permute-start(bf16[128,1024]{1,0:T(8,128)(2,1)S(1)} %get-tuple-element.99), channel_id=1, source_target_pairs={{0,8},{8,0},{16,24},{24,16},{1,9},{9,1},{17,25},{25,17},{2,10},{10... | collective-permute-start | bytes 786440 | tf_op jit(solution)/shard_map/ppermute | solution.py:349
  89.9 3.2 %shard_map.107 = (bf16[512,4096]{1,0:T(8,128)(2,1)}, bf16[512,1024]{1,0:T(8,128)(2,1)S(1)}, f32[512,128]{1,0:T(8,128)S(1)}) custom-call(bf16[512,4096]{1,0:T(8,128)(2,1)S(1)} %get-tuple-element.76.x, bf16[512,4096]{1,0:T(8,128)(2,1)S(1)} %get-tuple-element.79.v, bf16[512,4096]{1,0:T(8,128)(2,1)S(1)} %get-tuple-element.80.g, bf16[512,4096]{1,0:T(8,128)(2,1)S(1)} %bitcast.11, ...), custom_call_target="tpu_custom_call" | custom-call | flops 536870912 | bytes 9437184 | tf_op jit(solution)/shard_map/pallas_call | solution.py:520
  94.2 3.2 %shard_map.108 = (bf16[512,4096]{1,0:T(8,128)(2,1)}, bf16[512,1024]{1,0:T(8,128)(2,1)S(1)}, f32[512,128]{1,0:T(8,128)S(1)}) custom-call(bf16[512,4096]{1,0:T(8,128)(2,1)S(1)} %get-tuple-element.76.x, bf16[512,4096]{1,0:T(8,128)(2,1)S(1)} %get-tuple-element.79.v, bf16[512,4096]{1,0:T(8,128)(2,1)S(1)} %get-tuple-element.80.g, ...), custom_call_target="tpu_custom_call", output_to_operand_aliasing={{0}: (14, {})} | custom-call | flops 536870912 | bytes 9437184 | tf_op jit(solution)/shard_map/pallas_call | solution.py:520
  98.5 3.2 %shard_map.109 = (bf16[512,4096]{1,0:T(8,128)(2,1)}, bf16[512,1024]{1,0:T(8,128)(2,1)S(1)}, f32[512,128]{1,0:T(8,128)S(1)}) custom-call(bf16[512,4096]{1,0:T(8,128)(2,1)S(1)} %get-tuple-element.76.x, bf16[512,4096]{1,0:T(8,128)(2,1)S(1)} %get-tuple-element.79.v, bf16[512,4096]{1,0:T(8,128)(2,1)S(1)} %get-tuple-element.80.g, ...), custom_call_target="tpu_custom_call", output_to_operand_aliasing={{0}: (14, {})} | custom-call | flops 536870912 | bytes 9437184 | tf_op jit(solution)/shard_map/pallas_call | solution.py:520
  108.3 6.3 %collective-permute-done.23.gl = bf16[4,2,128,128]{3,2,1,0:T(8,128)(2,1)S(1)} collective-permute-done((bf16[4,2,128,128]{3,2,1,0:T(8,128)(2,1)S(1)}, bf16[4,2,128,128]{3,2,1,0:T(8,128)(2,1)S(1)}, u32[]{:S(2)}, u32[]{:S(2)}) %collective-permute-start.23) | collective-permute-done | bytes 262176 | tf_op jit(solution)/shard_map/ppermute | solution.py:581
  118.4 3.1 %shard_map.110 = (bf16[512,4096]{1,0:T(8,128)(2,1)}, bf16[512,1024]{1,0:T(8,128)(2,1)S(1)}, f32[512,128]{1,0:T(8,128)S(1)}) custom-call(bf16[512,4096]{1,0:T(8,128)(2,1)S(1)} %get-tuple-element.76.x, bf16[512,4096]{1,0:T(8,128)(2,1)S(1)} %get-tuple-element.79.v, bf16[512,4096]{1,0:T(8,128)(2,1)S(1)} %get-tuple-element.80.g, ...), custom_call_target="tpu_custom_call", output_to_operand_aliasing={{0}: (14, {})} | custom-call | flops 536870912 | bytes 9437184 | tf_op jit(solution)/shard_map/pallas_call | solution.py:520
  121.5 1.9 %shard_map.115.refs_8_ = bf16[512,4096]{1,0:T(8,128)(2,1)} custom-call(bf16[512,4096]{1,0:T(8,128)(2,1)S(1)} %get-tuple-element.76.x, bf16[512,4096]{1,0:T(8,128)(2,1)S(1)} %bitcast.19, bf16[512,256]{1,0:T(8,128)(2,1)S(1)} %lower.1.low, bf16[512,256]{1,0:T(8,128)(2,1)S(1)} %get-tuple-element.81.p, f32[512,1]{1,0:T(8,128)S(1)} %get-tuple-element.125.rstd, ...), custom_call_target="tpu_custom_call" | custom-call | flops 268435456 | bytes 4194304 | tf_op jit(solution)/shard_map/pallas_call | solution.py:567
  124.1 3.4 %collective-permute-start.27 = (bf16[128,256]{1,0:T(8,128)(2,1)S(1)}, bf16[128,256]{1,0:T(8,128)(2,1)S(1)}, u32[]{:S(2)}, u32[]{:S(2)}) collective-permute-start(bf16[128,256]{1,0:T(8,128)(2,1)S(1)} %get-tuple-element.146), channel_id=1, source_target_pairs={{0,8},{8,0},{16,24},{24,16},{1,9},{9,1},{17,25},{25,17},{2,10},{10... | collective-permute-start | bytes 196616 | tf_op jit(solution)/shard_map/ppermute | solution.py:675
  127.8 2.2 %collective-permute-start.29 = (bf16[128,256]{1,0:T(8,128)(2,1)S(1)}, bf16[128,256]{1,0:T(8,128)(2,1)S(1)}, u32[]{:S(2)}, u32[]{:S(2)}) collective-permute-start(bf16[128,256]{1,0:T(8,128)(2,1)S(1)} %get-tuple-element.148), channel_id=1, source_target_pairs={{0,24},{8,16},{16,8},{24,0},{1,25},{9,17},{17,9},{25,1},{2,26},{10... | collective-permute-start | bytes 196616 | tf_op jit(solution)/shard_map/ppermute | solution.py:675
  130.0 1.9 %shard_map.116.refs_8_ = bf16[512,4096]{1,0:T(8,128)(2,1)} custom-call(bf16[512,4096]{1,0:T(8,128)(2,1)S(1)} %get-tuple-element.76.x, bf16[512,4096]{1,0:T(8,128)(2,1)S(1)} %bitcast.20, bf16[512,256]{1,0:T(8,128)(2,1)S(1)} %lower.1.low, bf16[512,256]{1,0:T(8,128)(2,1)S(1)} %get-tuple-element.81.p, ...), custom_call_target="tpu_custom_call", output_to_operand_aliasing={{}: (14, {})} | custom-call | flops 268435456 | bytes 4194304 | tf_op jit(solution)/shard_map/pallas_call | solution.py:567
  131.9 2.9 %shard_map.117 = bf16[512,4096]{1,0:T(8,128)(2,1)} custom-call(bf16[512,4096]{1,0:T(8,128)(2,1)S(1)} %get-tuple-element.76.x, bf16[512,4096]{1,0:T(8,128)(2,1)S(1)} %bitcast.21, bf16[512,256]{1,0:T(8,128)(2,1)S(1)} %lower.1.low, bf16[512,256]{1,0:T(8,128)(2,1)S(1)} %get-tuple-element.81.p, ...), custom_call_target="tpu_custom_call", output_to_operand_aliasing={{}: (14, {})} | custom-call | flops 536870912 | bytes 8388608 | tf_op jit(solution)/shard_map/pallas_call | solution.py:567
  (86 shorter events, 37.9 us)
Async XLA Ops:
  0.6 9.6 %collective-permute-start = (bf16[512,256]{1,0:T(8,128)(2,1)}, bf16[512,256]{1,0:T(8,128)(2,1)S(1)}, u32[]{:S(2)}, u32[]{:S(2)}) collective-permute-start(bf16[512,256]{1,0:T(8,128)(2,1)} %refs_0_.1), channel_id=1, source_target_pairs={{0,2},{1,3},{2,0},{3,1},{4,6},{5,7},{6,4},{7,5},{8,10},{9,11},{10,... | collective-permute-start | bytes 786440 | tf_op jit(solution)/shard_map/ppermute | solution.py:581
  3.7 8.4 %collective-permute-start.1 = (bf16[512,256]{1,0:T(8,128)(2,1)}, bf16[512,256]{1,0:T(8,128)(2,1)S(1)}, u32[]{:S(2)}, u32[]{:S(2)}) collective-permute-start(bf16[512,256]{1,0:T(8,128)(2,1)} %refs_0_.1), channel_id=1, source_target_pairs={{0,4},{1,5},{2,6},{3,7},{4,0},{5,1},{6,2},{7,3},{8,12},{9,13},{10,... | collective-permute-start | bytes 786440 | tf_op jit(solution)/shard_map/ppermute | solution.py:581
  5.2 19.8 %collective-permute-start.4 = (bf16[512,256]{1,0:T(8,128)(2,1)}, bf16[512,256]{1,0:T(8,128)(2,1)S(1)}, u32[]{:S(2)}, u32[]{:S(2)}) collective-permute-start(bf16[512,256]{1,0:T(8,128)(2,1)} %refs_0_.1), channel_id=1, source_target_pairs={{0,1},{1,0},{2,3},{3,2},{4,5},{5,4},{6,7},{7,6},{8,9},{9,8},{10,11... | collective-permute-start | bytes 786440 | tf_op jit(solution)/shard_map/ppermute | solution.py:581
  10.2 5.0 %collective-permute-start.2 = (bf16[256,256]{1,0:T(8,128)(2,1)S(1)}, bf16[256,256]{1,0:T(8,128)(2,1)S(1)}, u32[]{:S(2)}, u32[]{:S(2)}) collective-permute-start(bf16[256,256]{1,0:T(8,128)(2,1)S(1)} %slice.8), channel_id=1, source_target_pairs={{0,4},{1,5},{2,6},{3,7},{4,0},{5,1},{6,2},{7,3},{8,12},{9,13},{10,... | collective-permute-start | bytes 393224 | tf_op jit(solution)/shard_map/ppermute | solution.py:581
  12.0 5.0 %collective-permute-start.3 = (bf16[256,256]{1,0:T(8,128)(2,1)S(1)}, bf16[256,256]{1,0:T(8,128)(2,1)S(1)}, u32[]{:S(2)}, u32[]{:S(2)}) collective-permute-start(bf16[256,256]{1,0:T(8,128)(2,1)S(1)} %slice.9), channel_id=1, source_target_pairs={{0,2},{1,3},{2,0},{3,1},{4,6},{5,7},{6,4},{7,5},{8,10},{9,11},{10,... | collective-permute-start | bytes 393224 | tf_op jit(solution)/shard_map/ppermute | solution.py:581
  13.6 15.1 %collective-permute-start.5 = (bf16[512,256]{1,0:T(8,128)(2,1)S(1)}, bf16[512,256]{1,0:T(8,128)(2,1)S(1)}, u32[]{:S(2)}, u32[]{:S(2)}) collective-permute-start(bf16[512,256]{1,0:T(8,128)(2,1)S(1)} %collective-permute-done.refs_1_), channel_id=1, source_target_pairs={{0,1},{1,0},{2,3},{3,2},{4,5},{5,4},{6,7},{7,6},{8,9},{9,8},{10,11... | collective-permute-start | bytes 786440 | tf_op jit(solution)/shard_map/ppermute | solution.py:581
  13.6 15.1 %collective-permute-start.6 = (bf16[512,256]{1,0:T(8,128)(2,1)S(1)}, bf16[512,256]{1,0:T(8,128)(2,1)S(1)}, u32[]{:S(2)}, u32[]{:S(2)}) collective-permute-start(bf16[512,256]{1,0:T(8,128)(2,1)S(1)} %collective-permute-done.1.refs_2_), channel_id=1, source_target_pairs={{0,1},{1,0},{2,3},{3,2},{4,5},{5,4},{6,7},{7,6},{8,9},{9,8},{10,11... | collective-permute-start | bytes 786440 | tf_op jit(solution)/shard_map/ppermute | solution.py:581
  15.2 13.4 %collective-permute-start.7 = (bf16[256,256]{1,0:T(8,128)(2,1)S(1)}, bf16[256,256]{1,0:T(8,128)(2,1)S(1)}, u32[]{:S(2)}, u32[]{:S(2)}) collective-permute-start(bf16[256,256]{1,0:T(8,128)(2,1)S(1)} %collective-permute-done.2.refs_3_), channel_id=1, source_target_pairs={{0,1},{1,0},{2,3},{3,2},{4,5},{5,4},{6,7},{7,6},{8,9},{9,8},{10,11... | collective-permute-start | bytes 393224 | tf_op jit(solution)/shard_map/ppermute | solution.py:581
  17.1 11.6 %collective-permute-start.8 = (bf16[256,256]{1,0:T(8,128)(2,1)S(1)}, bf16[256,256]{1,0:T(8,128)(2,1)S(1)}, u32[]{:S(2)}, u32[]{:S(2)}) collective-permute-start(bf16[256,256]{1,0:T(8,128)(2,1)S(1)} %collective-permute-done.3.refs_4_), channel_id=1, source_target_pairs={{0,1},{1,0},{2,3},{3,2},{4,5},{5,4},{6,7},{7,6},{8,9},{9,8},{10,11... | collective-permute-start | bytes 393224 | tf_op jit(solution)/shard_map/ppermute | solution.py:581
  25.0 78.9 %collective-permute-start.21 = (bf16[2048,512]{1,0:T(8,128)(2,1)S(1)}, bf16[2048,512]{1,0:T(8,128)(2,1)S(1)}, u32[]{:S(2)}, u32[]{:S(2)}) collective-permute-start(bf16[2048,512]{1,0:T(8,128)(2,1)S(1)} %get-tuple-element.135), channel_id=1, source_target_pairs={{0,1},{1,0},{2,3},{3,2},{4,5},{5,4},{6,7},{7,6},{8,9},{9,8},{10,11... | collective-permute-start | bytes 6291464 | tf_op jit(solution)/shard_map/ppermute | solution.py:581
  25.6 3.1 %copy-start.4 = (bf16[512,256]{1,0:T(8,128)(2,1)S(1)}, bf16[512,256]{1,0:T(8,128)(2,1)}, u32[]{:S(2)}) copy-start(bf16[512,256]{1,0:T(8,128)(2,1)} %refs_0_.1) | copy-start | bytes 786436
  32.1 8.1 %collective-permute-start.10 = (bf16[128,1024]{1,0:T(8,128)(2,1)S(1)}, bf16[128,1024]{1,0:T(8,128)(2,1)S(1)}, u32[]{:S(2)}, u32[]{:S(2)}) collective-permute-start(bf16[128,1024]{1,0:T(8,128)(2,1)S(1)} %get-tuple-element.88), channel_id=1, source_target_pairs={{8,16},{16,8},{9,17},{17,9},{10,18},{18,10},{11,19},{19,11},{12,20... | collective-permute-start | bytes 786440 | tf_op jit(solution)/shard_map/ppermute | solution.py:350
  32.8 10.7 %collective-permute-start.9 = (bf16[128,1024]{1,0:T(8,128)(2,1)S(1)}, bf16[128,1024]{1,0:T(8,128)(2,1)S(1)}, u32[]{:S(2)}, u32[]{:S(2)}) collective-permute-start(bf16[128,1024]{1,0:T(8,128)(2,1)S(1)} %get-tuple-element.87), channel_id=1, source_target_pairs={{0,8},{8,0},{16,24},{24,16},{1,9},{9,1},{17,25},{25,17},{2,10},{10... | collective-permute-start | bytes 786440 | tf_op jit(solution)/shard_map/ppermute | solution.py:349
  44.3 7.5 %collective-permute-start.11 = (bf16[128,1024]{1,0:T(8,128)(2,1)S(1)}, bf16[128,1024]{1,0:T(8,128)(2,1)S(1)}, u32[]{:S(2)}, u32[]{:S(2)}) collective-permute-start(bf16[128,1024]{1,0:T(8,128)(2,1)S(1)} %get-tuple-element.91), channel_id=1, source_target_pairs={{0,8},{8,0},{16,24},{24,16},{1,9},{9,1},{17,25},{25,17},{2,10},{10... | collective-permute-start | bytes 786440 | tf_op jit(solution)/shard_map/ppermute | solution.py:349
  46.1 5.7 %collective-permute-start.12 = (bf16[128,1024]{1,0:T(8,128)(2,1)S(1)}, bf16[128,1024]{1,0:T(8,128)(2,1)S(1)}, u32[]{:S(2)}, u32[]{:S(2)}) collective-permute-start(bf16[128,1024]{1,0:T(8,128)(2,1)S(1)} %get-tuple-element.92), channel_id=1, source_target_pairs={{8,16},{16,8},{9,17},{17,9},{10,18},{18,10},{11,19},{19,11},{12,20... | collective-permute-start | bytes 786440 | tf_op jit(solution)/shard_map/ppermute | solution.py:350
  52.5 8.3 %collective-permute-start.13 = (bf16[128,1024]{1,0:T(8,128)(2,1)S(1)}, bf16[128,1024]{1,0:T(8,128)(2,1)S(1)}, u32[]{:S(2)}, u32[]{:S(2)}) collective-permute-start(bf16[128,1024]{1,0:T(8,128)(2,1)S(1)} %get-tuple-element.93), channel_id=1, source_target_pairs={{0,8},{8,0},{16,24},{24,16},{1,9},{9,1},{17,25},{25,17},{2,10},{10... | collective-permute-start | bytes 786440 | tf_op jit(solution)/shard_map/ppermute | solution.py:349
  56.2 4.6 %collective-permute-start.14 = (bf16[128,1024]{1,0:T(8,128)(2,1)S(1)}, bf16[128,1024]{1,0:T(8,128)(2,1)S(1)}, u32[]{:S(2)}, u32[]{:S(2)}) collective-permute-start(bf16[128,1024]{1,0:T(8,128)(2,1)S(1)} %get-tuple-element.94), channel_id=1, source_target_pairs={{8,16},{16,8},{9,17},{17,9},{10,18},{18,10},{11,19},{19,11},{12,20... | collective-permute-start | bytes 786440 | tf_op jit(solution)/shard_map/ppermute | solution.py:350
  61.5 8.1 %collective-permute-start.15 = (bf16[128,1024]{1,0:T(8,128)(2,1)S(1)}, bf16[128,1024]{1,0:T(8,128)(2,1)S(1)}, u32[]{:S(2)}, u32[]{:S(2)}) collective-permute-start(bf16[128,1024]{1,0:T(8,128)(2,1)S(1)} %get-tuple-element.95), channel_id=1, source_target_pairs={{0,8},{8,0},{16,24},{24,16},{1,9},{9,1},{17,25},{25,17},{2,10},{10... | collective-permute-start | bytes 786440 | tf_op jit(solution)/shard_map/ppermute | solution.py:349
  65.3 4.4 %collective-permute-start.16 = (bf16[128,1024]{1,0:T(8,128)(2,1)S(1)}, bf16[128,1024]{1,0:T(8,128)(2,1)S(1)}, u32[]{:S(2)}, u32[]{:S(2)}) collective-permute-start(bf16[128,1024]{1,0:T(8,128)(2,1)S(1)} %get-tuple-element.96), channel_id=1, source_target_pairs={{8,16},{16,8},{9,17},{17,9},{10,18},{18,10},{11,19},{19,11},{12,20... | collective-permute-start | bytes 786440 | tf_op jit(solution)/shard_map/ppermute | solution.py:350
  70.3 11.7 %collective-permute-start.17 = (bf16[128,1024]{1,0:T(8,128)(2,1)S(1)}, bf16[128,1024]{1,0:T(8,128)(2,1)S(1)}, u32[]{:S(2)}, u32[]{:S(2)}) collective-permute-start(bf16[128,1024]{1,0:T(8,128)(2,1)S(1)} %get-tuple-element.97), channel_id=1, source_target_pairs={{0,8},{8,0},{16,24},{24,16},{1,9},{9,1},{17,25},{25,17},{2,10},{10... | collective-permute-start | bytes 786440 | tf_op jit(solution)/shard_map/ppermute | solution.py:349
  74.3 7.7 %collective-permute-start.18 = (bf16[128,1024]{1,0:T(8,128)(2,1)S(1)}, bf16[128,1024]{1,0:T(8,128)(2,1)S(1)}, u32[]{:S(2)}, u32[]{:S(2)}) collective-permute-start(bf16[128,1024]{1,0:T(8,128)(2,1)S(1)} %get-tuple-element.98), channel_id=1, source_target_pairs={{8,16},{16,8},{9,17},{17,9},{10,18},{18,10},{11,19},{19,11},{12,20... | collective-permute-start | bytes 786440 | tf_op jit(solution)/shard_map/ppermute | solution.py:350
  82.7 19.0 %collective-permute-start.19 = (bf16[128,1024]{1,0:T(8,128)(2,1)S(1)}, bf16[128,1024]{1,0:T(8,128)(2,1)S(1)}, u32[]{:S(2)}, u32[]{:S(2)}) collective-permute-start(bf16[128,1024]{1,0:T(8,128)(2,1)S(1)} %get-tuple-element.99), channel_id=1, source_target_pairs={{0,8},{8,0},{16,24},{24,16},{1,9},{9,1},{17,25},{25,17},{2,10},{10... | collective-permute-start | bytes 786440 | tf_op jit(solution)/shard_map/ppermute | solution.py:349
  84.5 17.2 %collective-permute-start.20 = (bf16[128,1024]{1,0:T(8,128)(2,1)S(1)}, bf16[128,1024]{1,0:T(8,128)(2,1)S(1)}, u32[]{:S(2)}, u32[]{:S(2)}) collective-permute-start(bf16[128,1024]{1,0:T(8,128)(2,1)S(1)} %get-tuple-element.100), channel_id=1, source_target_pairs={{8,16},{16,8},{9,17},{17,9},{10,18},{18,10},{11,19},{19,11},{12,20... | collective-permute-start | bytes 786440 | tf_op jit(solution)/shard_map/ppermute | solution.py:350
  103.1 1.6 %collective-permute-start.22 = (bf16[512,256]{1,0:T(8,128)(2,1)S(1)}, bf16[512,256]{1,0:T(8,128)(2,1)S(1)}, u32[]{:S(2)}, u32[]{:S(2)}) collective-permute-start(bf16[512,256]{1,0:T(8,128)(2,1)S(1)} %lower.1.low), channel_id=1, source_target_pairs={{0,1},{1,0},{2,3},{3,2},{4,5},{5,4},{6,7},{7,6},{8,9},{9,8},{10,11... | collective-permute-start | bytes 786440 | tf_op jit(solution)/shard_map/ppermute | solution.py:581
  106.2 8.4 %collective-permute-start.23 = (bf16[4,2,128,128]{3,2,1,0:T(8,128)(2,1)S(1)}, bf16[4,2,128,128]{3,2,1,0:T(8,128)(2,1)S(1)}, u32[]{:S(2)}, u32[]{:S(2)}) collective-permute-start(bf16[4,2,128,128]{3,2,1,0:T(8,128)(2,1)S(1)} %get-tuple-element.138), channel_id=1, source_target_pairs={{0,2},{1,3},{2,0},{3,1},{4,6},{5,7},{6,4},{7,5},{8,10},{9,11},{10,... | collective-permute-start | bytes 786440 | tf_op jit(solution)/shard_map/ppermute | solution.py:581
  107.8 8.1 %collective-permute-start.24 = (bf16[4,2,128,128]{3,2,1,0:T(8,128)(2,1)S(1)}, bf16[4,2,128,128]{3,2,1,0:T(8,128)(2,1)S(1)}, u32[]{:S(2)}, u32[]{:S(2)}) collective-permute-start(bf16[4,2,128,128]{3,2,1,0:T(8,128)(2,1)S(1)} %get-tuple-element.140), channel_id=1, source_target_pairs={{0,4},{1,5},{2,6},{3,7},{4,0},{5,1},{6,2},{7,3},{8,12},{9,13},{10,... | collective-permute-start | bytes 786440 | tf_op jit(solution)/shard_map/ppermute | solution.py:581
  116.7 6.8 %collective-permute-start.25 = (bf16[4,1,128,128]{3,2,1,0:T(8,128)(2,1)S(1)}, bf16[4,1,128,128]{3,2,1,0:T(8,128)(2,1)S(1)}, u32[]{:S(2)}, u32[]{:S(2)}) collective-permute-start(bf16[4,1,128,128]{3,2,1,0:T(8,128)(2,1)S(1)} %get-tuple-element.142), channel_id=1, source_target_pairs={{0,4},{1,5},{2,6},{3,7},{4,0},{5,1},{6,2},{7,3},{8,12},{9,13},{10,... | collective-permute-start | bytes 393224 | tf_op jit(solution)/shard_map/ppermute | solution.py:581
  117.3 6.2 %collective-permute-start.26 = (bf16[4,1,128,128]{3,2,1,0:T(8,128)(2,1)S(1)}, bf16[4,1,128,128]{3,2,1,0:T(8,128)(2,1)S(1)}, u32[]{:S(2)}, u32[]{:S(2)}) collective-permute-start(bf16[4,1,128,128]{3,2,1,0:T(8,128)(2,1)S(1)} %get-tuple-element.144), channel_id=1, source_target_pairs={{0,2},{1,3},{2,0},{3,1},{4,6},{5,7},{6,4},{7,5},{8,10},{9,11},{10,... | collective-permute-start | bytes 393224 | tf_op jit(solution)/shard_map/ppermute | solution.py:581
  118.4 3.1 %copy-start.2 = (bf16[1,512,4096]{2,1,0:T(8,128)(2,1)S(1)}, bf16[1,512,4096]{2,1,0:T(8,128)(2,1)}, u32[]{:S(2)}) copy-start(bf16[1,512,4096]{2,1,0:T(8,128)(2,1)} %param.9) | copy-start | bytes 12582916
  124.1 10.7 %collective-permute-start.27 = (bf16[128,256]{1,0:T(8,128)(2,1)S(1)}, bf16[128,256]{1,0:T(8,128)(2,1)S(1)}, u32[]{:S(2)}, u32[]{:S(2)}) collective-permute-start(bf16[128,256]{1,0:T(8,128)(2,1)S(1)} %get-tuple-element.146), channel_id=1, source_target_pairs={{0,8},{8,0},{16,24},{24,16},{1,9},{9,1},{17,25},{25,17},{2,10},{10... | collective-permute-start | bytes 196616 | tf_op jit(solution)/shard_map/ppermute | solution.py:675
  127.5 7.3 %collective-permute-start.28 = (bf16[128,256]{1,0:T(8,128)(2,1)S(1)}, bf16[128,256]{1,0:T(8,128)(2,1)S(1)}, u32[]{:S(2)}, u32[]{:S(2)}) collective-permute-start(bf16[128,256]{1,0:T(8,128)(2,1)S(1)} %get-tuple-element.147), channel_id=1, source_target_pairs={{0,16},{8,24},{16,0},{24,8},{1,17},{9,25},{17,1},{25,9},{2,18},{10... | collective-permute-start | bytes 196616 | tf_op jit(solution)/shard_map/ppermute | solution.py:675
  127.8 7.0 %collective-permute-start.29 = (bf16[128,256]{1,0:T(8,128)(2,1)S(1)}, bf16[128,256]{1,0:T(8,128)(2,1)S(1)}, u32[]{:S(2)}, u32[]{:S(2)}) collective-permute-start(bf16[128,256]{1,0:T(8,128)(2,1)S(1)} %get-tuple-element.148), channel_id=1, source_target_pairs={{0,24},{8,16},{16,8},{24,0},{1,25},{9,17},{17,9},{25,1},{2,26},{10... | collective-permute-start | bytes 196616 | tf_op jit(solution)/shard_map/ppermute | solution.py:675
  (4 other events, 8.6 us)
